TPU v7x, 32 devices: a whole 2x2x4 slice. The times are simulated.
32 devices in a mesh: dp: 8 (over z, y), tensor: 4 (over x, core).
Axes of the slice: x: 2, y: 2, z: 4, core: 2. Of those that a mesh axis runs over, the one named last changes fastest.
Arguments:
- hidden_in: bfloat16 [4096, 640], P(('dp', 'tensor')), may hold values from -6 to 6
- cotangent: bfloat16 [4096, 640], P(('dp', 'tensor')), may hold values from -6 to 6
- segments: int32 [4096], P('dp'), may hold values from 0 to 3, as said below
- positions: int32 [4096], P('dp'), may hold values from 0 to 508, as said below
- w_query: bfloat16 [2, 640, 1024], P(None, None, 'tensor'), may hold values from -0.25 to 0.25
- w_key: bfloat16 [2, 640, 256], replicated, may hold values from -0.25 to 0.25
- w_value: bfloat16 [2, 640, 256], replicated, may hold values from -0.25 to 0.25
- w_out: bfloat16 [2, 1024, 640], P(None, 'tensor'), may hold values from -0.1875 to 0.1875
- w_gate: bfloat16 [2, 640, 2048], P(None, None, 'tensor'), may hold values from -0.25 to 0.25
- w_up: bfloat16 [2, 640, 2048], P(None, None, 'tensor'), may hold values from -0.25 to 0.25
- w_down: bfloat16 [2, 2048, 640], P(None, 'tensor'), may hold values from -0.125 to 0.125
- norm_gains: float32 [2, 4, 640], replicated, may hold values from 0.5 to 1.5
- qk_gains: float32 [2, 2, 256], replicated, may hold values from 0.5 to 1.5
Outputs:
- output: bfloat16 [4096, 640], P(('dp', 'tensor'))
- grad_input: bfloat16 [4096, 640], P(('dp', 'tensor'))
- grad_w_query: float32 [2, 640, 1024], P(None, 'dp', 'tensor')
- grad_w_key: float32 [2, 640, 256], P(None, 'dp')
- grad_w_value: float32 [2, 640, 256], P(None, 'dp')
- grad_w_out: float32 [2, 1024, 640], P(None, ('tensor', 'dp'))
- grad_w_gate: float32 [2, 640, 2048], P(None, 'dp', 'tensor')
- grad_w_up: float32 [2, 640, 2048], P(None, 'dp', 'tensor')
- grad_w_down: float32 [2, 2048, 640], P(None, ('tensor', 'dp'))
- grad_norm_gains: float32 [2, 4, 640], P(None, None, 'dp')
- grad_qk_gains: float32 [2, 2, 256], P(None, None, 'dp')
Inputs may be any that keep to these rules, and one draw needn't show every extreme that they name: `segments`: in each sequence (aligned runs of 512 tokens) the numbers start at 0, never fall, and each of 0 to 3 marks one document of one token or more. `positions`: each token's place in its document, 0 at the document's first token.
All inputs are finite; a program needn't handle non-finite values.
Results may differ from a plain program's by a relative error of at most 0.033.
Values may be sent and summed in bfloat16 or wider, within the bound.
No kernel may reach another device: no remote copies, remote signals or barrier semaphores. Data moves between devices by JAX's collectives and lax.ppermute only.
A program may use at most 128 MiB of HBM per device.

v0:
```python
import jax
import jax.numpy as jnp
from jax import lax
from jax.sharding import PartitionSpec as P

WINDOW = 512
SEQ_LEN = 512


epsilon = 1e-06
score_scale = 0.0625
masked_fill = -1e30
thetas = (10000.0, 1000000.0)


def product(left, right):
    return jnp.dot(left, right, preferred_element_type=jnp.float32)


def product_left(left, right):
    return lax.dot_general(
        left, right, (((0,), (0,)), ((), ())), preferred_element_type=jnp.float32
    )


def product_right(left, right):
    return lax.dot_general(
        left, right, (((1,), (1,)), ((), ())), preferred_element_type=jnp.float32
    )


def rms_scale(vector, gain_row):
    return (
        vector * lax.rsqrt(jnp.mean(vector * vector, axis=-1, keepdims=True) + epsilon) * gain_row
    )


def angles(place, width, theta):
    half_width = width // 2
    frequency = theta ** (-(2.0 * jnp.arange(half_width, dtype=jnp.float32)) / width)
    phases = place.astype(jnp.float32)[:, None] * frequency[None, :]
    return (jnp.cos(phases), jnp.sin(phases))


def rotate(vector, cosine, sine):
    half_width = vector.shape[-1] // 2
    first_half = vector[:, :half_width]
    second_half = vector[:, half_width:]
    return jnp.concatenate(
        [first_half * cosine - second_half * sine, second_half * cosine + first_half * sine],
        axis=-1,
    )


def allowed_mask(seg_piece, window):
    length = seg_piece.shape[0]
    rows_iota = lax.broadcasted_iota(jnp.int32, (length, length), 0)
    cols_iota = lax.broadcasted_iota(jnp.int32, (length, length), 1)
    return (
        (seg_piece[:, None] == seg_piece[None, :])
        & (cols_iota <= rows_iota)
        & (rows_iota - cols_iota < window)
    )


def split_seqs(array):
    return array.reshape((-1, SEQ_LEN) + array.shape[1:])


def attend_forward(pieces, window):
    queries, key_rows, values, seg_piece = pieces
    scores = product_right(queries, key_rows) * score_scale
    allowed = allowed_mask(seg_piece, window)
    masked = jnp.where(allowed, scores, masked_fill)
    row_max = jnp.max(masked, axis=-1, keepdims=True)
    expo = jnp.where(allowed, jnp.exp(masked - row_max), 0.0)
    row_sum = jnp.sum(expo, axis=-1, keepdims=True)
    probability = (expo / row_sum).astype(jnp.bfloat16)
    attended = product(probability, values)
    return (attended, (row_max + jnp.log(row_sum))[:, 0])


def attend_backward(pieces, window):
    queries, key_rows, values, seg_piece, row_lse, grad_out = pieces
    scores = product_right(queries, key_rows) * score_scale
    allowed = allowed_mask(seg_piece, window)
    probability = jnp.where(allowed, jnp.exp(scores - row_lse[:, None]), 0.0)
    prob_low = probability.astype(jnp.bfloat16)
    grad_values = product_left(prob_low, grad_out).astype(jnp.bfloat16)
    grad_prob = product_right(grad_out, values)
    inner_sum = jnp.sum(probability * grad_prob, axis=-1, keepdims=True)
    grad_scores = (probability * (grad_prob - inner_sum)).astype(jnp.bfloat16)
    grad_queries = (product(grad_scores, key_rows) * score_scale).astype(jnp.bfloat16)
    grad_keys = (product_left(grad_scores, queries) * score_scale).astype(jnp.bfloat16)
    return (grad_queries, grad_keys, grad_values)


def norm_back(vector, gain_row, grad_out):
    unused, pullback = jax.vjp(rms_scale, vector, gain_row)
    return pullback(grad_out)


def layer_forward(stream, weights, segments, cosine, sine, window):
    w_query, w_key, w_value, w_out, w_gate, w_up, w_down, gains, qk_gain = weights
    head_width = w_key.shape[1]
    normed_share = rms_scale(stream, gains[0]).astype(jnp.bfloat16)
    normed = lax.all_gather(normed_share, "tensor", axis=0, tiled=True)
    query_raw = product(normed, w_query)
    key_raw = product(normed, w_key)
    values = product(normed, w_value).astype(jnp.bfloat16)
    queries = rotate(rms_scale(query_raw, qk_gain[0]), cosine, sine).astype(jnp.bfloat16)
    key_rows = rotate(rms_scale(key_raw, qk_gain[1]), cosine, sine).astype(jnp.bfloat16)
    attended, row_lse = lax.map(
        lambda pieces: attend_forward(pieces, window),
        (split_seqs(queries), split_seqs(key_rows), split_seqs(values), split_seqs(segments)),
    )
    row_lse = row_lse.reshape(-1)
    attn_low = attended.reshape(-1, head_width).astype(jnp.bfloat16)
    attn_sum = lax.psum_scatter(
        product(attn_low, w_out).astype(jnp.bfloat16), "tensor", scatter_dimension=0, tiled=True
    ).astype(jnp.float32)
    middle = stream + rms_scale(attn_sum, gains[1])
    mlp_share = rms_scale(middle, gains[2]).astype(jnp.bfloat16)
    normed_mlp = lax.all_gather(mlp_share, "tensor", axis=0, tiled=True)
    gate_pre = product(normed_mlp, w_gate)
    up_pre = product(normed_mlp, w_up)
    hidden = (jax.nn.gelu(gate_pre, approximate=True) * up_pre).astype(jnp.bfloat16)
    mlp_sum = lax.psum_scatter(
        product(hidden, w_down).astype(jnp.bfloat16), "tensor", scatter_dimension=0, tiled=True
    ).astype(jnp.float32)
    result = middle + rms_scale(mlp_sum, gains[3])
    saved = (
        stream,
        normed,
        query_raw,
        key_raw,
        queries,
        key_rows,
        values,
        row_lse,
        attn_low,
        attn_sum,
        middle,
        normed_mlp,
        gate_pre,
        up_pre,
        hidden,
        mlp_sum,
    )
    return (result, saved)


def gated_unit(gate_in, up_in):
    return jax.nn.gelu(gate_in, approximate=True) * up_in


def layer_backward(grad_stream, weights, saved, segments, cosine, sine, window):
    w_query, w_key, w_value, w_out, w_gate, w_up, w_down, gains, qk_gain = weights
    (
        stream,
        normed,
        query_raw,
        key_raw,
        queries,
        key_rows,
        values,
        row_lse,
        attn_low,
        attn_sum,
        middle,
        normed_mlp,
        gate_pre,
        up_pre,
        hidden,
        mlp_sum,
    ) = saved
    head_width = w_key.shape[1]
    grad_mlp, grad_gain3 = norm_back(mlp_sum, gains[3], grad_stream)
    mlp_low = lax.all_gather(grad_mlp.astype(jnp.bfloat16), "tensor", axis=0, tiled=True)
    grad_w_down = product_left(hidden, mlp_low)
    grad_hidden = product_right(mlp_low, w_down)
    unused, gate_pull = jax.vjp(gated_unit, gate_pre, up_pre)
    grad_gate, grad_up = gate_pull(grad_hidden)
    gate_low = grad_gate.astype(jnp.bfloat16)
    up_low = grad_up.astype(jnp.bfloat16)
    grad_w_gate = product_left(normed_mlp, gate_low)
    grad_w_up = product_left(normed_mlp, up_low)
    grad_normed_mlp = lax.psum_scatter(
        (product_right(gate_low, w_gate) + product_right(up_low, w_up)).astype(jnp.bfloat16),
        "tensor",
        scatter_dimension=0,
        tiled=True,
    ).astype(jnp.float32)
    grad_middle_norm, grad_gain2 = norm_back(middle, gains[2], grad_normed_mlp)
    grad_middle = grad_stream + grad_middle_norm
    grad_attn, grad_gain1 = norm_back(attn_sum, gains[1], grad_middle)
    attn_grad_low = lax.all_gather(grad_attn.astype(jnp.bfloat16), "tensor", axis=0, tiled=True)
    grad_w_out = product_left(attn_low, attn_grad_low)
    grad_attended = product_right(attn_grad_low, w_out).astype(jnp.bfloat16)
    grad_queries, grad_keys, grad_values = lax.map(
        lambda pieces: attend_backward(pieces, window),
        (
            split_seqs(queries),
            split_seqs(key_rows),
            split_seqs(values),
            split_seqs(segments),
            split_seqs(row_lse),
            split_seqs(grad_attended),
        ),
    )
    grad_queries = grad_queries.reshape(-1, head_width).astype(jnp.float32)
    grad_keys = grad_keys.reshape(-1, head_width).astype(jnp.float32)
    grad_values = grad_values.reshape(-1, head_width)

    def qk_chain(raw_rows, gain_row):
        return rotate(rms_scale(raw_rows, gain_row), cosine, sine)

    unused, query_pull = jax.vjp(qk_chain, query_raw, qk_gain[0])
    grad_query_raw, grad_query_gain = query_pull(grad_queries)
    unused, key_pull = jax.vjp(qk_chain, key_raw, qk_gain[1])
    grad_key_raw, grad_key_gain = key_pull(grad_keys)
    query_low = grad_query_raw.astype(jnp.bfloat16)
    key_low = grad_key_raw.astype(jnp.bfloat16)
    grad_w_query = product_left(normed, query_low)
    grad_w_key = product_left(normed, key_low)
    grad_w_value = product_left(normed, grad_values)
    grad_normed = lax.psum_scatter(
        (
            product_right(query_low, w_query)
            + product_right(key_low, w_key)
            + product_right(grad_values, w_value)
        ).astype(jnp.bfloat16),
        "tensor",
        scatter_dimension=0,
        tiled=True,
    ).astype(jnp.float32)
    grad_stream_norm, grad_gain0 = norm_back(stream, gains[0], grad_normed)
    grad_input = grad_middle + grad_stream_norm
    grads = (
        grad_w_query,
        grad_w_key,
        grad_w_value,
        grad_w_out,
        grad_w_gate,
        grad_w_up,
        grad_w_down,
        grad_gain0,
        grad_gain1,
        grad_gain2,
        grad_gain3,
        grad_query_gain,
        grad_key_gain,
    )
    return (grad_input, grads)


def assemble(summed, shared, offset, shared_offset):
    return [
        summed[offset],
        shared[shared_offset],
        shared[shared_offset + 1],
        summed[offset + 3],
        summed[offset + 4],
        summed[offset + 5],
        summed[offset + 6],
        shared[shared_offset + 2],
        shared[shared_offset + 3],
        shared[shared_offset + 4],
        shared[shared_offset + 5],
        shared[shared_offset + 6],
        shared[shared_offset + 7],
    ]


def local(
    hidden_in,
    cotangent,
    segments,
    positions,
    w_query,
    w_key,
    w_value,
    w_out,
    w_gate,
    w_up,
    w_down,
    norm_gains,
    qk_gains,
):
    head_width = w_key.shape[2]
    windows = (WINDOW, SEQ_LEN)
    stream = hidden_in.astype(jnp.float32)
    saved_all = []
    tables = []
    layer_weights = []
    for layer_idx in range(2):
        cosine, sine = angles(positions, head_width, thetas[layer_idx])
        weights = (
            w_query[layer_idx],
            w_key[layer_idx],
            w_value[layer_idx],
            w_out[layer_idx],
            w_gate[layer_idx],
            w_up[layer_idx],
            w_down[layer_idx],
            norm_gains[layer_idx],
            qk_gains[layer_idx],
        )
        stream, saved = layer_forward(stream, weights, segments, cosine, sine, windows[layer_idx])
        saved_all.append(saved)
        tables.append((cosine, sine))
        layer_weights.append(weights)
    output = stream.astype(jnp.bfloat16)
    grad_stream = cotangent.astype(jnp.float32)
    reduced = [None, None]
    collected = [None, None]
    for layer_idx in (1, 0):
        grad_stream, collected[layer_idx] = layer_backward(
            grad_stream,
            layer_weights[layer_idx],
            saved_all[layer_idx],
            segments,
            tables[layer_idx][0],
            tables[layer_idx][1],
            windows[layer_idx],
        )
    first = collected[0]
    second = collected[1]
    summed = (
        lax.psum_scatter(first[0], "dp", scatter_dimension=0, tiled=True),
        lax.psum_scatter(first[1], "dp", scatter_dimension=0, tiled=True),
        lax.psum_scatter(first[2], "dp", scatter_dimension=0, tiled=True),
        lax.psum_scatter(first[3], "dp", scatter_dimension=0, tiled=True),
        lax.psum_scatter(first[4], "dp", scatter_dimension=0, tiled=True),
        lax.psum_scatter(first[5], "dp", scatter_dimension=0, tiled=True),
        lax.psum_scatter(first[6], "dp", scatter_dimension=0, tiled=True),
        lax.psum_scatter(first[7], "dp", scatter_dimension=0, tiled=True),
        lax.psum_scatter(first[8], "dp", scatter_dimension=0, tiled=True),
        lax.psum_scatter(first[9], "dp", scatter_dimension=0, tiled=True),
        lax.psum_scatter(first[10], "dp", scatter_dimension=0, tiled=True),
        lax.psum_scatter(first[11], "dp", scatter_dimension=0, tiled=True),
        lax.psum_scatter(first[12], "dp", scatter_dimension=0, tiled=True),
        lax.psum_scatter(second[0], "dp", scatter_dimension=0, tiled=True),
        lax.psum_scatter(second[1], "dp", scatter_dimension=0, tiled=True),
        lax.psum_scatter(second[2], "dp", scatter_dimension=0, tiled=True),
        lax.psum_scatter(second[3], "dp", scatter_dimension=0, tiled=True),
        lax.psum_scatter(second[4], "dp", scatter_dimension=0, tiled=True),
        lax.psum_scatter(second[5], "dp", scatter_dimension=0, tiled=True),
        lax.psum_scatter(second[6], "dp", scatter_dimension=0, tiled=True),
        lax.psum_scatter(second[7], "dp", scatter_dimension=0, tiled=True),
        lax.psum_scatter(second[8], "dp", scatter_dimension=0, tiled=True),
        lax.psum_scatter(second[9], "dp", scatter_dimension=0, tiled=True),
        lax.psum_scatter(second[10], "dp", scatter_dimension=0, tiled=True),
        lax.psum_scatter(second[11], "dp", scatter_dimension=0, tiled=True),
        lax.psum_scatter(second[12], "dp", scatter_dimension=0, tiled=True),
    )
    shared = (
        lax.psum(summed[1].astype(jnp.bfloat16), "tensor").astype(jnp.float32),
        lax.psum(summed[2].astype(jnp.bfloat16), "tensor").astype(jnp.float32),
        lax.psum(summed[7].astype(jnp.bfloat16), "tensor").astype(jnp.float32),
        lax.psum(summed[8].astype(jnp.bfloat16), "tensor").astype(jnp.float32),
        lax.psum(summed[9].astype(jnp.bfloat16), "tensor").astype(jnp.float32),
        lax.psum(summed[10].astype(jnp.bfloat16), "tensor").astype(jnp.float32),
        lax.psum(summed[11].astype(jnp.bfloat16), "tensor").astype(jnp.float32),
        lax.psum(summed[12].astype(jnp.bfloat16), "tensor").astype(jnp.float32),
        lax.psum(summed[14].astype(jnp.bfloat16), "tensor").astype(jnp.float32),
        lax.psum(summed[15].astype(jnp.bfloat16), "tensor").astype(jnp.float32),
        lax.psum(summed[20].astype(jnp.bfloat16), "tensor").astype(jnp.float32),
        lax.psum(summed[21].astype(jnp.bfloat16), "tensor").astype(jnp.float32),
        lax.psum(summed[22].astype(jnp.bfloat16), "tensor").astype(jnp.float32),
        lax.psum(summed[23].astype(jnp.bfloat16), "tensor").astype(jnp.float32),
        lax.psum(summed[24].astype(jnp.bfloat16), "tensor").astype(jnp.float32),
        lax.psum(summed[25].astype(jnp.bfloat16), "tensor").astype(jnp.float32),
    )
    reduced[0] = assemble(summed, shared, 0, 0)
    reduced[1] = assemble(summed, shared, 13, 8)
    final = [jnp.stack([reduced[0][member], reduced[1][member]]) for member in range(13)]
    grad_input = grad_stream.astype(jnp.bfloat16)
    grad_norm_gains = jnp.stack([final[7], final[8], final[9], final[10]], axis=1)
    grad_qk_gains = jnp.stack([final[11], final[12]], axis=1)
    return (
        output,
        grad_input,
        final[0],
        final[1],
        final[2],
        final[3],
        final[4],
        final[5],
        final[6],
        grad_norm_gains,
        grad_qk_gains,
    )


def solution(mesh):
    return jax.shard_map(
        local,
        mesh=mesh,
        in_specs=(
            P(("dp", "tensor"), None),
            P(("dp", "tensor"), None),
            P("dp"),
            P("dp"),
            P(None, None, "tensor"),
            P(),
            P(),
            P(None, "tensor", None),
            P(None, None, "tensor"),
            P(None, None, "tensor"),
            P(None, "tensor", None),
            P(),
            P(),
        ),
        out_specs=(
            P(("dp", "tensor"), None),
            P(("dp", "tensor"), None),
            P(None, "dp", "tensor"),
            P(None, "dp", None),
            P(None, "dp", None),
            P(None, ("tensor", "dp"), None),
            P(None, "dp", "tensor"),
            P(None, "dp", "tensor"),
            P(None, ("tensor", "dp"), None),
            P(None, None, "dp"),
            P(None, None, "dp"),
        ),
        check_vma=False,
    )
```

profile of v0, /device:TPU:0, one launch (start us, length us, event | category | flops | bytes accessed | tf_op | source)
XLA Modules:
  0.0 1291.3 jit_solution(1494286481221944409)
XLA Ops:
  11.9 9.3 all_gather.24
  27.8 23.4 %reduce-scatter.23.cloned.1.call-done = bf16[128,640]{1,0:T(8,128)(2,1)} async-done(((bf16[512,640]{1,0:T(8,128)(2,1)}), bf16[128,640]{1,0:T(8,128)(2,1)}) %reduce-scatter.23.cloned.1.call-update) | async-done | bytes 163856 | tf_op jit(solution)/shard_map/reduce_scatter | solution.py:119
  55.1 7.5 all_gather.25
  67.8 22.9 %reduce-scatter.25.cloned.1.call-done = bf16[128,640]{1,0:T(8,128)(2,1)} async-done(((bf16[512,640]{1,0:T(8,128)(2,1)}), bf16[128,640]{1,0:T(8,128)(2,1)}) %reduce-scatter.25.cloned.1.call-update) | async-done | bytes 163856 | tf_op jit(solution)/shard_map/reduce_scatter | solution.py:128
  93.2 7.6 all_gather.26
  108.4 23.0 %reduce-scatter.27.cloned.1.call-done = bf16[128,640]{1,0:T(8,128)(2,1)} async-done(((bf16[512,640]{1,0:T(8,128)(2,1)}), bf16[128,640]{1,0:T(8,128)(2,1)}) %reduce-scatter.27.cloned.1.call-update) | async-done | bytes 163856 | tf_op jit(solution)/shard_map/reduce_scatter | solution.py:119
  135.0 7.7 all_gather.27
  147.9 22.9 %reduce-scatter.29.cloned.1.call-done = bf16[128,640]{1,0:T(8,128)(2,1)} async-done(((bf16[512,640]{1,0:T(8,128)(2,1)}), bf16[128,640]{1,0:T(8,128)(2,1)}) %reduce-scatter.29.cloned.1.call-update) | async-done | bytes 163856 | tf_op jit(solution)/shard_map/reduce_scatter | solution.py:128
  174.9 7.5 all_gather.28
  189.9 21.6 %reduce-scatter.31.cloned.1.call-done = bf16[128,640]{1,0:T(8,128)(2,1)} async-done(((bf16[512,640]{1,0:T(8,128)(2,1)}), bf16[128,640]{1,0:T(8,128)(2,1)}) %reduce-scatter.31.cloned.1.call-update) | async-done | bytes 163856 | tf_op jit(solution)/shard_map/reduce_scatter | solution.py:188
  218.4 7.5 all_gather.29
  236.3 22.9 %reduce-scatter.33.cloned.1.call-done = bf16[128,640]{1,0:T(8,128)(2,1)} async-done(((bf16[512,640]{1,0:T(8,128)(2,1)}), bf16[128,640]{1,0:T(8,128)(2,1)}) %reduce-scatter.33.cloned.1.call-update) | async-done | bytes 163856 | tf_op jit(solution)/shard_map/reduce_scatter | solution.py:227
  262.4 7.7 all_gather.30
  280.8 18.3 %reduce-scatter.35.cloned.1.call-done = bf16[128,640]{1,0:T(8,128)(2,1)} async-done(((bf16[512,640]{1,0:T(8,128)(2,1)}), bf16[128,640]{1,0:T(8,128)(2,1)}) %reduce-scatter.35.cloned.1.call-update) | async-done | bytes 163856 | tf_op jit(solution)/shard_map/reduce_scatter | solution.py:188
  302.0 7.6 all_gather.31
  343.5 21.1 %reduce-scatter.49.cloned.1.call-done = f32[80,256]{1,0:T(8,128)} async-done(((f32[640,256]{1,0:T(8,128)}), f32[80,256]{1,0:T(8,128)}) %reduce-scatter.49.cloned.1.call-update) | async-done | bytes 81936 | tf_op jit(solution)/shard_map/reduce_scatter | solution.py:345
  366.1 63.3 %reduce-scatter.45.cloned.1.call-done = f32[80,256]{1,0:T(8,128)} async-done(((f32[640,256]{1,0:T(8,128)}), f32[80,256]{1,0:T(8,128)}) %reduce-scatter.45.cloned.1.call-update) | async-done | bytes 81936 | tf_op jit(solution)/shard_map/reduce_scatter | solution.py:344
  430.9 22.3 %reduce-scatter.37.cloned.1.call-done = bf16[128,640]{1,0:T(8,128)(2,1)} async-done(((bf16[512,640]{1,0:T(8,128)(2,1)}), bf16[128,640]{1,0:T(8,128)(2,1)}) %reduce-scatter.37.cloned.1.call-update) | async-done | bytes 163856 | tf_op jit(solution)/shard_map/reduce_scatter | solution.py:227
  454.4 37.8 %all-reduce.20 = (bf16[640]{0:T(1024)(128)(2,1)S(1)}, bf16[640]{0:T(1024)(128)(2,1)S(1)}, bf16[640]{0:T(1024)(128)(2,1)S(1)}, bf16[640]{0:T(1024)(128)(2,1)S(1)}...) all-reduce(f32[640]{0:T(1024)S(1)} %copy-done.97, ...), channel_id=31, replica_groups=mesh['dp'=8,'tensor'=4] {'dp'}, use_global_device_ids=true, to_apply=%region_78.79.clone | all-reduce | flops 6144 | bytes 36864
  499.4 19.4 %reduce-scatter.53.cloned.1.call-done = f32[32,640]{1,0:T(8,128)} async-done(((f32[256,640]{1,0:T(8,128)}), f32[32,640]{1,0:T(8,128)}) %reduce-scatter.53.cloned.1.call-update) | async-done | bytes 81936 | tf_op jit(solution)/shard_map/reduce_scatter | solution.py:346
  518.8 64.6 %reduce-scatter.51.cloned.1.call-done = f32[32,640]{1,0:T(8,128)} async-done(((f32[256,640]{1,0:T(8,128)}), f32[32,640]{1,0:T(8,128)}) %reduce-scatter.51.cloned.1.call-update) | async-done | bytes 81936 | tf_op jit(solution)/shard_map/reduce_scatter | solution.py:333
  585.0 62.9 %reduce-scatter.41.cloned.1.call-done = f32[80,256]{1,0:T(8,128)} async-done(((f32[640,256]{1,0:T(8,128)}), f32[80,256]{1,0:T(8,128)}) %reduce-scatter.41.cloned.1.call-update) | async-done | bytes 81936 | tf_op jit(solution)/shard_map/reduce_scatter | solution.py:343
  647.9 64.6 %reduce-scatter.39.cloned.1.call-done = f32[80,256]{1,0:T(8,128)} async-done(((f32[640,256]{1,0:T(8,128)}), f32[80,256]{1,0:T(8,128)}) %reduce-scatter.39.cloned.1.call-update) | async-done | bytes 81936 | tf_op jit(solution)/shard_map/reduce_scatter | solution.py:330
  714.2 62.8 %reduce-scatter.47.cloned.1.call-done = f32[80,256]{1,0:T(8,128)} async-done(((f32[640,256]{1,0:T(8,128)}), f32[80,256]{1,0:T(8,128)}) %reduce-scatter.47.cloned.1.call-update) | async-done | bytes 81936 | tf_op jit(solution)/shard_map/reduce_scatter | solution.py:332
  778.4 63.1 %reduce-scatter.43.cloned.1.call-done = f32[80,256]{1,0:T(8,128)} async-done(((f32[640,256]{1,0:T(8,128)}), f32[80,256]{1,0:T(8,128)}) %reduce-scatter.43.cloned.1.call-update) | async-done | bytes 81936 | tf_op jit(solution)/shard_map/reduce_scatter | solution.py:331
  843.9 64.3 %reduce-scatter.65.cloned.1.call-done = f32[64,640]{1,0:T(8,128)} async-done(((f32[512,640]{1,0:T(8,128)}), f32[64,640]{1,0:T(8,128)}) %reduce-scatter.65.cloned.1.call-update) | async-done | bytes 163856 | tf_op jit(solution)/shard_map/reduce_scatter | solution.py:349
  908.3 66.6 %reduce-scatter.63.cloned.1.call-done = f32[64,640]{1,0:T(8,128)} async-done(((f32[512,640]{1,0:T(8,128)}), f32[64,640]{1,0:T(8,128)}) %reduce-scatter.63.cloned.1.call-update) | async-done | bytes 163856 | tf_op jit(solution)/shard_map/reduce_scatter | solution.py:336
  976.6 65.1 %reduce-scatter.61.cloned.1.call-done = f32[80,512]{1,0:T(8,128)} async-done(((f32[640,512]{1,0:T(8,128)}), f32[80,512]{1,0:T(8,128)}) %reduce-scatter.61.cloned.1.call-update) | async-done | bytes 163856 | tf_op jit(solution)/shard_map/reduce_scatter | solution.py:348
  1041.7 66.6 %reduce-scatter.59.cloned.1.call-done = f32[80,512]{1,0:T(8,128)} async-done(((f32[640,512]{1,0:T(8,128)}), f32[80,512]{1,0:T(8,128)}) %reduce-scatter.59.cloned.1.call-update) | async-done | bytes 163856 | tf_op jit(solution)/shard_map/reduce_scatter | solution.py:335
  1110.0 65.0 %reduce-scatter.57.cloned.1.call-done = f32[80,512]{1,0:T(8,128)} async-done(((f32[640,512]{1,0:T(8,128)}), f32[80,512]{1,0:T(8,128)}) %reduce-scatter.57.cloned.1.call-update) | async-done | bytes 163856 | tf_op jit(solution)/shard_map/reduce_scatter | solution.py:347
  1175.0 66.7 %reduce-scatter.55.cloned.1.call-done = f32[80,512]{1,0:T(8,128)} async-done(((f32[640,512]{1,0:T(8,128)}), f32[80,512]{1,0:T(8,128)}) %reduce-scatter.55.cloned.1.call-update) | async-done | bytes 163856 | tf_op jit(solution)/shard_map/reduce_scatter | solution.py:334
  1243.5 33.1 %all-reduce.24.cloned.1.call-done = (bf16[1,80,256]{2,1,0:T(8,128)(2,1)}, bf16[1,80,256]{2,1,0:T(8,128)(2,1)}, bf16[1,80,256]{2,1,0:T(8,128)(2,1)}, bf16[1,80,25...) async-done(((bf16[1,80,256]{2,1,0:T(8,128)(2,1)}, ...) | async-done | bytes 165392 | tf_op jit(solution)/shard_map/psum | solution.py:366
  (503 shorter events, 147.2 us)
Async XLA Ops:
  7.2 44.0 %reduce-scatter.23.cloned.1.call-start = ((), (), s32[]{:S(2)}) async-start(), calls=%async_computation.22 | async-start | bytes 819200 | tf_op jit(solution)/shard_map/reduce_scatter | solution.py:119
  9.9 93.4 %copy-start.100 = (f32[1,1,256]{2,1,0:T(1,128)}, f32[1,1,256]{2,1,0:T(1,128)S(1)}, u32[]{:S(2)}) copy-start(f32[1,1,256]{2,1,0:T(1,128)S(1)} %get-tuple-element.223) | copy-start | bytes 3076
  27.7 63.1 %reduce-scatter.25.cloned.1.call-start = ((), (), s32[]{:S(2)}) async-start(), calls=%async_computation.23 | async-start | bytes 819200 | tf_op jit(solution)/shard_map/reduce_scatter | solution.py:128
  67.8 63.5 %reduce-scatter.27.cloned.1.call-start = ((), (), s32[]{:S(2)}) async-start(), calls=%async_computation.24 | async-start | bytes 819200 | tf_op jit(solution)/shard_map/reduce_scatter | solution.py:119
  108.3 62.6 %reduce-scatter.29.cloned.1.call-start = ((), (), s32[]{:S(2)}) async-start(), calls=%async_computation.25 | async-start | bytes 819200 | tf_op jit(solution)/shard_map/reduce_scatter | solution.py:128
  147.9 63.7 %reduce-scatter.31.cloned.1.call-start = ((), (), s32[]{:S(2)}) async-start(), calls=%async_computation.26 | async-start | bytes 819200 | tf_op jit(solution)/shard_map/reduce_scatter | solution.py:188
  188.6 70.7 %reduce-scatter.33.cloned.1.call-start = ((), (), s32[]{:S(2)}) async-start(), calls=%async_computation.27 | async-start | bytes 819200 | tf_op jit(solution)/shard_map/reduce_scatter | solution.py:227
  236.3 62.8 %reduce-scatter.35.cloned.1.call-start = ((), (), s32[]{:S(2)}) async-start(), calls=%async_computation.28 | async-start | bytes 819200 | tf_op jit(solution)/shard_map/reduce_scatter | solution.py:188
  276.1 88.5 %reduce-scatter.49.cloned.1.call-start = ((), (), s32[]{:S(2)}) async-start(), calls=%async_computation.35 | async-start | bytes 737280 | tf_op jit(solution)/shard_map/reduce_scatter | solution.py:345
  278.4 150.9 %reduce-scatter.45.cloned.1.call-start = ((), (), s32[]{:S(2)}) async-start(), calls=%async_computation.33 | async-start | bytes 737280 | tf_op jit(solution)/shard_map/reduce_scatter | solution.py:344
  280.8 172.4 %reduce-scatter.37.cloned.1.call-start = ((), (), s32[]{:S(2)}) async-start(), calls=%async_computation.29 | async-start | bytes 819200 | tf_op jit(solution)/shard_map/reduce_scatter | solution.py:227
  319.5 199.3 %reduce-scatter.53.cloned.1.call-start = ((), (), s32[]{:S(2)}) async-start(), calls=%async_computation.37 | async-start | bytes 737280 | tf_op jit(solution)/shard_map/reduce_scatter | solution.py:346
  321.9 261.5 %reduce-scatter.51.cloned.1.call-start = ((), (), s32[]{:S(2)}) async-start(), calls=%async_computation.36 | async-start | bytes 737280 | tf_op jit(solution)/shard_map/reduce_scatter | solution.py:333
  324.4 323.6 %reduce-scatter.41.cloned.1.call-start = ((), (), s32[]{:S(2)}) async-start(), calls=%async_computation.31 | async-start | bytes 737280 | tf_op jit(solution)/shard_map/reduce_scatter | solution.py:343
  325.7 386.8 %reduce-scatter.39.cloned.1.call-start = ((), (), s32[]{:S(2)}) async-start(), calls=%async_computation.30 | async-start | bytes 737280 | tf_op jit(solution)/shard_map/reduce_scatter | solution.py:330
  327.1 449.8 %reduce-scatter.47.cloned.1.call-start = ((), (), s32[]{:S(2)}) async-start(), calls=%async_computation.34 | async-start | bytes 737280 | tf_op jit(solution)/shard_map/reduce_scatter | solution.py:332
  328.4 513.2 %reduce-scatter.43.cloned.1.call-start = ((), (), s32[]{:S(2)}) async-start(), calls=%async_computation.32 | async-start | bytes 737280 | tf_op jit(solution)/shard_map/reduce_scatter | solution.py:331
  329.8 578.5 %reduce-scatter.65.cloned.1.call-start = ((), (), s32[]{:S(2)}) async-start(), calls=%async_computation.43 | async-start | bytes 1474560 | tf_op jit(solution)/shard_map/reduce_scatter | solution.py:349
  332.7 642.2 %reduce-scatter.63.cloned.1.call-start = ((), (), s32[]{:S(2)}) async-start(), calls=%async_computation.42 | async-start | bytes 1474560 | tf_op jit(solution)/shard_map/reduce_scatter | solution.py:336
  334.5 707.3 %reduce-scatter.61.cloned.1.call-start = ((), (), s32[]{:S(2)}) async-start(), calls=%async_computation.41 | async-start | bytes 1474560 | tf_op jit(solution)/shard_map/reduce_scatter | solution.py:348
  336.1 772.1 %reduce-scatter.59.cloned.1.call-start = ((), (), s32[]{:S(2)}) async-start(), calls=%async_computation.40 | async-start | bytes 1474560 | tf_op jit(solution)/shard_map/reduce_scatter | solution.py:335
  338.1 836.9 %reduce-scatter.57.cloned.1.call-start = ((), (), s32[]{:S(2)}) async-start(), calls=%async_computation.39 | async-start | bytes 1474560 | tf_op jit(solution)/shard_map/reduce_scatter | solution.py:347
  339.8 901.9 %reduce-scatter.55.cloned.1.call-start = ((), (), s32[]{:S(2)}) async-start(), calls=%async_computation.38 | async-start | bytes 1474560 | tf_op jit(solution)/shard_map/reduce_scatter | solution.py:334
  343.4 109.8 %copy-start.112 = (f32[128]{0:T(128)S(1)}, f32[128]{0:T(128)}, u32[]{:S(2)}) copy-start(f32[128]{0:T(128)} %copy-done.111) | copy-start | bytes 1540
  343.4 111.0 %copy-start.97 = (f32[640]{0:T(1024)S(1)}, f32[640]{0:T(1024)}, u32[]{:S(2)}) copy-start(f32[640]{0:T(1024)} %get-tuple-element.157) | copy-start | bytes 7684
  343.4 111.0 %copy-start.98 = (f32[640]{0:T(1024)S(1)}, f32[640]{0:T(1024)}, u32[]{:S(2)}) copy-start(f32[640]{0:T(1024)} %get-tuple-element.151) | copy-start | bytes 7684
  343.4 111.0 %copy-start.99 = (f32[640]{0:T(1024)S(1)}, f32[640]{0:T(1024)}, u32[]{:S(2)}) copy-start(f32[640]{0:T(1024)} %get-tuple-element.149) | copy-start | bytes 7684
  343.4 111.0 %copy-start.122 = (f32[256]{0:T(256)S(1)}, f32[256]{0:T(256)}, u32[]{:S(2)}) copy-start(f32[256]{0:T(256)} %get-tuple-element.141) | copy-start | bytes 3076
  343.4 370.8 %copy-start.128 = (f32[128]{0:T(128)S(1)}, f32[128]{0:T(128)}, u32[]{:S(2)}) copy-start(f32[128]{0:T(128)} %copy-done.127) | copy-start | bytes 1540
  343.4 499.7 %copy-start.18 = (f32[128,640]{1,0:T(8,128)S(1)}, f32[128,640]{1,0:T(8,128)}, u32[]{:S(2)}) copy-start(f32[128,640]{1,0:T(8,128)} %copy-done.17) | copy-start | bytes 983044
  343.4 933.2 %all-reduce.24.cloned.1.call-start = ((), (), s32[]{:S(2)}) async-start(), calls=%async_computation.44 | async-start | bytes 339968 | tf_op jit(solution)/shard_map/psum | solution.py:366
  453.2 389.9 %copy-start.70 = (bf16[128,640]{1,0:T(8,128)(2,1)S(1)}, bf16[128,640]{1,0:T(8,128)(2,1)}, u32[]{:S(2)}) copy-start(bf16[128,640]{1,0:T(8,128)(2,1)} %reduce-scatter.37.cloned.1.call-done) | copy-start | bytes 491524
  (138 other events, 864.6 us)
Sparse Core Ops, SparseCore 0:
  27.8 23.3 reduce-scatter.22
  67.9 22.8 reduce-scatter.24
  108.4 22.8 reduce-scatter.26
  148.0 22.8 reduce-scatter.28
  188.7 22.8 reduce-scatter.30
  236.4 22.8 reduce-scatter.32
  276.3 22.8 reduce-scatter.34
  302.4 62.1 reduce-scatter.48
  368.2 61.0 reduce-scatter.44
  431.7 21.4 reduce-scatter.36
  456.5 62.3 reduce-scatter.52
  522.3 61.0 reduce-scatter.50
  586.7 61.1 reduce-scatter.40
  651.4 61.0 reduce-scatter.38
  715.7 61.2 reduce-scatter.46
  780.4 61.1 reduce-scatter.42
  844.8 63.4 reduce-scatter.64
  911.5 63.3 reduce-scatter.62
  978.3 63.4 reduce-scatter.60
  1045.0 63.2 reduce-scatter.58
  1111.7 63.2 reduce-scatter.56
  1178.4 63.2 reduce-scatter.54
  1246.3 30.2 all-reduce.23
where the time goes:
time: 1290 us
  waiting for transfers between devices  1030 us (80%)
  blocking collectives  100 us (8%)
  other arithmetic  60.6 us (5%)
  matrix products  59.1 us (5%)
  local copies, waits for them, and re-layouts  25.8 us (2%)
  between operations  17.2 us (1%)
    reduce_scatter x1, waiting for transfers between devices, local(): lax.psum_scatter(first[4], 'dp', scatter_dimension=0, tiled=True)  66.7 us
    reduce_scatter x1, waiting for transfers between devices, local(): lax.psum_scatter(first[6], 'dp', scatter_dimension=0, tiled=True)  66.6 us
    reduce_scatter x1, waiting for transfers between devices, local(): lax.psum_scatter(first[5], 'dp', scatter_dimension=0, tiled=True)  66.6 us
    reduce_scatter x1, waiting for transfers between devices, local(): lax.psum_scatter(second[5], 'dp', scatter_dimension=0, tiled=True)  65.1 us
    reduce_scatter x1, waiting for transfers between devices, local(): lax.psum_scatter(second[4], 'dp', scatter_dimension=0, tiled=True)  65 us
    reduce_scatter x1, waiting for transfers between devices, local(): lax.psum_scatter(first[0], 'dp', scatter_dimension=0, tiled=True)  64.6 us
    reduce_scatter x1, waiting for transfers between devices, local(): lax.psum_scatter(first[3], 'dp', scatter_dimension=0, tiled=True)  64.6 us
    reduce_scatter x1, waiting for transfers between devices, local(): lax.psum_scatter(second[6], 'dp', scatter_dimension=0, tiled=True)  64.3 us
  transfers between devices with their start and end apart: 23, of which 23 were waited for; matrix products, arithmetic and copies ran while one was open for 5% of the time, Pallas kernels for 0%

commit v1 on v0

v1 whole, which is shorter than its diff:
```python
import jax
import jax.numpy as jnp
from jax import lax
from jax.sharding import PartitionSpec as P

WINDOW = 512
SEQ_LEN = 512
LANES = 128
GAIN_ROWS = 16

epsilon = 1e-06
score_scale = 0.0625
masked_fill = -1e30
thetas = (10000.0, 1000000.0)


def product(left, right):
    return jnp.dot(left, right, preferred_element_type=jnp.float32)


def product_left(left, right):
    return lax.dot_general(
        left, right, (((0,), (0,)), ((), ())), preferred_element_type=jnp.float32
    )


def product_right(left, right):
    return lax.dot_general(
        left, right, (((1,), (1,)), ((), ())), preferred_element_type=jnp.float32
    )


def rms_scale(vector, gain_row):
    return (
        vector * lax.rsqrt(jnp.mean(vector * vector, axis=-1, keepdims=True) + epsilon) * gain_row
    )


def angles(place, width, theta):
    half_width = width // 2
    frequency = theta ** (-(2.0 * jnp.arange(half_width, dtype=jnp.float32)) / width)
    phases = place.astype(jnp.float32)[:, None] * frequency[None, :]
    return (jnp.cos(phases), jnp.sin(phases))


def rotate(vector, cosine, sine):
    half_width = vector.shape[-1] // 2
    first_half = vector[:, :half_width]
    second_half = vector[:, half_width:]
    return jnp.concatenate(
        [first_half * cosine - second_half * sine, second_half * cosine + first_half * sine],
        axis=-1,
    )


def allowed_mask(seg_piece, place, window):
    return (
        (seg_piece[:, None] == seg_piece[None, :])
        & (place[None, :] <= place[:, None])
        & (place[:, None] - place[None, :] < window)
    )


def swap(array, axis, bit):
    size = lax.axis_size(axis)
    return lax.ppermute(array, axis, [(i, i ^ bit) for i in range(size)])


def relative_order(array, quarter):
    parts = array.reshape((4, -1) + array.shape[1:])
    return jnp.concatenate(
        [lax.dynamic_index_in_dim(parts, quarter ^ bit, 0, False) for bit in (0, 2, 1, 3)]
    )


def own_rows(partial):
    half = partial.shape[0] // 2
    low = partial.astype(jnp.bfloat16)
    pair = (
        low[:half].astype(jnp.float32) + swap(low[half:], "tensor", 1).astype(jnp.float32)
    ).astype(jnp.bfloat16)
    other = swap(pair, "tensor", 2)
    quarter = half // 2
    flipped = jnp.concatenate([other[quarter:], other[:quarter]])
    return pair.astype(jnp.float32) + flipped.astype(jnp.float32)


def all_rows(own):
    return jnp.concatenate([own, swap(own, "tensor", 1)])


def two_quarters(array):
    return jnp.concatenate([array, swap(array, "tensor", 2)])


def norm_back(vector, gain_row, grad_out):
    unused, pullback = jax.vjp(rms_scale, vector, gain_row)
    return pullback(grad_out)


def attend_forward(queries, key_rows, values, allowed):
    scores = product_right(queries, key_rows) * score_scale
    masked = jnp.where(allowed, scores, masked_fill)
    row_max = jnp.max(masked, axis=-1, keepdims=True)
    expo = jnp.where(allowed, jnp.exp(masked - row_max), 0.0)
    row_sum = jnp.sum(expo, axis=-1, keepdims=True)
    probability = (expo / row_sum).astype(jnp.bfloat16)
    attended = product(probability, values)
    return (attended, row_max + jnp.log(row_sum))


def attend_backward(queries, key_rows, values, allowed, row_lse, grad_out):
    scores = product_right(queries, key_rows) * score_scale
    probability = jnp.where(allowed, jnp.exp(scores - row_lse), 0.0)
    prob_low = probability.astype(jnp.bfloat16)
    grad_values = product_left(prob_low, grad_out).astype(jnp.bfloat16)
    grad_prob = product_right(grad_out, values)
    inner_sum = jnp.sum(probability * grad_prob, axis=-1, keepdims=True)
    grad_scores = (probability * (grad_prob - inner_sum)).astype(jnp.bfloat16)
    grad_queries = (product(grad_scores, key_rows) * score_scale).astype(jnp.bfloat16)
    grad_keys = (product_left(grad_scores, queries) * score_scale).astype(jnp.bfloat16)
    return (grad_queries, grad_keys, grad_values)


def gated_unit(gate_in, up_in):
    return jax.nn.gelu(gate_in, approximate=True) * up_in


def layer_forward(stream, weights, allowed, cosine, sine):
    w_query, w_key, w_value, w_out, w_gate, w_up, w_down, gains, qk_gain = weights
    normed = all_rows(rms_scale(stream, gains[0]).astype(jnp.bfloat16))
    query_raw = product(normed, w_query)
    key_raw = product(normed, w_key)
    values = product(normed, w_value).astype(jnp.bfloat16)
    queries = rotate(rms_scale(query_raw, qk_gain[0]), cosine, sine).astype(jnp.bfloat16)
    key_rows = rotate(rms_scale(key_raw, qk_gain[1]), cosine, sine).astype(jnp.bfloat16)
    attended, row_lse = attend_forward(queries, key_rows, values, allowed)
    attn_low = attended.astype(jnp.bfloat16)
    attn_sum = own_rows(product(attn_low, w_out))
    middle = stream + rms_scale(attn_sum, gains[1])
    normed_mlp = all_rows(rms_scale(middle, gains[2]).astype(jnp.bfloat16))
    gate_pre = product(normed_mlp, w_gate)
    up_pre = product(normed_mlp, w_up)
    hidden = gated_unit(gate_pre, up_pre).astype(jnp.bfloat16)
    mlp_sum = own_rows(product(hidden, w_down))
    result = middle + rms_scale(mlp_sum, gains[3])
    saved = (
        stream,
        normed,
        query_raw,
        key_raw,
        queries,
        key_rows,
        values,
        row_lse,
        attn_low,
        attn_sum,
        middle,
        normed_mlp,
        gate_pre,
        up_pre,
        hidden,
        mlp_sum,
    )
    return (result, saved)


def layer_backward(grad_stream, weights, saved, allowed, cosine, sine):
    w_query, w_key, w_value, w_out, w_gate, w_up, w_down, gains, qk_gain = weights
    (
        stream,
        normed,
        query_raw,
        key_raw,
        queries,
        key_rows,
        values,
        row_lse,
        attn_low,
        attn_sum,
        middle,
        normed_mlp,
        gate_pre,
        up_pre,
        hidden,
        mlp_sum,
    ) = saved
    grad_mlp, grad_gain3 = norm_back(mlp_sum, gains[3], grad_stream)
    mlp_low = all_rows(grad_mlp.astype(jnp.bfloat16))
    grad_hidden = product_right(mlp_low, w_down)
    unused, gate_pull = jax.vjp(gated_unit, gate_pre, up_pre)
    grad_gate, grad_up = gate_pull(grad_hidden)
    gate_low = grad_gate.astype(jnp.bfloat16)
    up_low = grad_up.astype(jnp.bfloat16)
    grad_normed_mlp = own_rows(product_right(gate_low, w_gate) + product_right(up_low, w_up))
    grad_w_down = product_left(hidden, mlp_low)
    grad_w_gate = product_left(normed_mlp, gate_low)
    grad_w_up = product_left(normed_mlp, up_low)
    grad_middle_norm, grad_gain2 = norm_back(middle, gains[2], grad_normed_mlp)
    grad_middle = grad_stream + grad_middle_norm
    grad_attn, grad_gain1 = norm_back(attn_sum, gains[1], grad_middle)
    attn_grad_low = all_rows(grad_attn.astype(jnp.bfloat16))
    grad_attended = product_right(attn_grad_low, w_out).astype(jnp.bfloat16)
    grad_queries, grad_keys, grad_values = attend_backward(
        queries, key_rows, values, allowed, row_lse, grad_attended
    )

    def qk_chain(raw_rows, gain_row):
        return rotate(rms_scale(raw_rows, gain_row), cosine, sine)

    unused, query_pull = jax.vjp(qk_chain, query_raw, qk_gain[0])
    grad_query_raw, grad_query_gain = query_pull(grad_queries.astype(jnp.float32))
    unused, key_pull = jax.vjp(qk_chain, key_raw, qk_gain[1])
    grad_key_raw, grad_key_gain = key_pull(grad_keys.astype(jnp.float32))
    query_low = grad_query_raw.astype(jnp.bfloat16)
    key_low = grad_key_raw.astype(jnp.bfloat16)
    grad_normed = own_rows(
        product_right(query_low, w_query)
        + product_right(key_low, w_key)
        + product_right(grad_values, w_value)
    )
    grad_w_out = product_left(attn_low, attn_grad_low)
    grad_w_query = product_left(normed, query_low)
    grad_w_key = product_left(normed, key_low)
    grad_w_value = product_left(normed, grad_values)
    grad_stream_norm, grad_gain0 = norm_back(stream, gains[0], grad_normed)
    grad_input = grad_middle + grad_stream_norm
    mlp_grads = (grad_w_gate, grad_w_up, grad_w_down)
    attn_grads = (grad_w_query, grad_w_out, grad_w_key, grad_w_value)
    norm_gain_grads = jnp.stack([grad_gain0, grad_gain1, grad_gain2, grad_gain3])
    qk_gain_grads = jnp.stack([grad_query_gain, grad_key_gain])
    return (grad_input, mlp_grads, attn_grads, norm_gain_grads, qk_gain_grads)


def packed(array, pieces):
    rows, columns = array.shape
    low = array.astype(jnp.bfloat16).reshape(pieces, rows // pieces, columns // LANES, LANES)
    return low.transpose(0, 2, 1, 3).reshape(pieces, -1, LANES)


def unpacked(rows, columns):
    count = columns // LANES
    return rows.reshape(count, -1, LANES).transpose(1, 0, 2).reshape(-1, columns)


def packed_gains(norm_gain_grads, qk_gain_grads, pieces):
    def spread(array):
        count, columns = array.shape
        block = array.reshape(count, pieces, columns // pieces).transpose(1, 0, 2)
        return jnp.pad(block, ((0, 0), (0, 0), (0, LANES - columns // pieces)))

    block = jnp.concatenate([spread(norm_gain_grads * 0.5), spread(qk_gain_grads)], axis=1)
    return jnp.pad(block, ((0, 0), (0, GAIN_ROWS - block.shape[1]), (0, 0))).astype(jnp.bfloat16)


def halved(blocks):
    me = lax.axis_index("dp")
    bit = 1
    while blocks.shape[0] > 1:
        low = blocks.astype(jnp.bfloat16).reshape((-1, 2) + blocks.shape[1:])
        side = jnp.bitwise_and(me // bit, 1)
        kept = lax.dynamic_index_in_dim(low, side, 1, False)
        sent = lax.dynamic_index_in_dim(low, 1 - side, 1, False)
        blocks = kept.astype(jnp.float32) + swap(sent, "dp", bit).astype(jnp.float32)
        bit *= 2
    return blocks[0]


def over_tensor(rows):
    for bit in (1, 2):
        low = rows.astype(jnp.bfloat16)
        rows = low.astype(jnp.float32) + swap(low, "tensor", bit).astype(jnp.float32)
    return rows


def local(
    hidden_in,
    cotangent,
    segments,
    positions,
    w_query,
    w_key,
    w_value,
    w_out,
    w_gate,
    w_up,
    w_down,
    norm_gains,
    qk_gains,
):
    head_width = w_key.shape[2]
    windows = (WINDOW, SEQ_LEN)
    pieces = lax.axis_size("dp")
    quarter = lax.axis_index("tensor")
    seg_rows = relative_order(segments, quarter)
    pos_rows = relative_order(positions, quarter)
    places = relative_order(jnp.arange(SEQ_LEN, dtype=jnp.int32), quarter)
    stream = two_quarters(hidden_in).astype(jnp.float32)
    saved_all = []
    tables = []
    layer_weights = []
    for layer_idx in range(2):
        cosine, sine = angles(pos_rows, head_width, thetas[layer_idx])
        allowed = allowed_mask(seg_rows, places, windows[layer_idx])
        weights = (
            w_query[layer_idx],
            w_key[layer_idx],
            w_value[layer_idx],
            w_out[layer_idx],
            w_gate[layer_idx],
            w_up[layer_idx],
            w_down[layer_idx],
            norm_gains[layer_idx],
            qk_gains[layer_idx],
        )
        stream, saved = layer_forward(stream, weights, allowed, cosine, sine)
        saved_all.append(saved)
        tables.append((allowed, cosine, sine))
        layer_weights.append(weights)
    own = hidden_in.shape[0]
    output = stream[:own].astype(jnp.bfloat16)
    grad_stream = two_quarters(cotangent).astype(jnp.float32)

    grad_stream, mlp1, attn1, norm1, qk1 = layer_backward(
        grad_stream, layer_weights[1], saved_all[1], *tables[1]
    )
    whole = jnp.concatenate([packed(g, pieces) for g in mlp1 + attn1], axis=1)
    rows1 = lax.psum_scatter(
        whole.reshape(-1, LANES), "dp", scatter_dimension=0, tiled=True
    ).astype(jnp.float32)

    grad_stream, mlp0, attn0, norm0, qk0 = layer_backward(
        grad_stream, layer_weights[0], saved_all[0], *tables[0]
    )
    mlp_rows0 = halved(jnp.concatenate([packed(g, pieces) for g in mlp0], axis=1))
    attn_rows0 = halved(jnp.concatenate([packed(g, pieces) for g in attn0], axis=1))
    gain_rows = halved(
        jnp.concatenate(
            [packed_gains(norm0, qk0, pieces), packed_gains(norm1, qk1, pieces)], axis=1
        )
    )
    rows0 = jnp.concatenate([mlp_rows0, attn_rows0])

    sizes = [w.shape[0] * w.shape[1] // (LANES * pieces) for w in mlp1 + attn1]
    columns = [w.shape[1] for w in mlp1 + attn1]
    starts = [sum(sizes[:i]) for i in range(len(sizes) + 1)]
    shared = over_tensor(
        jnp.concatenate([rows1[starts[5] :], rows0[starts[5] :], gain_rows])
    )
    both = sizes[5] + sizes[6]

    def outs(member):
        if member < 5:
            picks = [rows[starts[member] : starts[member + 1]] for rows in (rows0, rows1)]
        else:
            offset = starts[member] - starts[5]
            picks = [
                shared[base + offset : base + offset + sizes[member]] for base in (both, 0)
            ]
        return jnp.stack([unpacked(rows, columns[member]) for rows in picks])

    gains = shared[2 * both :].reshape(2, GAIN_ROWS, LANES)
    grad_norm_gains = gains[:, :4, : norm_gains.shape[2] // pieces]
    grad_qk_gains = gains[:, 4:6, : qk_gains.shape[2] // pieces]
    grad_input = grad_stream[:own].astype(jnp.bfloat16)
    return (
        output,
        grad_input,
        outs(3),
        outs(5),
        outs(6),
        outs(4),
        outs(0),
        outs(1),
        outs(2),
        grad_norm_gains,
        grad_qk_gains,
    )


def solution(mesh):
    return jax.shard_map(
        local,
        mesh=mesh,
        in_specs=(
            P(("dp", "tensor"), None),
            P(("dp", "tensor"), None),
            P("dp"),
            P("dp"),
            P(None, None, "tensor"),
            P(),
            P(),
            P(None, "tensor", None),
            P(None, None, "tensor"),
            P(None, None, "tensor"),
            P(None, "tensor", None),
            P(),
            P(),
        ),
        out_specs=(
            P(("dp", "tensor"), None),
            P(("dp", "tensor"), None),
            P(None, "dp", "tensor"),
            P(None, "dp", None),
            P(None, "dp", None),
            P(None, ("tensor", "dp"), None),
            P(None, "dp", "tensor"),
            P(None, "dp", "tensor"),
            P(None, ("tensor", "dp"), None),
            P(None, None, "dp"),
            P(None, None, "dp"),
        ),
        check_vma=False,
    )
```

time: 1290 us -> 333 us (0.26)
  waiting for transfers between devices: 1030 us -> 98.5 us
  blocking collectives: 100 us -> 0 us
  local copies, waits for them, and re-layouts: 25.8 us -> 71.2 us
  starting transfers between devices: 1.22 us -> 33.3 us
    reduce_scatter x22 -> x1, waiting for transfers between devices: 994 us -> 0.02 us  [local(): lax.psum_scatter(whole.reshape(-1, LANES), 'dp', scatter_dimension=0, til...]
    ppermute x0 -> x37, waiting for transfers between devices: none -> 98.5 us  [swap(): return lax.ppermute(array, axis, [(i, i ^ bit) for i in range(size)])]
    all_gather x8 -> x0, blocking collectives: 62.5 us -> none  [the longest x2 16.9 us: layer_forward(): normed = lax.all_gather(normed_share, 'tensor', axis=0, tiled=True)]
    unnamed x1 -> x0, blocking collectives: 37.8 us -> none
    ppermute x0 -> x37, starting transfers between devices: none -> 33.3 us  [swap(): return lax.ppermute(array, axis, [(i, i ^ bit) for i in range(size)])]
    psum x1 -> x0, waiting for transfers between devices: 33.1 us -> none  [local(): lax.psum(summed[14].astype(jnp.bfloat16), 'tensor').astype(jnp.float32)]
    reshape x0 -> x27, local copies, waits for them, and re-layouts: none -> 23.2 us  [the longest x24 23 us: packed(): array.astype(jnp.bfloat16)]
  transfers between devices with their start and end apart: 23 -> 38, of which waited for: 23 -> 26; matrix products, arithmetic and copies ran while one was open for 5% -> 30% of each run, Pallas kernels for 0% -> 0%
where the time goes in v1:
time: 333 us; the launch traced here: 329 us
  waiting for transfers between devices  98.5 us (30%)
  local copies, waits for them, and re-layouts  71.2 us (21%)
  other arithmetic  56 us (17%)
  matrix products  52.2 us (16%)
  starting transfers between devices  33.3 us (10%)
  between operations  17.2 us (5%)
    ppermute x37, waiting for transfers between devices, swap(): return lax.ppermute(array, axis, [(i, i ^ bit) for i in range(size)])  98.5 us
    ppermute x37, starting transfers between devices, swap(): return lax.ppermute(array, axis, [(i, i ^ bit) for i in range(size)])  33.3 us
    dot_general x18, matrix products, product_left(): lax.dot_general(left, right, (((0,), (0,)), ((), ())), preferred_element_...  24.6 us
    reshape x24, local copies, waits for them, and re-layouts, packed(): array.astype(jnp.bfloat16)  23 us
    unnamed x386, local copies, waits for them, and re-layouts  22.8 us
    dot_general x18, matrix products, product_right(): lax.dot_general(left, right, (((1,), (1,)), ((), ())), preferred_element_...  15.5 us
    another operation x4, other arithmetic  15.4 us
    dot_general x18, matrix products, product(): return jnp.dot(left, right, preferred_element_type=jnp.float32)  12.1 us
  transfers between devices with their start and end apart: 38, of which 26 were waited for; matrix products, arithmetic and copies ran while one was open for 30% of the time, Pallas kernels for 0%

profile of v1, /device:TPU:0, one launch (start us, length us, event | category | flops | bytes accessed | tf_op | source)
XLA Modules:
  0.0 328.5 jit_solution(11018300408586571119)
XLA Ops:
  7.2 3.0 collective-permute-start
  30.2 8.0 %collective-permute-done.3 = bf16[256,640]{1,0:T(8,128)(2,1)S(1)} collective-permute-done((bf16[256,640]{1,0:T(8,128)(2,1)S(1)}, bf16[256,640]{1,0:T(8,128)(2,1)S(1)}, u32[]{:S(2)}, u32[]{:S(2)}) %collective-permute-start.3) | collective-permute-done | bytes 327712 | tf_op jit(solution)/shard_map/ppermute | solution.py:66
  47.8 8.0 %collective-permute-done.6 = bf16[256,640]{1,0:T(8,128)(2,1)S(1)} collective-permute-done((bf16[256,640]{1,0:T(8,128)(2,1)S(1)}, bf16[256,640]{1,0:T(8,128)(2,1)S(1)}, u32[]{:S(2)}, u32[]{:S(2)}) %collective-permute-start.6) | collective-permute-done | bytes 327712 | tf_op jit(solution)/shard_map/ppermute | solution.py:66
  59.8 12.7 %fusion.174 = (bf16[512,128]{0,1:T(8,128)(2,1)S(1)}, bf16[512,128]{0,1:T(8,128)(2,1)S(1)}, bf16[512,128]{0,1:T(8,128)(2,1)S(1)}, bf16[512,128]{0,1:T(8,128)(2,1)S(1)}) fusion(f32[512,256]{0,1:T(8,128)S(1)} %multiply_multiply_fusion.7, f32[128]{0:T(128)S(1)} %broadcast_power_fusion, f32[512]{0:T(512)S(1)} %add_convert_fusion.10, ...), kind=kLoop, calls=%fused_computation.359 | loop fusion | flops 1114112 | bytes 1575424 | tf_op jit(solution)/shard_map/convert.45
  79.2 8.0 %collective-permute-done.9 = bf16[256,640]{1,0:T(8,128)(2,1)S(1)} collective-permute-done((bf16[256,640]{1,0:T(8,128)(2,1)S(1)}, bf16[256,640]{1,0:T(8,128)(2,1)S(1)}, u32[]{:S(2)}, u32[]{:S(2)}) %collective-permute-start.9) | collective-permute-done | bytes 327712 | tf_op jit(solution)/shard_map/ppermute | solution.py:66
  98.7 1.9 fusion.247
  100.5 5.8 %collective-permute-done.12 = bf16[256,640]{1,0:T(8,128)(2,1)} collective-permute-done((bf16[256,640]{1,0:T(8,128)(2,1)}, bf16[256,640]{1,0:T(8,128)(2,1)}, u32[]{:S(2)}, u32[]{:S(2)}) %collective-permute-start.12) | collective-permute-done | bytes 327712 | tf_op jit(solution)/shard_map/ppermute | solution.py:66
  120.6 2.7 convolution_convert_fusion.7
  128.3 2.3 reshape.602
  130.6 2.0 copy.114
  132.6 2.3 reshape.604
  135.0 2.2 copy.115
  138.6 2.6 reshape.606
  145.5 2.2 multiply_reduce_fusion.3
  172.4 2.3 convolution_convert_fusion.11
  181.1 6.8 %collective-permute-done.19 = bf16[256,640]{1,0:T(8,128)(2,1)} collective-permute-done((bf16[256,640]{1,0:T(8,128)(2,1)S(1)}, bf16[256,640]{1,0:T(8,128)(2,1)}, u32[]{:S(2)}, u32[]{:S(2)}) %collective-permute-start.19) | collective-permute-done | bytes 327712 | tf_op jit(solution)/shard_map/ppermute | solution.py:66
  193.5 3.2 multiply_convert_fusion.1
  201.3 1.8 convolution_convert_fusion.2
  204.6 6.4 %collective-permute-done.22 = bf16[256,640]{1,0:T(8,128)(2,1)S(1)} collective-permute-done((bf16[256,640]{1,0:T(8,128)(2,1)S(1)}, bf16[256,640]{1,0:T(8,128)(2,1)S(1)}, u32[]{:S(2)}, u32[]{:S(2)}) %collective-permute-start.22) | collective-permute-done | bytes 327712 | tf_op jit(solution)/shard_map/ppermute | solution.py:66
  234.3 2.1 convolution_convert_fusion.15
  238.2 2.3 convolution_convert_fusion.16
  242.6 2.1 convolution_convert_fusion.17
  245.8 6.9 %collective-permute-done.34 = bf16[4,960,128]{2,1,0:T(8,128)(2,1)} collective-permute-done((bf16[4,960,128]{2,1,0:T(8,128)(2,1)}, bf16[4,960,128]{2,1,0:T(8,128)(2,1)}, u32[]{:S(2)}, u32[]{:S(2)}) %collective-permute-start.34) | collective-permute-done | bytes 983072 | tf_op jit(solution)/shard_map/ppermute | solution.py:66
  261.1 14.3 %collective-permute-done.35 = bf16[2,960,128]{2,1,0:T(8,128)(2,1)} collective-permute-done((bf16[2,960,128]{2,1,0:T(8,128)(2,1)}, bf16[2,960,128]{2,1,0:T(8,128)(2,1)}, u32[]{:S(2)}, u32[]{:S(2)}) %collective-permute-start.35) | collective-permute-done | bytes 491552 | tf_op jit(solution)/shard_map/ppermute | solution.py:66
  276.6 5.5 %collective-permute-start.36 = (bf16[1,960,128]{2,1,0:T(8,128)(2,1)S(1)}, bf16[1,960,128]{2,1,0:T(8,128)(2,1)S(1)}, u32[]{:S(2)}, u32[]{:S(2)}) collective-permute-start(bf16[1,960,128]{2,1,0:T(8,128)(2,1)S(1)} %constant_dynamic-slice_fusion), channel_id=1, source_target_pairs={{0,16},{4,20},{8,24},{12,28},{16,0},{20,4},{24,8},{28,12},{1,17},{... | collective-permute-start | bytes 737288 | tf_op jit(solution)/shard_map/ppermute | solution.py:66
  283.3 2.7 collective-permute-start.29
  288.0 2.7 collective-permute-start.30
  290.8 2.6 collective-permute-done.30
  294.3 4.0 %collective-permute-done.31 = bf16[1,32,128]{2,1,0:T(8,128)(2,1)S(1)} collective-permute-done((bf16[1,32,128]{2,1,0:T(8,128)(2,1)S(1)}, bf16[1,32,128]{2,1,0:T(8,128)(2,1)S(1)}, u32[]{:S(2)}, u32[]{:S(2)}) %collective-permute-start.31) | collective-permute-done | bytes 8224 | tf_op jit(solution)/shard_map/ppermute | solution.py:66
  298.5 2.0 collective-permute-start.28
  301.0 5.5 %collective-permute-done.28 = bf16[1,640,128]{2,1,0:T(8,128)(2,1)S(1)} collective-permute-done((bf16[1,640,128]{2,1,0:T(8,128)(2,1)S(1)}, bf16[1,640,128]{2,1,0:T(8,128)(2,1)S(1)}, u32[]{:S(2)}, u32[]{:S(2)}) %collective-permute-start.28) | collective-permute-done | bytes 163872 | tf_op jit(solution)/shard_map/ppermute | solution.py:66
  313.2 5.2 %collective-permute-done.33 = bf16[672,128]{1,0:T(8,128)(2,1)S(1)} collective-permute-done((bf16[672,128]{1,0:T(8,128)(2,1)S(1)}, bf16[672,128]{1,0:T(8,128)(2,1)S(1)}, u32[]{:S(2)}, u32[]{:S(2)}) %collective-permute-start.33) | collective-permute-done | bytes 172064 | tf_op jit(solution)/shard_map/ppermute | solution.py:66
  (707 shorter events, 169.3 us)
Async XLA Ops:
  7.2 299.7 %reduce-scatter.2.cloned.1.call-start = ((), (), s32[]{:S(2)}) async-start(), calls=%async_computation.1 | async-start | bytes 3686400 | tf_op jit(solution)/shard_map/reduce_scatter | solution.py:328
  7.2 7.4 %collective-permute-start = (bf16[128,640]{1,0:T(8,128)(2,1)}, bf16[128,640]{1,0:T(8,128)(2,1)S(1)}, u32[]{:S(2)}, u32[]{:S(2)}) collective-permute-start(bf16[128,640]{1,0:T(8,128)(2,1)} %param.13), channel_id=1, source_target_pairs={{0,2},{1,3},{2,0},{3,1},{4,6},{5,7},{6,4},{7,5},{8,10},{9,11},{10,... | collective-permute-start | bytes 491528 | tf_op jit(solution)/shard_map/ppermute | solution.py:66
  17.5 1.7 collective-permute-start.1
  28.4 9.8 %collective-permute-start.3 = (bf16[256,640]{1,0:T(8,128)(2,1)S(1)}, bf16[256,640]{1,0:T(8,128)(2,1)S(1)}, u32[]{:S(2)}, u32[]{:S(2)}) collective-permute-start(bf16[256,640]{1,0:T(8,128)(2,1)S(1)} %add_convert_fusion.7), channel_id=1, source_target_pairs={{0,2},{1,3},{2,0},{3,1},{4,6},{5,7},{6,4},{7,5},{8,10},{9,11},{10,... | collective-permute-start | bytes 983048 | tf_op jit(solution)/shard_map/ppermute | solution.py:66
  39.2 1.7 collective-permute-start.4
  44.2 1.7 collective-permute-start.5
  46.0 9.8 %collective-permute-start.6 = (bf16[256,640]{1,0:T(8,128)(2,1)S(1)}, bf16[256,640]{1,0:T(8,128)(2,1)S(1)}, u32[]{:S(2)}, u32[]{:S(2)}) collective-permute-start(bf16[256,640]{1,0:T(8,128)(2,1)S(1)} %add_convert_fusion.6), channel_id=1, source_target_pairs={{0,2},{1,3},{2,0},{3,1},{4,6},{5,7},{6,4},{7,5},{8,10},{9,11},{10,... | collective-permute-start | bytes 983048 | tf_op jit(solution)/shard_map/ppermute | solution.py:66
  77.4 9.8 %collective-permute-start.9 = (bf16[256,640]{1,0:T(8,128)(2,1)S(1)}, bf16[256,640]{1,0:T(8,128)(2,1)S(1)}, u32[]{:S(2)}, u32[]{:S(2)}) collective-permute-start(bf16[256,640]{1,0:T(8,128)(2,1)S(1)} %add_convert_fusion.5), channel_id=1, source_target_pairs={{0,2},{1,3},{2,0},{3,1},{4,6},{5,7},{6,4},{7,5},{8,10},{9,11},{10,... | collective-permute-start | bytes 983048 | tf_op jit(solution)/shard_map/ppermute | solution.py:66
  95.5 10.9 %collective-permute-start.12 = (bf16[256,640]{1,0:T(8,128)(2,1)}, bf16[256,640]{1,0:T(8,128)(2,1)}, u32[]{:S(2)}, u32[]{:S(2)}) collective-permute-start(bf16[256,640]{1,0:T(8,128)(2,1)} %add_convert_fusion.4), channel_id=1, source_target_pairs={{0,2},{1,3},{2,0},{3,1},{4,6},{5,7},{6,4},{7,5},{8,10},{9,11},{10,... | collective-permute-start | bytes 983048 | tf_op jit(solution)/shard_map/ppermute | solution.py:66
  97.2 11.8 %collective-permute-start.13 = (bf16[128,640]{1,0:T(8,128)(2,1)}, bf16[128,640]{1,0:T(8,128)(2,1)}, u32[]{:S(2)}, u32[]{:S(2)}) collective-permute-start(bf16[128,640]{1,0:T(8,128)(2,1)} %param.14), channel_id=1, source_target_pairs={{0,2},{1,3},{2,0},{3,1},{4,6},{5,7},{6,4},{7,5},{8,10},{9,11},{10,... | collective-permute-start | bytes 491528 | tf_op jit(solution)/shard_map/ppermute | solution.py:66
  119.1 4.3 %collective-permute-start.15 = (bf16[256,640]{1,0:T(8,128)(2,1)}, bf16[256,640]{1,0:T(8,128)(2,1)}, u32[]{:S(2)}, u32[]{:S(2)}) collective-permute-start(bf16[256,640]{1,0:T(8,128)(2,1)} %slice.428), channel_id=1, source_target_pairs={{0,1},{1,0},{2,3},{3,2},{4,5},{5,4},{6,7},{7,6},{8,9},{9,8},{10,11... | collective-permute-start | bytes 983048 | tf_op jit(solution)/shard_map/ppermute | solution.py:66
  125.1 17.4 %collective-permute-start.16 = (bf16[256,640]{1,0:T(8,128)(2,1)}, bf16[256,640]{1,0:T(8,128)(2,1)}, u32[]{:S(2)}, u32[]{:S(2)}) collective-permute-start(bf16[256,640]{1,0:T(8,128)(2,1)} %add_convert_fusion.3), channel_id=1, source_target_pairs={{0,2},{1,3},{2,0},{3,1},{4,6},{5,7},{6,4},{7,5},{8,10},{9,11},{10,... | collective-permute-start | bytes 983048 | tf_op jit(solution)/shard_map/ppermute | solution.py:66
  148.6 6.3 %collective-permute-start.17 = (bf16[256,640]{1,0:T(8,128)(2,1)}, bf16[256,640]{1,0:T(8,128)(2,1)}, u32[]{:S(2)}, u32[]{:S(2)}) collective-permute-start(bf16[256,640]{1,0:T(8,128)(2,1)} %fusion.37), channel_id=1, source_target_pairs={{0,1},{1,0},{2,3},{3,2},{4,5},{5,4},{6,7},{7,6},{8,9},{9,8},{10,11... | collective-permute-start | bytes 983048 | tf_op jit(solution)/shard_map/ppermute | solution.py:66
  167.5 9.0 %collective-permute-start.18 = (bf16[256,640]{1,0:T(8,128)(2,1)}, bf16[256,640]{1,0:T(8,128)(2,1)}, u32[]{:S(2)}, u32[]{:S(2)}) collective-permute-start(bf16[256,640]{1,0:T(8,128)(2,1)} %slice.432), channel_id=1, source_target_pairs={{0,1},{1,0},{2,3},{3,2},{4,5},{5,4},{6,7},{7,6},{8,9},{9,8},{10,11... | collective-permute-start | bytes 983048 | tf_op jit(solution)/shard_map/ppermute | solution.py:66
  177.6 10.2 %collective-permute-start.19 = (bf16[256,640]{1,0:T(8,128)(2,1)S(1)}, bf16[256,640]{1,0:T(8,128)(2,1)}, u32[]{:S(2)}, u32[]{:S(2)}) collective-permute-start(bf16[256,640]{1,0:T(8,128)(2,1)S(1)} %add_convert_fusion.2), channel_id=1, source_target_pairs={{0,2},{1,3},{2,0},{3,1},{4,6},{5,7},{6,4},{7,5},{8,10},{9,11},{10,... | collective-permute-start | bytes 983048 | tf_op jit(solution)/shard_map/ppermute | solution.py:66
  190.1 2.7 collective-permute-start.20
  199.1 1.8 collective-permute-start.21
  201.0 10.1 %collective-permute-start.22 = (bf16[256,640]{1,0:T(8,128)(2,1)S(1)}, bf16[256,640]{1,0:T(8,128)(2,1)S(1)}, u32[]{:S(2)}, u32[]{:S(2)}) collective-permute-start(bf16[256,640]{1,0:T(8,128)(2,1)S(1)} %add_convert_fusion.1), channel_id=1, source_target_pairs={{0,2},{1,3},{2,0},{3,1},{4,6},{5,7},{6,4},{7,5},{8,10},{9,11},{10,... | collective-permute-start | bytes 983048 | tf_op jit(solution)/shard_map/ppermute | solution.py:66
  213.0 8.6 %collective-permute-start.23 = (bf16[256,640]{1,0:T(8,128)(2,1)}, bf16[256,640]{1,0:T(8,128)(2,1)S(1)}, u32[]{:S(2)}, u32[]{:S(2)}) collective-permute-start(bf16[256,640]{1,0:T(8,128)(2,1)} %fusion.41), channel_id=1, source_target_pairs={{0,1},{1,0},{2,3},{3,2},{4,5},{5,4},{6,7},{7,6},{8,9},{9,8},{10,11... | collective-permute-start | bytes 983048 | tf_op jit(solution)/shard_map/ppermute | solution.py:66
  220.0 32.8 %collective-permute-start.34 = (bf16[4,960,128]{2,1,0:T(8,128)(2,1)}, bf16[4,960,128]{2,1,0:T(8,128)(2,1)}, u32[]{:S(2)}, u32[]{:S(2)}) collective-permute-start(bf16[4,960,128]{2,1,0:T(8,128)(2,1)} %dynamic-slice_bitcast_fusion), channel_id=1, source_target_pairs={{0,4},{4,0},{8,12},{12,8},{16,20},{20,16},{24,28},{28,24},{1,5},{5... | collective-permute-start | bytes 2949128 | tf_op jit(solution)/shard_map/ppermute | solution.py:66
  233.8 25.6 %collective-permute-start.24 = (bf16[256,640]{1,0:T(8,128)(2,1)}, bf16[256,640]{1,0:T(8,128)(2,1)}, u32[]{:S(2)}, u32[]{:S(2)}) collective-permute-start(bf16[256,640]{1,0:T(8,128)(2,1)} %slice.440), channel_id=1, source_target_pairs={{0,1},{1,0},{2,3},{3,2},{4,5},{5,4},{6,7},{7,6},{8,9},{9,8},{10,11... | collective-permute-start | bytes 983048 | tf_op jit(solution)/shard_map/ppermute | solution.py:66
  255.1 20.4 %collective-permute-start.35 = (bf16[2,960,128]{2,1,0:T(8,128)(2,1)}, bf16[2,960,128]{2,1,0:T(8,128)(2,1)}, u32[]{:S(2)}, u32[]{:S(2)}) collective-permute-start(bf16[2,960,128]{2,1,0:T(8,128)(2,1)} %dynamic-slice_bitcast_fusion.2), channel_id=1, source_target_pairs={{0,8},{4,12},{8,0},{12,4},{16,24},{20,28},{24,16},{28,20},{1,9},{5... | collective-permute-start | bytes 1474568 | tf_op jit(solution)/shard_map/ppermute | solution.py:66
  257.7 28.3 %collective-permute-start.26 = (bf16[4,640,128]{2,1,0:T(8,128)(2,1)}, bf16[4,640,128]{2,1,0:T(8,128)(2,1)}, u32[]{:S(2)}, u32[]{:S(2)}) collective-permute-start(bf16[4,640,128]{2,1,0:T(8,128)(2,1)} %dynamic-slice_bitcast_fusion.1), channel_id=1, source_target_pairs={{0,4},{4,0},{8,12},{12,8},{16,20},{20,16},{24,28},{28,24},{1,5},{5... | collective-permute-start | bytes 1966088 | tf_op jit(solution)/shard_map/ppermute | solution.py:66
  260.5 21.6 %collective-permute-start.25 = (bf16[256,640]{1,0:T(8,128)(2,1)S(1)}, bf16[256,640]{1,0:T(8,128)(2,1)S(1)}, u32[]{:S(2)}, u32[]{:S(2)}) collective-permute-start(bf16[256,640]{1,0:T(8,128)(2,1)S(1)} %add_convert_fusion), channel_id=1, source_target_pairs={{0,2},{1,3},{2,0},{3,1},{4,6},{5,7},{6,4},{7,5},{8,10},{9,11},{10,... | collective-permute-start | bytes 983048 | tf_op jit(solution)/shard_map/ppermute | solution.py:66
  276.6 21.6 %collective-permute-start.36 = (bf16[1,960,128]{2,1,0:T(8,128)(2,1)S(1)}, bf16[1,960,128]{2,1,0:T(8,128)(2,1)S(1)}, u32[]{:S(2)}, u32[]{:S(2)}) collective-permute-start(bf16[1,960,128]{2,1,0:T(8,128)(2,1)S(1)} %constant_dynamic-slice_fusion), channel_id=1, source_target_pairs={{0,16},{4,20},{8,24},{12,28},{16,0},{20,4},{24,8},{28,12},{1,17},{... | collective-permute-start | bytes 737288 | tf_op jit(solution)/shard_map/ppermute | solution.py:66
  283.3 4.6 %collective-permute-start.29 = (bf16[4,32,128]{2,1,0:T(8,128)(2,1)S(1)}, bf16[4,32,128]{2,1,0:T(8,128)(2,1)S(1)}, u32[]{:S(2)}, u32[]{:S(2)}) collective-permute-start(bf16[4,32,128]{2,1,0:T(8,128)(2,1)S(1)} %dynamic-slice_bitcast_fusion.4), channel_id=1, source_target_pairs={{0,4},{4,0},{8,12},{12,8},{16,20},{20,16},{24,28},{28,24},{1,5},{5... | collective-permute-start | bytes 98312 | tf_op jit(solution)/shard_map/ppermute | solution.py:66
  288.0 5.4 %collective-permute-start.30 = (bf16[2,32,128]{2,1,0:T(8,128)(2,1)S(1)}, bf16[2,32,128]{2,1,0:T(8,128)(2,1)S(1)}, u32[]{:S(2)}, u32[]{:S(2)}) collective-permute-start(bf16[2,32,128]{2,1,0:T(8,128)(2,1)S(1)} %dynamic-slice_bitcast_fusion.5), channel_id=1, source_target_pairs={{0,8},{4,12},{8,0},{12,4},{16,24},{20,28},{24,16},{28,20},{1,9},{5... | collective-permute-start | bytes 49160 | tf_op jit(solution)/shard_map/ppermute | solution.py:66
  290.7 7.7 %collective-permute-start.27 = (bf16[2,640,128]{2,1,0:T(8,128)(2,1)S(1)}, bf16[2,640,128]{2,1,0:T(8,128)(2,1)S(1)}, u32[]{:S(2)}, u32[]{:S(2)}) collective-permute-start(bf16[2,640,128]{2,1,0:T(8,128)(2,1)S(1)} %dynamic-slice_bitcast_fusion.3), channel_id=1, source_target_pairs={{0,8},{4,12},{8,0},{12,4},{16,24},{20,28},{24,16},{28,20},{1,9},{5... | collective-permute-start | bytes 983048 | tf_op jit(solution)/shard_map/ppermute | solution.py:66
  293.4 4.9 %collective-permute-start.31 = (bf16[1,32,128]{2,1,0:T(8,128)(2,1)S(1)}, bf16[1,32,128]{2,1,0:T(8,128)(2,1)S(1)}, u32[]{:S(2)}, u32[]{:S(2)}) collective-permute-start(bf16[1,32,128]{2,1,0:T(8,128)(2,1)S(1)} %constant_dynamic-slice_fusion.1), channel_id=1, source_target_pairs={{0,16},{4,20},{8,24},{12,28},{16,0},{20,4},{24,8},{28,12},{1,17},{... | collective-permute-start | bytes 24584 | tf_op jit(solution)/shard_map/ppermute | solution.py:66
  298.5 8.0 %collective-permute-start.28 = (bf16[1,640,128]{2,1,0:T(8,128)(2,1)S(1)}, bf16[1,640,128]{2,1,0:T(8,128)(2,1)S(1)}, u32[]{:S(2)}, u32[]{:S(2)}) collective-permute-start(bf16[1,640,128]{2,1,0:T(8,128)(2,1)S(1)} %constant_dynamic-slice_fusion.2), channel_id=1, source_target_pairs={{0,16},{4,20},{8,24},{12,28},{16,0},{20,4},{24,8},{28,12},{1,17},{... | collective-permute-start | bytes 491528 | tf_op jit(solution)/shard_map/ppermute | solution.py:66
  308.8 2.7 collective-permute-start.32
  311.5 6.8 %collective-permute-start.33 = (bf16[672,128]{1,0:T(8,128)(2,1)S(1)}, bf16[672,128]{1,0:T(8,128)(2,1)S(1)}, u32[]{:S(2)}, u32[]{:S(2)}) collective-permute-start(bf16[672,128]{1,0:T(8,128)(2,1)S(1)} %add_convert_fusion.8), channel_id=1, source_target_pairs={{0,2},{1,3},{2,0},{3,1},{4,6},{5,7},{6,4},{7,5},{8,10},{9,11},{10,... | collective-permute-start | bytes 516104 | tf_op jit(solution)/shard_map/ppermute | solution.py:66
  (195 other events, 839.3 us)
Sparse Core Ops, SparseCore 0:
  192.7 95.6 reduce-scatter.1

commit v2 on v1

v2 whole, which is shorter than its diff:
```python
import jax
import jax.numpy as jnp
from jax import lax
from jax.experimental import pallas as pl
from jax.experimental.pallas import tpu as pltpu
from jax.sharding import PartitionSpec as P

WINDOW = 512
SEQ_LEN = 512
LANES = 128

epsilon = 1e-06
score_scale = 0.0625
masked_fill = -1e30
thetas = (10000.0, 1000000.0)
gelu_slope = 0.7978845608028654
gelu_cubic = 0.044715

F32 = jnp.float32
BF16 = jnp.bfloat16


def product(left, right):
    return jnp.dot(left, right, preferred_element_type=F32)


def product_left(left, right):
    return lax.dot_general(left, right, (((0,), (0,)), ((), ())), preferred_element_type=F32)


def product_right(left, right):
    return lax.dot_general(left, right, (((1,), (1,)), ((), ())), preferred_element_type=F32)


def angles(place, width, theta):
    half_width = width // 2
    frequency = theta ** (-(2.0 * jnp.arange(half_width, dtype=F32)) / width)
    phases = place.astype(F32)[:, None] * frequency[None, :]
    return (jnp.cos(phases), jnp.sin(phases))


def swap(array, axis, bit):
    size = lax.axis_size(axis)
    return lax.ppermute(array, axis, [(i, i ^ bit) for i in range(size)])


def relative_order(array, quarter):
    parts = array.reshape((4, -1) + array.shape[1:])
    return jnp.concatenate(
        [lax.dynamic_index_in_dim(parts, quarter ^ bit, 0, False) for bit in (0, 2, 1, 3)]
    )


def two_quarters(array):
    return jnp.concatenate([array, swap(array, "tensor", 2)])


def summed_pair(kept, sent):
    pair = (kept.astype(F32) + swap(sent, "tensor", 1).astype(F32)).astype(BF16)
    return (pair, swap(pair, "tensor", 2))


def kernel_call(body, outs, args, layers=None, flops=0):
    layers = layers or {}

    def spec(place, arg):
        if place in layers:
            rest = arg.shape[1:]
            fixed = (layers[place],) + (0,) * len(rest)
            return pl.BlockSpec((1,) + rest, lambda i, fixed=fixed: fixed)
        if arg.shape == (1,):
            return pl.BlockSpec(memory_space=pltpu.SMEM)
        return pl.BlockSpec(arg.shape, lambda i, n=arg.ndim: (0,) * n)

    moved = sum(a.size * a.dtype.itemsize for a in args)
    return pl.pallas_call(
        body,
        grid=(1,),
        in_specs=[spec(place, arg) for place, arg in enumerate(args)],
        out_specs=[pl.BlockSpec(o.shape, lambda i, n=len(o.shape): (0,) * n) for o in outs],
        out_shape=list(outs),
        compiler_params=pltpu.CompilerParams(vmem_limit_bytes=40 << 20),
        cost_estimate=pl.CostEstimate(flops=flops, transcendentals=0, bytes_accessed=moved),
    )(*args)


def shape(rows, columns, dtype):
    return jax.ShapeDtypeStruct((rows, columns), dtype)


def inverse_rms(vector):
    return lax.rsqrt(jnp.mean(vector * vector, axis=-1, keepdims=True) + epsilon)


def norm_forward(vector, gain_row):
    return vector * inverse_rms(vector) * gain_row


def norm_back(vector, gain_row, grad_out):
    scale = inverse_rms(vector)
    scaled = grad_out * gain_row
    inner = jnp.mean(scaled * vector, axis=-1, keepdims=True)
    grad = scale * scaled - vector * (scale * scale * scale * inner)
    grad_gain = jnp.sum(grad_out * (vector * scale), axis=0, keepdims=True)
    return (grad, grad_gain)


def rotate(vector, cosine, sine):
    half_width = vector.shape[-1] // 2
    first_half = vector[:, :half_width]
    second_half = vector[:, half_width:]
    return jnp.concatenate(
        [first_half * cosine - second_half * sine, second_half * cosine + first_half * sine],
        axis=-1,
    )


def total(pair_ref, other_ref):
    quarter = pair_ref.shape[0] // 2
    other = jnp.concatenate([other_ref[quarter:, :], other_ref[:quarter, :]], axis=0)
    return pair_ref[...].astype(F32) + other.astype(F32)


def first_norm(stream, gains, layer):
    def body(stream_ref, gains_ref, normed_ref):
        normed_ref[...] = norm_forward(
            stream_ref[...].astype(F32), gains_ref[0, 0:1, :]
        ).astype(BF16)

    return kernel_call(body, [shape(*stream.shape, BF16)], (stream, gains), {1: layer})[0]


def after_attention(pair, other, stream, gains, layer):
    def body(pair_ref, other_ref, stream_ref, gains_ref, sum_ref, middle_ref, normed_ref):
        attn_sum = total(pair_ref, other_ref)
        middle = stream_ref[...].astype(F32) + norm_forward(attn_sum, gains_ref[0, 1:2, :])
        sum_ref[...] = attn_sum
        middle_ref[...] = middle
        normed_ref[...] = norm_forward(middle, gains_ref[0, 2:3, :]).astype(BF16)

    size = pair.shape
    return kernel_call(
        body,
        [shape(*size, F32), shape(*size, F32), shape(*size, BF16)],
        (pair, other, stream, gains),
        {3: layer},
    )


def between_layers(pair, other, middle, gains, layer):
    def body(pair_ref, other_ref, middle_ref, gains_ref, next_ref, sum_ref, result_ref, low_ref):
        mlp_sum = total(pair_ref, other_ref)
        result = middle_ref[...] + norm_forward(mlp_sum, gains_ref[0, 3:4, :])
        sum_ref[...] = mlp_sum
        result_ref[...] = result
        low_ref[...] = norm_forward(result, next_ref[0, 0:1, :]).astype(BF16)

    size = pair.shape
    return kernel_call(
        body,
        [shape(*size, F32), shape(*size, F32), shape(*size, BF16)],
        (pair, other, middle, gains, gains),
        {3: layer, 4: layer + 1},
    )


def turn_around(pair, other, middle, cotangent, gains, layer):
    def body(pair_ref, other_ref, middle_ref, grad_ref, gains_ref, out_ref, low_ref, gain_ref):
        mlp_sum = total(pair_ref, other_ref)
        gain_row = gains_ref[0, 3:4, :]
        own = out_ref.shape[0]
        result = middle_ref[:own, :] + norm_forward(mlp_sum[:own, :], gain_row)
        out_ref[...] = result.astype(BF16)
        grad, grad_gain = norm_back(mlp_sum, gain_row, grad_ref[...].astype(F32))
        low_ref[...] = grad.astype(BF16)
        gain_ref[...] = grad_gain

    rows, columns = pair.shape
    return kernel_call(
        body,
        [shape(rows // 2, columns, BF16), shape(rows, columns, BF16), shape(1, columns, F32)],
        (pair, other, middle, cotangent, gains),
        {4: layer},
    )


def back_to_attention(pair, other, middle, attn_sum, grad_stream, gains, layer):
    def body(
        pair_ref, other_ref, middle_ref, attn_ref, grad_ref, gains_ref,
        grad_middle_ref, low_ref, gain1_ref, gain2_ref,
    ):
        grad_normed = total(pair_ref, other_ref)
        step, gain2_ref[...] = norm_back(middle_ref[...], gains_ref[0, 2:3, :], grad_normed)
        grad_middle = grad_ref[...].astype(F32) + step
        grad_middle_ref[...] = grad_middle
        grad_attn, gain1_ref[...] = norm_back(attn_ref[...], gains_ref[0, 1:2, :], grad_middle)
        low_ref[...] = grad_attn.astype(BF16)

    rows, columns = pair.shape
    return kernel_call(
        body,
        [shape(rows, columns, F32), shape(rows, columns, BF16)] + [shape(1, columns, F32)] * 2,
        (pair, other, middle, attn_sum, grad_stream, gains),
        {5: layer},
    )


def back_between(pair, other, stream, grad_middle, mlp_sum, gains, layer):
    def body(
        pair_ref, other_ref, stream_ref, grad_ref, mlp_ref, gains_ref, below_ref,
        grad_stream_ref, low_ref, gain0_ref, gain3_ref,
    ):
        grad_normed = total(pair_ref, other_ref)
        step, gain0_ref[...] = norm_back(stream_ref[...], gains_ref[0, 0:1, :], grad_normed)
        grad_stream = grad_ref[...] + step
        grad_stream_ref[...] = grad_stream
        grad_mlp, gain3_ref[...] = norm_back(mlp_ref[...], below_ref[0, 3:4, :], grad_stream)
        low_ref[...] = grad_mlp.astype(BF16)

    rows, columns = pair.shape
    return kernel_call(
        body,
        [shape(rows, columns, F32), shape(rows, columns, BF16)] + [shape(1, columns, F32)] * 2,
        (pair, other, stream, grad_middle, mlp_sum, gains, gains),
        {5: layer, 6: layer - 1},
    )


def back_to_input(pair, other, stream, grad_middle, gains, layer):
    def body(pair_ref, other_ref, stream_ref, grad_ref, gains_ref, out_ref, gain0_ref):
        grad_normed = total(pair_ref, other_ref)
        step, gain0_ref[...] = norm_back(
            stream_ref[...].astype(F32), gains_ref[0, 0:1, :], grad_normed
        )
        own = out_ref.shape[0]
        out_ref[...] = (grad_ref[:own, :] + step[:own, :]).astype(BF16)

    rows, columns = pair.shape
    return kernel_call(
        body,
        [shape(rows // 2, columns, BF16), shape(1, columns, F32)],
        (pair, other, stream, grad_middle, gains),
        {4: layer},
    )


def allowed_rows(down_ref, across_ref, start, count, window):
    seg_down = down_ref[start : start + count, 0:1]
    place_down = down_ref[start : start + count, 1:2]
    seg_across = across_ref[0:1, :]
    place_across = across_ref[1:2, :]
    allowed = (seg_down == seg_across) & (place_across <= place_down)
    if window < SEQ_LEN:
        allowed = allowed & (place_down - place_across < window)
    return allowed


def attention(own, received, weights, tables, layer, window):
    w_query, w_key, w_value, w_out, qk_gains = weights
    cosine, sine, down, across = tables
    half = own.shape[0]
    length = 2 * half
    head_width = w_key.shape[2]

    def body(
        own_ref, received_ref, wq_ref, wk_ref, wv_ref, wo_ref, gain_ref,
        cos_ref, sin_ref, down_ref, across_ref,
        kept_ref, sent_ref, qraw_ref, kraw_ref, q_ref, k_ref, v_ref, attended_ref, lse_ref,
    ):
        for part, source in ((0, own_ref), (1, received_ref)):
            rows = slice(part * half, (part + 1) * half)
            normed = source[...]
            cos_rows, sin_rows = cos_ref[rows, :], sin_ref[rows, :]
            key_raw = product(normed, wk_ref[0])
            kraw_ref[rows, :] = key_raw
            k_ref[rows, :] = rotate(
                norm_forward(key_raw, gain_ref[0, 1:2, :]), cos_rows, sin_rows
            ).astype(BF16)
            v_ref[rows, :] = product(normed, wv_ref[0]).astype(BF16)
            query_raw = product(normed, wq_ref[0])
            qraw_ref[rows, :] = query_raw
            q_ref[rows, :] = rotate(
                norm_forward(query_raw, gain_ref[0, 0:1, :]), cos_rows, sin_rows
            ).astype(BF16)
        for part, target in ((1, sent_ref), (0, kept_ref)):
            rows = slice(part * half, (part + 1) * half)
            scores = product_right(q_ref[rows, :], k_ref[...]) * score_scale
            allowed = allowed_rows(down_ref, across_ref, part * half, half, window)
            masked = jnp.where(allowed, scores, masked_fill)
            row_max = jnp.max(masked, axis=-1, keepdims=True)
            expo = jnp.where(allowed, jnp.exp(masked - row_max), 0.0)
            row_sum = jnp.sum(expo, axis=-1, keepdims=True)
            probability = (expo * (1.0 / row_sum)).astype(BF16)
            lse_ref[rows, :] = row_max + jnp.log(row_sum)
            attended = product(probability, v_ref[...]).astype(BF16)
            attended_ref[rows, :] = attended
            target[...] = product(attended, wo_ref[0]).astype(BF16)

    width = own.shape[1]
    return kernel_call(
        body,
        [shape(half, width, BF16)] * 2
        + [shape(length, head_width, F32)] * 2
        + [shape(length, head_width, BF16)] * 4
        + [shape(length, 1, F32)],
        (own, received, w_query, w_key, w_value, w_out, qk_gains, cosine, sine, down, across),
        {place: layer for place in (2, 3, 4, 5, 6)},
        flops=1_000_000_000,
    )


def feed_forward(own, received, weights, layer):
    half, width = own.shape
    w_gate, w_up, w_down = weights
    hidden_width = w_gate.shape[2]
    length = 2 * half

    def body(own_ref, received_ref, wg_ref, wu_ref, wd_ref, kept_ref, sent_ref, g_ref, u_ref, h_ref):
        for part, source, target in ((1, received_ref, sent_ref), (0, own_ref, kept_ref)):
            rows = slice(part * half, (part + 1) * half)
            normed = source[...]
            gate = product(normed, wg_ref[0])
            up = product(normed, wu_ref[0])
            g_ref[rows, :] = gate
            u_ref[rows, :] = up
            bend = jnp.tanh(gelu_slope * (gate + gelu_cubic * (gate * gate * gate)))
            hidden = (gate * (0.5 * (1.0 + bend)) * up).astype(BF16)
            h_ref[rows, :] = hidden
            target[...] = product(hidden, wd_ref[0]).astype(BF16)

    return kernel_call(
        body,
        [shape(half, width, BF16)] * 2
        + [shape(length, hidden_width, F32)] * 2
        + [shape(length, hidden_width, BF16)],
        (own, received, w_gate, w_up, w_down),
        {2: layer, 3: layer, 4: layer},
        flops=1_000_000_000,
    )


def feed_forward_back(own, received, weights, gate, up, layer):
    half, width = own.shape
    w_gate, w_up, w_down = weights
    hidden_width = w_gate.shape[2]
    length = 2 * half

    def body(
        own_ref, received_ref, wg_ref, wu_ref, wd_ref, g_ref, u_ref,
        kept_ref, sent_ref, gate_low_ref, up_low_ref,
    ):
        for part, source, target in ((1, received_ref, sent_ref), (0, own_ref, kept_ref)):
            rows = slice(part * half, (part + 1) * half)
            grad_hidden = product_right(source[...], wd_ref[0])
            gate_in = g_ref[rows, :]
            square = gate_in * gate_in
            bend = jnp.tanh(gelu_slope * gate_in * (1.0 + gelu_cubic * square))
            lift = 0.5 * (1.0 + bend)
            slope = lift + 0.5 * gate_in * (1.0 - bend * bend) * (
                gelu_slope * (1.0 + 3.0 * gelu_cubic * square)
            )
            gate_low = (grad_hidden * u_ref[rows, :] * slope).astype(BF16)
            up_low = (grad_hidden * (gate_in * lift)).astype(BF16)
            gate_low_ref[rows, :] = gate_low
            up_low_ref[rows, :] = up_low
            target[...] = (
                product_right(gate_low, wg_ref[0]) + product_right(up_low, wu_ref[0])
            ).astype(BF16)

    return kernel_call(
        body,
        [shape(half, width, BF16)] * 2 + [shape(length, hidden_width, BF16)] * 2,
        (own, received, w_gate, w_up, w_down, gate, up),
        {2: layer, 3: layer, 4: layer},
        flops=1_000_000_000,
    )


def attention_back(own, received, weights, tables, saved, layer, window):
    w_query, w_key, w_value, w_out, qk_gains = weights
    cosine, sine, down, across = tables
    query_raw, key_raw, queries, key_rows, values, row_lse = saved
    half, width = own.shape
    length = 2 * half
    head_width = w_key.shape[2]

    def body(
        own_ref, received_ref, wq_ref, wk_ref, wv_ref, wo_ref, gain_ref,
        cos_ref, sin_ref, down_ref, across_ref,
        qraw_ref, kraw_ref, q_ref, k_ref, v_ref, lse_ref,
        kept_ref, sent_ref, gq_ref, gk_ref, gv_ref, qgain_ref, kgain_ref,
    ):
        grad_keys = None
        grad_values = None
        query_gain = None
        for part, source in ((0, own_ref), (1, received_ref)):
            rows = slice(part * half, (part + 1) * half)
            grad_attended = product_right(source[...], wo_ref[0]).astype(BF16)
            queries_part = q_ref[rows, :]
            scores = product_right(queries_part, k_ref[...]) * score_scale
            allowed = allowed_rows(down_ref, across_ref, part * half, half, window)
            probability = jnp.where(allowed, jnp.exp(scores - lse_ref[rows, :]), 0.0)
            values_term = product_left(probability.astype(BF16), grad_attended)
            grad_prob = product_right(grad_attended, v_ref[...])
            inner_sum = jnp.sum(probability * grad_prob, axis=-1, keepdims=True)
            grad_scores = (probability * (grad_prob - inner_sum)).astype(BF16)
            keys_term = product_left(grad_scores, queries_part)
            grad_values = values_term if grad_values is None else grad_values + values_term
            grad_keys = keys_term if grad_keys is None else grad_keys + keys_term
            grad_queries = (product(grad_scores, k_ref[...]) * score_scale).astype(BF16)
            turned = rotate(grad_queries.astype(F32), cos_ref[rows, :], -sin_ref[rows, :])
            grad_raw, gain_term = norm_back(qraw_ref[rows, :], gain_ref[0, 0:1, :], turned)
            query_gain = gain_term if query_gain is None else query_gain + gain_term
            gq_ref[rows, :] = grad_raw.astype(BF16)
        qgain_ref[...] = query_gain
        grad_keys = (grad_keys * score_scale).astype(BF16)
        turned = rotate(grad_keys.astype(F32), cos_ref[...], -sin_ref[...])
        grad_raw, kgain_ref[...] = norm_back(kraw_ref[...], gain_ref[0, 1:2, :], turned)
        gk_ref[...] = grad_raw.astype(BF16)
        gv_ref[...] = grad_values.astype(BF16)
        for part, target in ((1, sent_ref), (0, kept_ref)):
            rows = slice(part * half, (part + 1) * half)
            target[...] = (
                product_right(gq_ref[rows, :], wq_ref[0])
                + product_right(gk_ref[rows, :], wk_ref[0])
                + product_right(gv_ref[rows, :], wv_ref[0])
            ).astype(BF16)

    return kernel_call(
        body,
        [shape(half, width, BF16)] * 2
        + [shape(length, head_width, BF16)] * 3
        + [shape(1, head_width, F32)] * 2,
        (
            own, received, w_query, w_key, w_value, w_out, qk_gains,
            cosine, sine, down, across, query_raw, key_raw, queries, key_rows, values, row_lse,
        ),
        {place: layer for place in (2, 3, 4, 5, 6)},
        flops=1_500_000_000,
    )


def slot_masks(bits):
    count = len(bits)
    return [
        sum(bit for place, bit in enumerate(bits) if slot >> (count - 1 - place) & 1)
        for slot in range(1 << count)
    ]


def gradient_blocks(factors, me, bits):
    pieces = 1 << len(bits)
    masks = slot_masks(bits)
    sizes = [(l[0].shape[1] // pieces, r[0].shape[1] // LANES) for l, r in factors]
    rows = sum(tall * wide for tall, wide in sizes)
    if any(tall % 16 for tall, wide in sizes):
        chunks = me[0] ^ jnp.array(masks, jnp.int32)
        parts = []
        for (left, right), (tall, wide) in zip(factors, sizes):
            grad = product_left(jnp.concatenate(left), jnp.concatenate(right)).astype(BF16)
            cut = grad.reshape(pieces, tall, wide, LANES).transpose(0, 2, 1, 3)
            parts.append(cut.reshape(pieces, tall * wide, LANES))
        blocks = jnp.take(jnp.concatenate(parts, axis=1), chunks, axis=0)
        return (blocks[: pieces // 2], blocks[pieces // 2 :])
    flat = []
    where = []
    for pair in factors:
        places = []
        for side in pair:
            places.append(list(range(len(flat), len(flat) + len(side))))
            flat.extend(side)
        where.append(places)

    def body(*refs):
        me_ref, inputs, (kept_ref, sent_ref, *scratch) = refs[0], refs[1 : 1 + len(flat)], refs[1 + len(flat) :]
        base = 0
        for (lefts, rights), (tall, wide), held in zip(where, sizes, scratch):
            def side(places):
                arrays = [inputs[place][...] for place in places]
                return arrays[0] if len(arrays) == 1 else jnp.concatenate(arrays, axis=0)

            held[...] = product_left(side(lefts), side(rights))
            for slot, mask in enumerate(masks):
                chunk = jnp.bitwise_xor(me_ref[0], mask)
                start = pl.multiple_of(chunk * tall, tall)
                target = kept_ref if slot < pieces // 2 else sent_ref
                block = held[pl.ds(start, tall), :].astype(BF16)
                for column in range(wide):
                    low = base + column * tall
                    target[slot % (pieces // 2), low : low + tall, :] = block[
                        :, column * LANES : (column + 1) * LANES
                    ]
            base += tall * wide

    out = jax.ShapeDtypeStruct((pieces // 2, rows, LANES), BF16)
    args = (me, *flat)
    specs = [pl.BlockSpec(memory_space=pltpu.SMEM)] + [
        pl.BlockSpec(a.shape, lambda i: (0, 0)) for a in flat
    ]
    return pl.pallas_call(
        body,
        grid=(1,),
        in_specs=specs,
        out_specs=[pl.BlockSpec(out.shape, lambda i: (0, 0, 0))] * 2,
        out_shape=[out, out],
        scratch_shapes=[
            pltpu.VMEM((tall * pieces, wide * LANES), F32) for tall, wide in sizes
        ],
        compiler_params=pltpu.CompilerParams(vmem_limit_bytes=40 << 20),
        cost_estimate=pl.CostEstimate(
            flops=1_000_000_000,
            transcendentals=0,
            bytes_accessed=sum(a.size * a.dtype.itemsize for a in args),
        ),
    )(*args)


def halved(blocks, bits):
    kept, sent = blocks
    for bit in bits[:-1]:
        arrived = swap(sent, "dp", bit)
        middle = kept.shape[0] // 2
        sent = (kept[middle:].astype(F32) + arrived[middle:].astype(F32)).astype(BF16)
        kept = kept[:middle].astype(F32) + arrived[:middle].astype(F32)
    return kept[0].astype(F32) + swap(sent, "dp", bits[-1])[0].astype(F32)


def over_tensor(rows):
    for bit in (1, 2):
        low = rows.astype(BF16)
        rows = low.astype(F32) + swap(low, "tensor", bit).astype(F32)
    return rows


def over_all(rows):
    bit = 1
    while bit < lax.axis_size("dp"):
        low = rows.astype(BF16)
        rows = low.astype(F32) + swap(low, "dp", bit).astype(F32)
        bit *= 2
    return over_tensor(rows)


def assembled(sources, layout, tall_of, columns_of):
    outs = [
        jax.ShapeDtypeStruct((2, tall, columns), F32)
        for tall, columns in zip(tall_of, columns_of)
    ]

    def cut(read, start, tall, columns):
        return [
            read(start + column * tall, tall) for column in range(columns // LANES)
        ]

    if any(tall % 8 for tall in tall_of):
        results = []
        for member, (tall, columns) in enumerate(zip(tall_of, columns_of)):
            both = [
                jnp.concatenate(
                    cut(lambda a, n: sources[source][a : a + n], start, tall, columns), axis=1
                )
                for source, start in layout[member]
            ]
            results.append(jnp.stack(both))
        return results

    def body(*refs):
        inputs, targets = refs[: len(sources)], refs[len(sources) :]
        for member, (tall, columns) in enumerate(zip(tall_of, columns_of)):
            for layer, (source, start) in enumerate(layout[member]):
                for column in range(columns // LANES):
                    low = start + column * tall
                    targets[member][layer, :, column * LANES : (column + 1) * LANES] = inputs[
                        source
                    ][low : low + tall, :]

    return pl.pallas_call(
        body,
        grid=(1,),
        in_specs=[pl.BlockSpec(a.shape, lambda i: (0, 0)) for a in sources],
        out_specs=[pl.BlockSpec(o.shape, lambda i: (0, 0, 0)) for o in outs],
        out_shape=outs,
        compiler_params=pltpu.CompilerParams(vmem_limit_bytes=40 << 20),
    )(*sources)


def local(
    hidden_in,
    cotangent,
    segments,
    positions,
    w_query,
    w_key,
    w_value,
    w_out,
    w_gate,
    w_up,
    w_down,
    norm_gains,
    qk_gains,
):
    head_width = w_key.shape[2]
    windows = (WINDOW, SEQ_LEN)
    pieces = lax.axis_size("dp")
    quarter = lax.axis_index("tensor")
    me = lax.axis_index("dp").astype(jnp.int32).reshape(1)
    bits = [1 << place for place in range(pieces.bit_length() - 1)]
    turned_bits = bits[1::-1] + bits[2:]
    seg_rows = relative_order(segments, quarter)
    pos_rows = relative_order(positions, quarter)
    places = relative_order(jnp.arange(SEQ_LEN, dtype=jnp.int32), quarter)
    down = jnp.stack([seg_rows, places], axis=1)
    across = jnp.stack([seg_rows, places], axis=0)
    attn_weights = (w_query, w_key, w_value, w_out, qk_gains)
    mlp_weights = (w_gate, w_up, w_down)
    tables = [angles(pos_rows, head_width, theta) + (down, across) for theta in thetas]

    stream = two_quarters(hidden_in)
    low = first_norm(stream, norm_gains, 0)
    saved = []
    for layer in range(2):
        received = swap(low, "tensor", 1)
        kept, sent, *kept_attn = attention(
            low, received, attn_weights, tables[layer], layer, windows[layer]
        )
        attn_in = (low, received)
        pair, other = summed_pair(kept, sent)
        attn_sum, middle, low = after_attention(pair, other, stream, norm_gains, layer)
        received = swap(low, "tensor", 1)
        kept, sent, *kept_mlp = feed_forward(low, received, mlp_weights, layer)
        mlp_in = (low, received)
        pair, other = summed_pair(kept, sent)
        saved.append([attn_in, kept_attn, attn_sum, middle, mlp_in, kept_mlp, stream])
        if layer == 0:
            mlp_sum, stream, low = between_layers(pair, other, middle, norm_gains, layer)

    grad_stream = two_quarters(cotangent)
    output, low, gain3 = turn_around(pair, other, middle, grad_stream, norm_gains, 1)
    sums = [None, None]
    gain_rows = [None, None]
    for layer in (1, 0):
        attn_in, kept_attn, attn_sum, middle, mlp_in, kept_mlp, stream = saved[layer]
        gate, up, hidden = kept_mlp
        query_raw, key_raw, queries, key_rows, values, attended, row_lse = kept_attn
        received = swap(low, "tensor", 1)
        kept, sent, gate_low, up_low = feed_forward_back(
            low, received, mlp_weights, gate, up, layer
        )
        mlp_out = (low, received)
        pair, other = summed_pair(kept, sent)
        mlp_order = bits if layer == 1 else turned_bits
        mlp_blocks = gradient_blocks(
            [(mlp_in, (gate_low,)), (mlp_in, (up_low,)), ((hidden,), mlp_out)], me, mlp_order
        )
        grad_middle, low, gain1, gain2 = back_to_attention(
            pair, other, middle, attn_sum, grad_stream, norm_gains, layer
        )
        received = swap(low, "tensor", 1)
        kept, sent, grad_q, grad_k, grad_v, gain_q, gain_k = attention_back(
            low,
            received,
            attn_weights,
            tables[layer],
            (query_raw, key_raw, queries, key_rows, values, row_lse),
            layer,
            windows[layer],
        )
        pair, other = summed_pair(kept, sent)
        attn_order = turned_bits if layer == 1 else bits
        attn_blocks = gradient_blocks(
            [
                (attn_in, (grad_q,)),
                ((attended,), (low, received)),
                (attn_in, (grad_k,)),
                (attn_in, (grad_v,)),
            ],
            me,
            attn_order,
        )
        sums[layer] = (halved(mlp_blocks, mlp_order), halved(attn_blocks, attn_order))
        gain_rows[layer] = [None, gain1, gain2, gain3, gain_q, gain_k]
        if layer == 1:
            grad_stream, low, gain_rows[1][0], gain3 = back_between(
                pair, other, stream, grad_middle, mlp_sum, norm_gains, layer
            )
        else:
            grad_input, gain_rows[0][0] = back_to_input(
                pair, other, stream, grad_middle, norm_gains, layer
            )

    width = norm_gains.shape[2]
    gain_terms = jnp.concatenate(
        [
            jnp.pad(row * 0.5 if place < 4 else row, ((0, 0), (0, width - row.shape[1])))
            for layer in range(2)
            for place, row in enumerate(gain_rows[layer])
        ]
    )
    gains = over_all(gain_terms).reshape(2, 6, width)

    def own_columns(array, columns):
        return lax.dynamic_slice_in_dim(array[:, :, :columns], me[0] * (columns // pieces), columns // pieces, 2)

    grad_norm_gains = own_columns(gains[:, :4], width)
    grad_qk_gains = own_columns(gains[:, 4:], head_width)

    tall = {
        "q": w_query.shape[1] // pieces,
        "o": w_out.shape[1] // pieces,
        "g": w_gate.shape[1] // pieces,
        "d": w_down.shape[1] // pieces,
    }
    heads_rows = tall["q"] * head_width // LANES
    out_rows = tall["o"] * w_out.shape[2] // LANES
    gate_rows = tall["g"] * w_gate.shape[2] // LANES
    shared = [over_tensor(sums[layer][1][heads_rows + out_rows :]) for layer in range(2)]
    sources = [sums[0][0], sums[1][0], sums[0][1], sums[1][1], shared[0], shared[1]]
    layout = [
        [(2, 0), (3, 0)],
        [(4, 0), (5, 0)],
        [(4, heads_rows), (5, heads_rows)],
        [(2, heads_rows), (3, heads_rows)],
        [(0, 0), (1, 0)],
        [(0, gate_rows), (1, gate_rows)],
        [(0, 2 * gate_rows), (1, 2 * gate_rows)],
    ]
    grads = assembled(
        sources,
        layout,
        [tall["q"], tall["q"], tall["q"], tall["o"], tall["g"], tall["g"], tall["d"]],
        [head_width] * 3 + [w_out.shape[2], w_gate.shape[2], w_up.shape[2], w_down.shape[2]],
    )
    return (output, grad_input, *grads, grad_norm_gains, grad_qk_gains)


def solution(mesh):
    return jax.shard_map(
        local,
        mesh=mesh,
        in_specs=(
            P(("dp", "tensor"), None),
            P(("dp", "tensor"), None),
            P("dp"),
            P("dp"),
            P(None, None, "tensor"),
            P(),
            P(),
            P(None, "tensor", None),
            P(None, None, "tensor"),
            P(None, None, "tensor"),
            P(None, "tensor", None),
            P(),
            P(),
        ),
        out_specs=(
            P(("dp", "tensor"), None),
            P(("dp", "tensor"), None),
            P(None, "dp", "tensor"),
            P(None, "dp", None),
            P(None, "dp", None),
            P(None, ("tensor", "dp"), None),
            P(None, "dp", "tensor"),
            P(None, "dp", "tensor"),
            P(None, ("tensor", "dp"), None),
            P(None, None, "dp"),
            P(None, None, "dp"),
        ),
        check_vma=False,
    )
```

time: 333 us -> 262 us (0.79); the launches traced: 329 us -> 261 us
  matrix products: 52.2 us -> 0 us
  other arithmetic: 56 us -> 11 us
  waiting for transfers between devices: 98.5 us -> 134 us
  Pallas kernels: 0 us -> 34.9 us
  local copies, waits for them, and re-layouts: 71.2 us -> 36.4 us
  between operations: 17.2 us -> 2.23 us
  starting transfers between devices: 33.3 us -> 42.9 us
    dot_general x54 -> x0, matrix products: 52.2 us -> none  [the longest x18 24.6 us: product_left(): lax.dot_general(left, right, (((0,), (0,)), ((), ())), preferred_element_...]
    ppermute x37 -> x47, waiting for transfers between devices: 98.5 us -> 134 us  [swap(): return lax.ppermute(array, axis, [(i, i ^ bit) for i in range(size)])]
    pallas_call x0 -> x22, Pallas kernels: none -> 34.9 us  [the longest x17 25.6 us: kernel_call(): pl.pallas_call(body, grid=(1,), in_specs=[spec(place, arg) for place, arg...]
    reshape x27 -> x1, local copies, waits for them, and re-layouts: 23.2 us -> 0.01 us  [local(): gains = over_all(gain_terms).reshape(2, 6, width)]
    another operation x11 -> x14, other arithmetic: 20.4 us -> 1.91 us
    reduce_sum x22 -> x0, other arithmetic: 13.9 us -> none  [the longest x13 10.2 us: rms_scale(): vector * lax.rsqrt(jnp.mean(vector * vector, axis=-1, keepdims=True) + ep...]
    slice x30 -> x2, local copies, waits for them, and re-layouts: 11.7 us -> 0.01 us  [the longest x1 0.01 us: local(): grad_norm_gains = own_columns(gains[:, :4], width)]
    convert_element_type x30 -> x23, other arithmetic: 16.1 us -> 5.94 us  [the longest x8 4.21 us: halved(): (kept[middle:].astype(F32) + arrived[middle:].astype(F32)).astype(BF16)]
  transfers between devices with their start and end apart: 38 -> 47, of which waited for: 26 -> 30; matrix products, arithmetic and copies ran while one was open for 30% -> 6% of each run, Pallas kernels for 0% -> 8%
where the time goes in v2:
time: 262 us; the launch traced here: 261 us
  waiting for transfers between devices  134 us (51%)
  starting transfers between devices  42.9 us (16%)
  local copies, waits for them, and re-layouts  36.4 us (14%)
  Pallas kernels  34.9 us (13%)
  other arithmetic  11 us (4%)
    ppermute x47, waiting for transfers between devices, swap(): return lax.ppermute(array, axis, [(i, i ^ bit) for i in range(size)])  134 us
    ppermute x47, starting transfers between devices, swap(): return lax.ppermute(array, axis, [(i, i ^ bit) for i in range(size)])  42.9 us
    unnamed x258, local copies, waits for them, and re-layouts  32.5 us
    pallas_call x17, Pallas kernels, kernel_call(): pl.pallas_call(body, grid=(1,), in_specs=[spec(place, arg) for place, arg...  25.6 us
    pallas_call x4, Pallas kernels, gradient_blocks(): pl.pallas_call(body, grid=(1,), in_specs=specs, out_specs=[pl.BlockSpec(o...  8.02 us
  transfers between devices with their start and end apart: 47, of which 30 were waited for; matrix products, arithmetic and copies ran while one was open for 6% of the time, Pallas kernels for 8%

profile of v2, /device:TPU:0, one launch (start us, length us, event | category | flops | bytes accessed | tf_op | source)
XLA Modules:
  0.0 260.9 jit_solution(7424818650634173985)
XLA Ops:
  0.6 3.0 %collective-permute-start = (bf16[128,640]{1,0:T(8,128)(2,1)}, bf16[128,640]{1,0:T(8,128)(2,1)S(1)}, u32[]{:S(2)}, u32[]{:S(2)}) collective-permute-start(bf16[128,640]{1,0:T(8,128)(2,1)} %param.13), channel_id=1, source_target_pairs={{0,2},{1,3},{2,0},{3,1},{4,6},{5,7},{6,4},{7,5},{8,10},{9,11},{10,... | collective-permute-start | bytes 491528 | tf_op jit(solution)/shard_map/ppermute | solution.py:44
  9.1 1.9 multiply_sine_fusion
  11.1 2.5 shard_map.213
  17.0 1.8 collective-permute-start.3
  18.8 8.2 %collective-permute-done.3.other_ref = bf16[256,640]{1,0:T(8,128)(2,1)S(1)} collective-permute-done((bf16[256,640]{1,0:T(8,128)(2,1)S(1)}, bf16[256,640]{1,0:T(8,128)(2,1)S(1)}, u32[]{:S(2)}, u32[]{:S(2)}) %collective-permute-start.3) | collective-permute-done | bytes 327712 | tf_op jit(solution)/shard_map/ppermute | solution.py:44
  36.1 8.0 %collective-permute-done.6.other_ref = bf16[256,640]{1,0:T(8,128)(2,1)S(1)} collective-permute-done((bf16[256,640]{1,0:T(8,128)(2,1)S(1)}, bf16[256,640]{1,0:T(8,128)(2,1)S(1)}, u32[]{:S(2)}, u32[]{:S(2)}) %collective-permute-start.6) | collective-permute-done | bytes 327712 | tf_op jit(solution)/shard_map/ppermute | solution.py:44
  46.2 2.5 shard_map.217
  53.7 8.0 %collective-permute-done.9.other_ref = bf16[256,640]{1,0:T(8,128)(2,1)S(1)} collective-permute-done((bf16[256,640]{1,0:T(8,128)(2,1)S(1)}, bf16[256,640]{1,0:T(8,128)(2,1)S(1)}, u32[]{:S(2)}, u32[]{:S(2)}) %collective-permute-start.9) | collective-permute-done | bytes 327712 | tf_op jit(solution)/shard_map/ppermute | solution.py:44
  69.4 11.2 %collective-permute-done.13 = bf16[128,640]{1,0:T(8,128)(2,1)S(1)} collective-permute-done((bf16[128,640]{1,0:T(8,128)(2,1)S(1)}, bf16[128,640]{1,0:T(8,128)(2,1)S(1)}, u32[]{:S(2)}, u32[]{:S(2)}) %collective-permute-start.13) | collective-permute-done | bytes 163872 | tf_op jit(solution)/shard_map/ppermute | solution.py:44
  84.0 1.9 shard_map.221
  95.5 2.4 shard_map.230
  102.3 8.2 %collective-permute-done.16.other_ref = bf16[256,640]{1,0:T(8,128)(2,1)S(1)} collective-permute-done((bf16[256,640]{1,0:T(8,128)(2,1)S(1)}, bf16[256,640]{1,0:T(8,128)(2,1)S(1)}, u32[]{:S(2)}, u32[]{:S(2)}) %collective-permute-start.16) | collective-permute-done | bytes 327712 | tf_op jit(solution)/shard_map/ppermute | solution.py:44
  125.9 4.3 %shard_map.223 = (bf16[256,640]{1,0:T(8,128)(2,1)S(1)}, bf16[256,640]{1,0:T(8,128)(2,1)S(1)}, bf16[512,256]{1,0:T(8,128)(2,1)S(1)}, bf16[512,256]{1,0:T(8,128)(2...) custom-call(bf16[256,640]{1,0:T(8,128)(2,1)} %get-tuple-element.123.own_ref.refs_5_, ...), custom_call_target="tpu_custom_call" | custom-call | flops 1500000000 | bytes 5650432 | tf_op jit(solution)/shard_map/pallas_call | solution.py:76
  133.6 2.2 shard_map.232
  139.2 6.7 %collective-permute-done.19.other_ref = bf16[256,640]{1,0:T(8,128)(2,1)S(1)} collective-permute-done((bf16[256,640]{1,0:T(8,128)(2,1)S(1)}, bf16[256,640]{1,0:T(8,128)(2,1)S(1)}, u32[]{:S(2)}, u32[]{:S(2)}) %collective-permute-start.19) | collective-permute-done | bytes 327712 | tf_op jit(solution)/shard_map/ppermute | solution.py:44
  146.9 2.7 %collective-permute-start.31 = (bf16[1,960,128]{2,1,0:T(8,128)(2,1)S(1)}, bf16[1,960,128]{2,1,0:T(8,128)(2,1)S(1)}, u32[]{:S(2)}, u32[]{:S(2)}) collective-permute-start(bf16[1,960,128]{2,1,0:T(8,128)(2,1)S(1)} %fusion), channel_id=1, source_target_pairs={{0,16},{4,20},{8,24},{12,28},{16,0},{20,4},{24,8},{28,12},{1,17},{... | collective-permute-start | bytes 737288 | tf_op jit(solution)/shard_map/ppermute | solution.py:44
  149.5 15.3 %collective-permute-done.35 = bf16[4,640,128]{2,1,0:T(8,128)(2,1)S(1)} collective-permute-done((bf16[4,640,128]{2,1,0:T(8,128)(2,1)S(1)}, bf16[4,640,128]{2,1,0:T(8,128)(2,1)S(1)}, u32[]{:S(2)}, u32[]{:S(2)}) %collective-permute-start.35) | collective-permute-done | bytes 655392 | tf_op jit(solution)/shard_map/ppermute | solution.py:44
  165.7 1.9 shard_map.225
  171.2 3.0 %collective-permute-done.36 = bf16[2,640,128]{2,1,0:T(8,128)(2,1)S(1)} collective-permute-done((bf16[2,640,128]{2,1,0:T(8,128)(2,1)S(1)}, bf16[2,640,128]{2,1,0:T(8,128)(2,1)S(1)}, u32[]{:S(2)}, u32[]{:S(2)}) %collective-permute-start.36) | collective-permute-done | bytes 327712 | tf_op jit(solution)/shard_map/ppermute | solution.py:44
  174.2 2.0 collective-permute-start.37
  176.3 2.9 %collective-permute-done.22.other_ref = bf16[256,640]{1,0:T(8,128)(2,1)S(1)} collective-permute-done((bf16[256,640]{1,0:T(8,128)(2,1)S(1)}, bf16[256,640]{1,0:T(8,128)(2,1)S(1)}, u32[]{:S(2)}, u32[]{:S(2)}) %collective-permute-start.22) | collective-permute-done | bytes 327712 | tf_op jit(solution)/shard_map/ppermute | solution.py:44
  180.1 3.6 %collective-permute-done.37 = bf16[1,640,128]{2,1,0:T(8,128)(2,1)S(1)} collective-permute-done((bf16[1,640,128]{2,1,0:T(8,128)(2,1)S(1)}, bf16[1,640,128]{2,1,0:T(8,128)(2,1)S(1)}, u32[]{:S(2)}, u32[]{:S(2)}) %collective-permute-start.37) | collective-permute-done | bytes 163872 | tf_op jit(solution)/shard_map/ppermute | solution.py:44
  184.0 3.0 %shard_map.227 = (bf16[256,640]{1,0:T(8,128)(2,1)S(1)}, bf16[256,640]{1,0:T(8,128)(2,1)S(1)}, bf16[512,256]{1,0:T(8,128)(2,1)S(1)}, bf16[512,256]{1,0:T(8,128)(2...) custom-call(bf16[256,640]{1,0:T(8,128)(2,1)S(1)} %get-tuple-element.141.own_ref.refs_5_, ...), custom_call_target="tpu_custom_call" | custom-call | flops 1500000000 | bytes 5650432 | tf_op jit(solution)/shard_map/pallas_call | solution.py:76
  189.2 2.4 shard_map.229
  194.0 7.4 %collective-permute-done.25.other_ref = bf16[256,640]{1,0:T(8,128)(2,1)S(1)} collective-permute-done((bf16[256,640]{1,0:T(8,128)(2,1)S(1)}, bf16[256,640]{1,0:T(8,128)(2,1)S(1)}, u32[]{:S(2)}, u32[]{:S(2)}) %collective-permute-start.25) | collective-permute-done | bytes 327712 | tf_op jit(solution)/shard_map/ppermute | solution.py:44
  211.3 4.4 %collective-permute-done.26 = bf16[4,960,128]{2,1,0:T(8,128)(2,1)} collective-permute-done((bf16[4,960,128]{2,1,0:T(8,128)(2,1)}, bf16[4,960,128]{2,1,0:T(8,128)(2,1)}, u32[]{:S(2)}, u32[]{:S(2)}) %collective-permute-start.26) | collective-permute-done | bytes 983072 | tf_op jit(solution)/shard_map/ppermute | solution.py:44
  219.5 6.4 %collective-permute-done.32 = bf16[4,640,128]{2,1,0:T(8,128)(2,1)S(1)} collective-permute-done((bf16[4,640,128]{2,1,0:T(8,128)(2,1)S(1)}, bf16[4,640,128]{2,1,0:T(8,128)(2,1)S(1)}, u32[]{:S(2)}, u32[]{:S(2)}) %collective-permute-start.32) | collective-permute-done | bytes 655392 | tf_op jit(solution)/shard_map/ppermute | solution.py:44
  228.0 5.7 %collective-permute-done.27 = bf16[2,960,128]{2,1,0:T(8,128)(2,1)S(1)} collective-permute-done((bf16[2,960,128]{2,1,0:T(8,128)(2,1)S(1)}, bf16[2,960,128]{2,1,0:T(8,128)(2,1)S(1)}, u32[]{:S(2)}, u32[]{:S(2)}) %collective-permute-start.27) | collective-permute-done | bytes 491552 | tf_op jit(solution)/shard_map/ppermute | solution.py:44
  234.6 3.0 %collective-permute-start.28 = (bf16[1,960,128]{2,1,0:T(8,128)(2,1)}, bf16[1,960,128]{2,1,0:T(8,128)(2,1)}, u32[]{:S(2)}, u32[]{:S(2)}) collective-permute-start(bf16[1,960,128]{2,1,0:T(8,128)(2,1)} %fusion.3), channel_id=1, source_target_pairs={{0,16},{4,20},{8,24},{12,28},{16,0},{20,4},{24,8},{28,12},{1,17},{... | collective-permute-start | bytes 737288 | tf_op jit(solution)/shard_map/ppermute | solution.py:44
  238.3 3.1 %collective-permute-done.46 = bf16[12,640]{1,0:T(8,128)(2,1)S(1)} collective-permute-done((bf16[12,640]{1,0:T(8,128)(2,1)S(1)}, bf16[12,640]{1,0:T(8,128)(2,1)S(1)}, u32[]{:S(2)}, u32[]{:S(2)}) %collective-permute-start.46) | collective-permute-done | bytes 15392 | tf_op jit(solution)/shard_map/ppermute | solution.py:44
  242.1 11.5 %collective-permute-done.34 = bf16[1,640,128]{2,1,0:T(8,128)(2,1)S(1)} collective-permute-done((bf16[1,640,128]{2,1,0:T(8,128)(2,1)S(1)}, bf16[1,640,128]{2,1,0:T(8,128)(2,1)S(1)}, u32[]{:S(2)}, u32[]{:S(2)}) %collective-permute-start.34) | collective-permute-done | bytes 163872 | tf_op jit(solution)/shard_map/ppermute | solution.py:44
  256.8 2.9 %collective-permute-done.39 = bf16[320,128]{1,0:T(8,128)(2,1)S(1)} collective-permute-done((bf16[320,128]{1,0:T(8,128)(2,1)S(1)}, bf16[320,128]{1,0:T(8,128)(2,1)S(1)}, u32[]{:S(2)}, u32[]{:S(2)}) %collective-permute-start.39) | collective-permute-done | bytes 81952 | tf_op jit(solution)/shard_map/ppermute | solution.py:44
  (408 shorter events, 104.7 us)
Async XLA Ops:
  0.6 7.4 %collective-permute-start = (bf16[128,640]{1,0:T(8,128)(2,1)}, bf16[128,640]{1,0:T(8,128)(2,1)S(1)}, u32[]{:S(2)}, u32[]{:S(2)}) collective-permute-start(bf16[128,640]{1,0:T(8,128)(2,1)} %param.13), channel_id=1, source_target_pairs={{0,2},{1,3},{2,0},{3,1},{4,6},{5,7},{6,4},{7,5},{8,10},{9,11},{10,... | collective-permute-start | bytes 491528 | tf_op jit(solution)/shard_map/ppermute | solution.py:44
  17.0 10.1 %collective-permute-start.3 = (bf16[256,640]{1,0:T(8,128)(2,1)S(1)}, bf16[256,640]{1,0:T(8,128)(2,1)S(1)}, u32[]{:S(2)}, u32[]{:S(2)}) collective-permute-start(bf16[256,640]{1,0:T(8,128)(2,1)S(1)} %add_convert_fusion.11.pair_ref), channel_id=1, source_target_pairs={{0,2},{1,3},{2,0},{3,1},{4,6},{5,7},{6,4},{7,5},{8,10},{9,11},{10,... | collective-permute-start | bytes 983048 | tf_op jit(solution)/shard_map/ppermute | solution.py:44
  34.3 9.8 %collective-permute-start.6 = (bf16[256,640]{1,0:T(8,128)(2,1)S(1)}, bf16[256,640]{1,0:T(8,128)(2,1)S(1)}, u32[]{:S(2)}, u32[]{:S(2)}) collective-permute-start(bf16[256,640]{1,0:T(8,128)(2,1)S(1)} %add_convert_fusion.10.pair_ref), channel_id=1, source_target_pairs={{0,2},{1,3},{2,0},{3,1},{4,6},{5,7},{6,4},{7,5},{8,10},{9,11},{10,... | collective-permute-start | bytes 983048 | tf_op jit(solution)/shard_map/ppermute | solution.py:44
  51.9 9.8 %collective-permute-start.9 = (bf16[256,640]{1,0:T(8,128)(2,1)S(1)}, bf16[256,640]{1,0:T(8,128)(2,1)S(1)}, u32[]{:S(2)}, u32[]{:S(2)}) collective-permute-start(bf16[256,640]{1,0:T(8,128)(2,1)S(1)} %add_convert_fusion.9.pair_ref), channel_id=1, source_target_pairs={{0,2},{1,3},{2,0},{3,1},{4,6},{5,7},{6,4},{7,5},{8,10},{9,11},{10,... | collective-permute-start | bytes 983048 | tf_op jit(solution)/shard_map/ppermute | solution.py:44
  67.2 13.4 %collective-permute-start.12 = (bf16[256,640]{1,0:T(8,128)(2,1)S(1)}, bf16[256,640]{1,0:T(8,128)(2,1)S(1)}, u32[]{:S(2)}, u32[]{:S(2)}) collective-permute-start(bf16[256,640]{1,0:T(8,128)(2,1)S(1)} %add_convert_fusion.8.pair_ref), channel_id=1, source_target_pairs={{0,2},{1,3},{2,0},{3,1},{4,6},{5,7},{6,4},{7,5},{8,10},{9,11},{10,... | collective-permute-start | bytes 983048 | tf_op jit(solution)/shard_map/ppermute | solution.py:44
  69.0 11.5 %collective-permute-start.13 = (bf16[128,640]{1,0:T(8,128)(2,1)S(1)}, bf16[128,640]{1,0:T(8,128)(2,1)S(1)}, u32[]{:S(2)}, u32[]{:S(2)}) collective-permute-start(bf16[128,640]{1,0:T(8,128)(2,1)S(1)} %copy-done.124), channel_id=1, source_target_pairs={{0,2},{1,3},{2,0},{3,1},{4,6},{5,7},{6,4},{7,5},{8,10},{9,11},{10,... | collective-permute-start | bytes 491528 | tf_op jit(solution)/shard_map/ppermute | solution.py:44
  88.3 11.3 %collective-permute-start.15 = (bf16[256,640]{1,0:T(8,128)(2,1)}, bf16[256,640]{1,0:T(8,128)(2,1)}, u32[]{:S(2)}, u32[]{:S(2)}) collective-permute-start(bf16[256,640]{1,0:T(8,128)(2,1)} %get-tuple-element.121), channel_id=1, source_target_pairs={{0,1},{1,0},{2,3},{3,2},{4,5},{5,4},{6,7},{7,6},{8,9},{9,8},{10,11... | collective-permute-start | bytes 983048 | tf_op jit(solution)/shard_map/ppermute | solution.py:44
  97.9 32.5 %collective-permute-start.29 = (bf16[4,960,128]{2,1,0:T(8,128)(2,1)}, bf16[4,960,128]{2,1,0:T(8,128)(2,1)}, u32[]{:S(2)}, u32[]{:S(2)}) collective-permute-start(bf16[4,960,128]{2,1,0:T(8,128)(2,1)} %get-tuple-element.161), channel_id=1, source_target_pairs={{0,4},{4,0},{8,12},{12,8},{16,20},{20,16},{24,28},{28,24},{1,5},{5... | collective-permute-start | bytes 2949128 | tf_op jit(solution)/shard_map/ppermute | solution.py:44
  100.7 9.8 %collective-permute-start.16 = (bf16[256,640]{1,0:T(8,128)(2,1)S(1)}, bf16[256,640]{1,0:T(8,128)(2,1)S(1)}, u32[]{:S(2)}, u32[]{:S(2)}) collective-permute-start(bf16[256,640]{1,0:T(8,128)(2,1)S(1)} %add_convert_fusion.7.pair_ref), channel_id=1, source_target_pairs={{0,2},{1,3},{2,0},{3,1},{4,6},{5,7},{6,4},{7,5},{8,10},{9,11},{10,... | collective-permute-start | bytes 983048 | tf_op jit(solution)/shard_map/ppermute | solution.py:44
  130.2 6.1 %collective-permute-start.18 = (bf16[256,640]{1,0:T(8,128)(2,1)S(1)}, bf16[256,640]{1,0:T(8,128)(2,1)S(1)}, u32[]{:S(2)}, u32[]{:S(2)}) collective-permute-start(bf16[256,640]{1,0:T(8,128)(2,1)S(1)} %get-tuple-element.131), channel_id=1, source_target_pairs={{0,1},{1,0},{2,3},{3,2},{4,5},{5,4},{6,7},{7,6},{8,9},{9,8},{10,11... | collective-permute-start | bytes 983048 | tf_op jit(solution)/shard_map/ppermute | solution.py:44
  131.9 14.9 %collective-permute-start.30 = (bf16[2,960,128]{2,1,0:T(8,128)(2,1)S(1)}, bf16[2,960,128]{2,1,0:T(8,128)(2,1)S(1)}, u32[]{:S(2)}, u32[]{:S(2)}) collective-permute-start(bf16[2,960,128]{2,1,0:T(8,128)(2,1)S(1)} %get-tuple-element.193), channel_id=1, source_target_pairs={{0,8},{4,12},{8,0},{12,4},{16,24},{20,28},{24,16},{28,20},{1,9},{5... | collective-permute-start | bytes 1474568 | tf_op jit(solution)/shard_map/ppermute | solution.py:44
  135.8 29.0 %collective-permute-start.35 = (bf16[4,640,128]{2,1,0:T(8,128)(2,1)S(1)}, bf16[4,640,128]{2,1,0:T(8,128)(2,1)S(1)}, u32[]{:S(2)}, u32[]{:S(2)}) collective-permute-start(bf16[4,640,128]{2,1,0:T(8,128)(2,1)S(1)} %get-tuple-element.173), channel_id=1, source_target_pairs={{0,8},{4,12},{8,0},{12,4},{16,24},{20,28},{24,16},{28,20},{1,9},{5... | collective-permute-start | bytes 1966088 | tf_op jit(solution)/shard_map/ppermute | solution.py:44
  136.4 9.5 %collective-permute-start.19 = (bf16[256,640]{1,0:T(8,128)(2,1)S(1)}, bf16[256,640]{1,0:T(8,128)(2,1)S(1)}, u32[]{:S(2)}, u32[]{:S(2)}) collective-permute-start(bf16[256,640]{1,0:T(8,128)(2,1)S(1)} %add_convert_fusion.6.pair_ref), channel_id=1, source_target_pairs={{0,2},{1,3},{2,0},{3,1},{4,6},{5,7},{6,4},{7,5},{8,10},{9,11},{10,... | collective-permute-start | bytes 983048 | tf_op jit(solution)/shard_map/ppermute | solution.py:44
  146.7 19.0 %collective-permute-start.20 = (bf16[256,640]{1,0:T(8,128)(2,1)S(1)}, bf16[256,640]{1,0:T(8,128)(2,1)S(1)}, u32[]{:S(2)}, u32[]{:S(2)}) collective-permute-start(bf16[256,640]{1,0:T(8,128)(2,1)S(1)} %get-tuple-element.134.own_ref.refs_8_), channel_id=1, source_target_pairs={{0,1},{1,0},{2,3},{3,2},{4,5},{5,4},{6,7},{7,6},{8,9},{9,8},{10,11... | collective-permute-start | bytes 983048 | tf_op jit(solution)/shard_map/ppermute | solution.py:44
  146.9 29.3 %collective-permute-start.31 = (bf16[1,960,128]{2,1,0:T(8,128)(2,1)S(1)}, bf16[1,960,128]{2,1,0:T(8,128)(2,1)S(1)}, u32[]{:S(2)}, u32[]{:S(2)}) collective-permute-start(bf16[1,960,128]{2,1,0:T(8,128)(2,1)S(1)} %fusion), channel_id=1, source_target_pairs={{0,16},{4,20},{8,24},{12,28},{16,0},{20,4},{24,8},{28,12},{1,17},{... | collective-permute-start | bytes 737288 | tf_op jit(solution)/shard_map/ppermute | solution.py:44
  164.9 9.2 %collective-permute-start.36 = (bf16[2,640,128]{2,1,0:T(8,128)(2,1)S(1)}, bf16[2,640,128]{2,1,0:T(8,128)(2,1)S(1)}, u32[]{:S(2)}, u32[]{:S(2)}) collective-permute-start(bf16[2,640,128]{2,1,0:T(8,128)(2,1)S(1)} %get-tuple-element.197), channel_id=1, source_target_pairs={{0,4},{4,0},{8,12},{12,8},{16,20},{20,16},{24,28},{28,24},{1,5},{5... | collective-permute-start | bytes 983048 | tf_op jit(solution)/shard_map/ppermute | solution.py:44
  169.4 9.8 %collective-permute-start.22 = (bf16[256,640]{1,0:T(8,128)(2,1)S(1)}, bf16[256,640]{1,0:T(8,128)(2,1)S(1)}, u32[]{:S(2)}, u32[]{:S(2)}) collective-permute-start(bf16[256,640]{1,0:T(8,128)(2,1)S(1)} %add_convert_fusion.5.pair_ref), channel_id=1, source_target_pairs={{0,2},{1,3},{2,0},{3,1},{4,6},{5,7},{6,4},{7,5},{8,10},{9,11},{10,... | collective-permute-start | bytes 983048 | tf_op jit(solution)/shard_map/ppermute | solution.py:44
  174.2 9.5 %collective-permute-start.37 = (bf16[1,640,128]{2,1,0:T(8,128)(2,1)S(1)}, bf16[1,640,128]{2,1,0:T(8,128)(2,1)S(1)}, u32[]{:S(2)}, u32[]{:S(2)}) collective-permute-start(bf16[1,640,128]{2,1,0:T(8,128)(2,1)S(1)} %fusion.6), channel_id=1, source_target_pairs={{0,16},{4,20},{8,24},{12,28},{16,0},{20,4},{24,8},{28,12},{1,17},{... | collective-permute-start | bytes 491528 | tf_op jit(solution)/shard_map/ppermute | solution.py:44
  187.1 5.1 %collective-permute-start.24 = (bf16[256,640]{1,0:T(8,128)(2,1)S(1)}, bf16[256,640]{1,0:T(8,128)(2,1)S(1)}, u32[]{:S(2)}, u32[]{:S(2)}) collective-permute-start(bf16[256,640]{1,0:T(8,128)(2,1)S(1)} %get-tuple-element.149), channel_id=1, source_target_pairs={{0,1},{1,0},{2,3},{3,2},{4,5},{5,4},{6,7},{7,6},{8,9},{9,8},{10,11... | collective-permute-start | bytes 983048 | tf_op jit(solution)/shard_map/ppermute | solution.py:44
  187.6 4.5 %collective-permute-start.41 = (bf16[320,128]{1,0:T(8,128)(2,1)S(1)}, bf16[320,128]{1,0:T(8,128)(2,1)S(1)}, u32[]{:S(2)}, u32[]{:S(2)}) collective-permute-start(bf16[320,128]{1,0:T(8,128)(2,1)S(1)} %add_convert_fusion.12), channel_id=1, source_target_pairs={{0,2},{1,3},{2,0},{3,1},{4,6},{5,7},{6,4},{7,5},{8,10},{9,11},{10,... | collective-permute-start | bytes 245768 | tf_op jit(solution)/shard_map/ppermute | solution.py:44
  191.6 24.0 %collective-permute-start.26 = (bf16[4,960,128]{2,1,0:T(8,128)(2,1)}, bf16[4,960,128]{2,1,0:T(8,128)(2,1)}, u32[]{:S(2)}, u32[]{:S(2)}) collective-permute-start(bf16[4,960,128]{2,1,0:T(8,128)(2,1)} %get-tuple-element.156), channel_id=1, source_target_pairs={{0,8},{4,12},{8,0},{12,4},{16,24},{20,28},{24,16},{28,20},{1,9},{5... | collective-permute-start | bytes 2949128 | tf_op jit(solution)/shard_map/ppermute | solution.py:44
  192.3 9.0 %collective-permute-start.25 = (bf16[256,640]{1,0:T(8,128)(2,1)S(1)}, bf16[256,640]{1,0:T(8,128)(2,1)S(1)}, u32[]{:S(2)}, u32[]{:S(2)}) collective-permute-start(bf16[256,640]{1,0:T(8,128)(2,1)S(1)} %add_convert_fusion.4.pair_ref), channel_id=1, source_target_pairs={{0,2},{1,3},{2,0},{3,1},{4,6},{5,7},{6,4},{7,5},{8,10},{9,11},{10,... | collective-permute-start | bytes 983048 | tf_op jit(solution)/shard_map/ppermute | solution.py:44
  202.5 7.0 %collective-permute-start.42 = (bf16[12,640]{1,0:T(8,128)(2,1)S(1)}, bf16[12,640]{1,0:T(8,128)(2,1)S(1)}, u32[]{:S(2)}, u32[]{:S(2)}) collective-permute-start(bf16[12,640]{1,0:T(8,128)(2,1)S(1)} %concatenate.40), channel_id=1, source_target_pairs={{0,4},{4,0},{8,12},{12,8},{16,20},{20,16},{24,28},{28,24},{1,5},{5... | collective-permute-start | bytes 46088 | tf_op jit(solution)/shard_map/ppermute | solution.py:44
  208.2 17.7 %collective-permute-start.32 = (bf16[4,640,128]{2,1,0:T(8,128)(2,1)S(1)}, bf16[4,640,128]{2,1,0:T(8,128)(2,1)S(1)}, u32[]{:S(2)}, u32[]{:S(2)}) collective-permute-start(bf16[4,640,128]{2,1,0:T(8,128)(2,1)S(1)} %get-tuple-element.167), channel_id=1, source_target_pairs={{0,4},{4,0},{8,12},{12,8},{16,20},{20,16},{24,28},{28,24},{1,5},{5... | collective-permute-start | bytes 1966088 | tf_op jit(solution)/shard_map/ppermute | solution.py:44
  209.5 8.6 %collective-permute-start.43 = (bf16[12,640]{1,0:T(8,128)(2,1)S(1)}, bf16[12,640]{1,0:T(8,128)(2,1)S(1)}, u32[]{:S(2)}, u32[]{:S(2)}) collective-permute-start(bf16[12,640]{1,0:T(8,128)(2,1)S(1)} %add_convert_fusion.17), channel_id=1, source_target_pairs={{0,8},{4,12},{8,0},{12,4},{16,24},{20,28},{24,16},{28,20},{1,9},{5... | collective-permute-start | bytes 46088 | tf_op jit(solution)/shard_map/ppermute | solution.py:44
  217.2 16.5 %collective-permute-start.27 = (bf16[2,960,128]{2,1,0:T(8,128)(2,1)S(1)}, bf16[2,960,128]{2,1,0:T(8,128)(2,1)S(1)}, u32[]{:S(2)}, u32[]{:S(2)}) collective-permute-start(bf16[2,960,128]{2,1,0:T(8,128)(2,1)S(1)} %get-tuple-element.195), channel_id=1, source_target_pairs={{0,4},{4,0},{8,12},{12,8},{16,20},{20,16},{24,28},{28,24},{1,5},{5... | collective-permute-start | bytes 1474568 | tf_op jit(solution)/shard_map/ppermute | solution.py:44
  218.1 9.8 %collective-permute-start.44 = (bf16[12,640]{1,0:T(8,128)(2,1)S(1)}, bf16[12,640]{1,0:T(8,128)(2,1)S(1)}, u32[]{:S(2)}, u32[]{:S(2)}) collective-permute-start(bf16[12,640]{1,0:T(8,128)(2,1)S(1)} %add_convert_fusion.16), channel_id=1, source_target_pairs={{0,16},{4,20},{8,24},{12,28},{16,0},{20,4},{24,8},{28,12},{1,17},{... | collective-permute-start | bytes 46088 | tf_op jit(solution)/shard_map/ppermute | solution.py:44
  226.1 12.1 %collective-permute-start.33 = (bf16[2,640,128]{2,1,0:T(8,128)(2,1)S(1)}, bf16[2,640,128]{2,1,0:T(8,128)(2,1)S(1)}, u32[]{:S(2)}, u32[]{:S(2)}) collective-permute-start(bf16[2,640,128]{2,1,0:T(8,128)(2,1)S(1)} %get-tuple-element.199), channel_id=1, source_target_pairs={{0,8},{4,12},{8,0},{12,4},{16,24},{20,28},{24,16},{28,20},{1,9},{5... | collective-permute-start | bytes 983048 | tf_op jit(solution)/shard_map/ppermute | solution.py:44
  227.9 9.7 %collective-permute-start.45 = (bf16[12,640]{1,0:T(8,128)(2,1)S(1)}, bf16[12,640]{1,0:T(8,128)(2,1)S(1)}, u32[]{:S(2)}, u32[]{:S(2)}) collective-permute-start(bf16[12,640]{1,0:T(8,128)(2,1)S(1)} %add_convert_fusion.15), channel_id=1, source_target_pairs={{0,1},{1,0},{2,3},{3,2},{4,5},{5,4},{6,7},{7,6},{8,9},{9,8},{10,11... | collective-permute-start | bytes 46088 | tf_op jit(solution)/shard_map/ppermute | solution.py:44
  234.6 21.1 %collective-permute-start.28 = (bf16[1,960,128]{2,1,0:T(8,128)(2,1)}, bf16[1,960,128]{2,1,0:T(8,128)(2,1)}, u32[]{:S(2)}, u32[]{:S(2)}) collective-permute-start(bf16[1,960,128]{2,1,0:T(8,128)(2,1)} %fusion.3), channel_id=1, source_target_pairs={{0,16},{4,20},{8,24},{12,28},{16,0},{20,4},{24,8},{28,12},{1,17},{... | collective-permute-start | bytes 737288 | tf_op jit(solution)/shard_map/ppermute | solution.py:44
  238.2 15.4 %collective-permute-start.34 = (bf16[1,640,128]{2,1,0:T(8,128)(2,1)S(1)}, bf16[1,640,128]{2,1,0:T(8,128)(2,1)S(1)}, u32[]{:S(2)}, u32[]{:S(2)}) collective-permute-start(bf16[1,640,128]{2,1,0:T(8,128)(2,1)S(1)} %fusion.8), channel_id=1, source_target_pairs={{0,16},{4,20},{8,24},{12,28},{16,0},{20,4},{24,8},{28,12},{1,17},{... | collective-permute-start | bytes 491528 | tf_op jit(solution)/shard_map/ppermute | solution.py:44
  255.1 4.6 %collective-permute-start.39 = (bf16[320,128]{1,0:T(8,128)(2,1)S(1)}, bf16[320,128]{1,0:T(8,128)(2,1)S(1)}, u32[]{:S(2)}, u32[]{:S(2)}) collective-permute-start(bf16[320,128]{1,0:T(8,128)(2,1)S(1)} %add_convert_fusion.13), channel_id=1, source_target_pairs={{0,2},{1,3},{2,0},{3,1},{4,6},{5,7},{6,4},{7,5},{8,10},{9,11},{10,... | collective-permute-start | bytes 245768 | tf_op jit(solution)/shard_map/ppermute | solution.py:44
  (143 other events, 974.0 us)

commit v3 on v2

--- a/solution.py
+++ b/solution.py
@@ -8,6 +8,8 @@
 WINDOW = 512
 SEQ_LEN = 512
 LANES = 128
+VMEM_BYTES = 12 << 20
+GAIN_ROWS = 16
 
 epsilon = 1e-06
 score_scale = 0.0625
@@ -60,7 +62,7 @@
     return (pair, swap(pair, "tensor", 2))
 
 
-def kernel_call(body, outs, args, layers=None, flops=0):
+def kernel_call(body, outs, args, layers=None, scratch=()):
     layers = layers or {}
 
     def spec(place, arg):
@@ -72,15 +74,15 @@
             return pl.BlockSpec(memory_space=pltpu.SMEM)
         return pl.BlockSpec(arg.shape, lambda i, n=arg.ndim: (0,) * n)
 
-    moved = sum(a.size * a.dtype.itemsize for a in args)
     return pl.pallas_call(
         body,
         grid=(1,),
         in_specs=[spec(place, arg) for place, arg in enumerate(args)],
         out_specs=[pl.BlockSpec(o.shape, lambda i, n=len(o.shape): (0,) * n) for o in outs],
         out_shape=list(outs),
-        compiler_params=pltpu.CompilerParams(vmem_limit_bytes=40 << 20),
-        cost_estimate=pl.CostEstimate(flops=flops, transcendentals=0, bytes_accessed=moved),
+        scratch_shapes=list(scratch),
+        compiler_params=pltpu.CompilerParams(vmem_limit_bytes=VMEM_BYTES),
+        cost_estimate=pl.CostEstimate(flops=1, transcendentals=0, bytes_accessed=1),
     )(*args)
 
 
@@ -227,21 +229,21 @@
 
 
 def back_to_input(pair, other, stream, grad_middle, gains, layer):
-    def body(pair_ref, other_ref, stream_ref, grad_ref, gains_ref, out_ref, gain0_ref):
-        grad_normed = total(pair_ref, other_ref)
-        step, gain0_ref[...] = norm_back(
-            stream_ref[...].astype(F32), gains_ref[0, 0:1, :], grad_normed
+    def body(pair_ref, other_ref, stream_ref, grad_ref, gains_ref, out_ref):
+        own = out_ref.shape[0]
+        grad_normed = pair_ref[:own, :].astype(F32) + other_ref[own:, :].astype(F32)
+        step, unused = norm_back(
+            stream_ref[:own, :].astype(F32), gains_ref[0, 0:1, :], grad_normed
         )
-        own = out_ref.shape[0]
-        out_ref[...] = (grad_ref[:own, :] + step[:own, :]).astype(BF16)
+        out_ref[...] = (grad_ref[:own, :] + step).astype(BF16)
 
     rows, columns = pair.shape
     return kernel_call(
         body,
-        [shape(rows // 2, columns, BF16), shape(1, columns, F32)],
+        [shape(rows // 2, columns, BF16)],
         (pair, other, stream, grad_middle, gains),
         {4: layer},
-    )
+    )[0]
 
 
 def allowed_rows(down_ref, across_ref, start, count, window):
@@ -305,7 +307,6 @@
         + [shape(length, 1, F32)],
         (own, received, w_query, w_key, w_value, w_out, qk_gains, cosine, sine, down, across),
         {place: layer for place in (2, 3, 4, 5, 6)},
-        flops=1_000_000_000,
     )
 
 
@@ -335,7 +336,6 @@
         + [shape(length, hidden_width, BF16)],
         (own, received, w_gate, w_up, w_down),
         {2: layer, 3: layer, 4: layer},
-        flops=1_000_000_000,
     )
 
 
@@ -372,11 +372,10 @@
         [shape(half, width, BF16)] * 2 + [shape(length, hidden_width, BF16)] * 2,
         (own, received, w_gate, w_up, w_down, gate, up),
         {2: layer, 3: layer, 4: layer},
-        flops=1_000_000_000,
-    )
-
-
-def attention_back(own, received, weights, tables, saved, layer, window):
+    )
+
+
+def attention_back(own, received, weights, tables, saved, side, layer, window, first=()):
     w_query, w_key, w_value, w_out, qk_gains = weights
     cosine, sine, down, across = tables
     query_raw, key_raw, queries, key_rows, values, row_lse = saved
@@ -387,9 +386,12 @@
     def body(
         own_ref, received_ref, wq_ref, wk_ref, wv_ref, wo_ref, gain_ref,
         cos_ref, sin_ref, down_ref, across_ref,
-        qraw_ref, kraw_ref, q_ref, k_ref, v_ref, lse_ref,
-        kept_ref, sent_ref, gq_ref, gk_ref, gv_ref, qgain_ref, kgain_ref,
+        qraw_ref, kraw_ref, q_ref, k_ref, v_ref, lse_ref, side_ref,
+        *rest,
     ):
+        firsts, rest = rest[: len(first)], rest[len(first) :]
+        kept_ref, sent_ref, gq_ref, mine_ref, theirs_ref, qgain_ref, kgain_ref = rest[:7]
+        *gain0_refs, gk_ref, gv_ref = rest[7:]
         grad_keys = None
         grad_values = None
         query_gain = None
@@ -418,6 +420,17 @@
         grad_raw, kgain_ref[...] = norm_back(kraw_ref[...], gain_ref[0, 1:2, :], turned)
         gk_ref[...] = grad_raw.astype(BF16)
         gv_ref[...] = grad_values.astype(BF16)
+
+        @pl.when(side_ref[0] == 0)
+        def keys_here():
+            mine_ref[...] = gk_ref[...]
+            theirs_ref[...] = gv_ref[...]
+
+        @pl.when(side_ref[0] != 0)
+        def values_here():
+            mine_ref[...] = gv_ref[...]
+            theirs_ref[...] = gk_ref[...]
+
         for part, target in ((1, sent_ref), (0, kept_ref)):
             rows = slice(part * half, (part + 1) * half)
             target[...] = (
@@ -425,18 +438,34 @@
                 + product_right(gk_ref[rows, :], wk_ref[0])
                 + product_right(gv_ref[rows, :], wv_ref[0])
             ).astype(BF16)
-
+        if first:
+            low_ref, other_ref, norm_ref = firsts
+            gain0_refs[0][...] = (
+                jnp.sum(
+                    kept_ref[...].astype(F32) * low_ref[...].astype(F32)
+                    + sent_ref[...].astype(F32) * other_ref[...].astype(F32),
+                    axis=0,
+                    keepdims=True,
+                )
+                / norm_ref[0, 0:1, :]
+            )
+
+    fixed = {place: layer for place in (2, 3, 4, 5, 6)}
+    if first:
+        fixed[20] = layer
     return kernel_call(
         body,
         [shape(half, width, BF16)] * 2
         + [shape(length, head_width, BF16)] * 3
-        + [shape(1, head_width, F32)] * 2,
+        + [shape(1, head_width, F32)] * 2
+        + [shape(1, width, F32)] * (1 if first else 0),
         (
             own, received, w_query, w_key, w_value, w_out, qk_gains,
-            cosine, sine, down, across, query_raw, key_raw, queries, key_rows, values, row_lse,
+            cosine, sine, down, across, query_raw, key_raw, queries, key_rows, values, row_lse, side,
+            *first,
         ),
-        {place: layer for place in (2, 3, 4, 5, 6)},
-        flops=1_500_000_000,
+        fixed,
+        scratch=[pltpu.VMEM((length, head_width), BF16)] * 2,
     )
 
 
@@ -448,7 +477,7 @@
     ]
 
 
-def gradient_blocks(factors, me, bits):
+def gradient_blocks(factors, me, bits, gains=()):
     pieces = 1 << len(bits)
     masks = slot_masks(bits)
     sizes = [(l[0].shape[1] // pieces, r[0].shape[1] // LANES) for l, r in factors]
@@ -460,6 +489,15 @@
             grad = product_left(jnp.concatenate(left), jnp.concatenate(right)).astype(BF16)
             cut = grad.reshape(pieces, tall, wide, LANES).transpose(0, 2, 1, 3)
             parts.append(cut.reshape(pieces, tall * wide, LANES))
+        if gains:
+            rows = [
+                jnp.pad(row.reshape(pieces, 1, -1), ((0, 0), (0, 0), (0, LANES - row.shape[1] // pieces)))
+                for row in gains
+            ]
+            block = jnp.concatenate(rows, axis=1)
+            parts.append(
+                jnp.pad(block, ((0, 0), (0, GAIN_ROWS - len(rows)), (0, 0))).astype(BF16)
+            )
         blocks = jnp.take(jnp.concatenate(parts, axis=1), chunks, axis=0)
         return (blocks[: pieces // 2], blocks[pieces // 2 :])
     flat = []
@@ -472,7 +510,9 @@
         where.append(places)
 
     def body(*refs):
-        me_ref, inputs, (kept_ref, sent_ref, *scratch) = refs[0], refs[1 : 1 + len(flat)], refs[1 + len(flat) :]
+        me_ref, inputs = refs[0], refs[1 : 1 + len(flat)]
+        gain_refs = refs[1 + len(flat) : 1 + len(flat) + len(gains)]
+        kept_ref, sent_ref, *scratch = refs[1 + len(flat) + len(gains) :]
         base = 0
         for (lefts, rights), (tall, wide), held in zip(where, sizes, scratch):
             def side(places):
@@ -491,11 +531,27 @@
                         :, column * LANES : (column + 1) * LANES
                     ]
             base += tall * wide
-
+        if gains:
+            table = scratch[-1]
+            table[...] = jnp.zeros_like(table)
+            for place, ref in enumerate(gain_refs):
+                count = ref.shape[1] // pieces
+                for chunk in range(pieces):
+                    line = chunk * GAIN_ROWS + place
+                    table[line : line + 1, :count] = ref[:, chunk * count : (chunk + 1) * count]
+            for slot, mask in enumerate(masks):
+                chunk = jnp.bitwise_xor(me_ref[0], mask)
+                start = pl.multiple_of(chunk * GAIN_ROWS, GAIN_ROWS)
+                target = kept_ref if slot < pieces // 2 else sent_ref
+                target[slot % (pieces // 2), base : base + GAIN_ROWS, :] = table[
+                    pl.ds(start, GAIN_ROWS), :
+                ].astype(BF16)
+
+    rows += GAIN_ROWS if gains else 0
     out = jax.ShapeDtypeStruct((pieces // 2, rows, LANES), BF16)
-    args = (me, *flat)
+    args = (me, *flat, *gains)
     specs = [pl.BlockSpec(memory_space=pltpu.SMEM)] + [
-        pl.BlockSpec(a.shape, lambda i: (0, 0)) for a in flat
+        pl.BlockSpec(a.shape, lambda i: (0, 0)) for a in args[1:]
     ]
     return pl.pallas_call(
         body,
@@ -505,83 +561,112 @@
         out_shape=[out, out],
         scratch_shapes=[
             pltpu.VMEM((tall * pieces, wide * LANES), F32) for tall, wide in sizes
-        ],
-        compiler_params=pltpu.CompilerParams(vmem_limit_bytes=40 << 20),
-        cost_estimate=pl.CostEstimate(
-            flops=1_000_000_000,
-            transcendentals=0,
-            bytes_accessed=sum(a.size * a.dtype.itemsize for a in args),
-        ),
+        ]
+        + [pltpu.VMEM((pieces * GAIN_ROWS, LANES), F32)] * (1 if gains else 0),
+        compiler_params=pltpu.CompilerParams(vmem_limit_bytes=VMEM_BYTES),
+        cost_estimate=pl.CostEstimate(flops=1, transcendentals=0, bytes_accessed=1),
     )(*args)
 
 
-def halved(blocks, bits):
-    kept, sent = blocks
-    for bit in bits[:-1]:
-        arrived = swap(sent, "dp", bit)
-        middle = kept.shape[0] // 2
-        sent = (kept[middle:].astype(F32) + arrived[middle:].astype(F32)).astype(BF16)
-        kept = kept[:middle].astype(F32) + arrived[:middle].astype(F32)
-    return kept[0].astype(F32) + swap(sent, "dp", bits[-1])[0].astype(F32)
-
-
-def over_tensor(rows):
-    for bit in (1, 2):
-        low = rows.astype(BF16)
-        rows = low.astype(F32) + swap(low, "tensor", bit).astype(F32)
-    return rows
-
-
-def over_all(rows):
-    bit = 1
-    while bit < lax.axis_size("dp"):
-        low = rows.astype(BF16)
-        rows = low.astype(F32) + swap(low, "dp", bit).astype(F32)
-        bit *= 2
-    return over_tensor(rows)
-
-
-def assembled(sources, layout, tall_of, columns_of):
-    outs = [
-        jax.ShapeDtypeStruct((2, tall, columns), F32)
-        for tall, columns in zip(tall_of, columns_of)
+def after(gate, *values):
+    return lax.optimization_barrier((gate,) + values)[1:]
+
+
+class Halving:
+    def __init__(self, terms, me, bits, gains=()):
+        self.kept, sent = gradient_blocks(terms, me, bits, gains)
+        self.bits = bits
+        self.arrived = swap(sent, "dp", bits[0])
+
+    def step(self, gate=None):
+        if not self.bits:
+            return
+        kept, arrived = self.kept, self.arrived
+        if gate is not None:
+            kept, arrived = after(gate, kept, arrived)
+        self.bits = self.bits[1:]
+        if self.bits:
+            middle = kept.shape[0] // 2
+            sent = (kept[middle:].astype(F32) + arrived[middle:].astype(F32)).astype(BF16)
+            self.arrived = swap(sent, "dp", self.bits[0])
+            self.kept = kept[:middle].astype(F32) + arrived[:middle].astype(F32)
+        else:
+            self.kept = kept[0].astype(F32) + arrived[0].astype(F32)
+
+    def finish(self):
+        while self.bits:
+            self.step()
+        return self.kept
+
+
+def assembled(sources, layout, sizes, exchanged, starts, shared_size, gains_at, gain_widths):
+    sizes = sizes + [shared_size] * 2
+    here, there, side = exchanged
+    outs = [jax.ShapeDtypeStruct((2, tall, columns), F32) for tall, columns in sizes]
+    outs += [
+        jax.ShapeDtypeStruct((2, 4, gain_widths[0]), F32),
+        jax.ShapeDtypeStruct((2, 2, gain_widths[1]), F32),
     ]
 
-    def cut(read, start, tall, columns):
-        return [
-            read(start + column * tall, tall) for column in range(columns // LANES)
+    if any(tall % 16 for tall, columns in sizes):
+
+        def joined(array, start, tall, columns):
+            return jnp.concatenate(
+                [
+                    array[start + place * tall : start + (place + 1) * tall]
+                    for place in range(columns // LANES)
+                ],
+                axis=1,
+            ).astype(F32)
+
+        results = [
+            jnp.stack([joined(sources[source], start, *size) for source, start in both])
+            for both, size in zip(layout, sizes)
         ]
-
-    if any(tall % 8 for tall in tall_of):
-        results = []
-        for member, (tall, columns) in enumerate(zip(tall_of, columns_of)):
-            both = [
-                jnp.concatenate(
-                    cut(lambda a, n: sources[source][a : a + n], start, tall, columns), axis=1
-                )
-                for source, start in layout[member]
-            ]
-            results.append(jnp.stack(both))
-        return results
+        for first, second in ((here, there), (there, here)):
+            picked = jnp.where(side == 0, first, second)
+            results.append(jnp.stack([joined(picked, start, *shared_size) for start in starts]))
+        gains = here[gains_at : gains_at + GAIN_ROWS].astype(F32)
+        gains = (gains + there[gains_at : gains_at + GAIN_ROWS].astype(F32))[:12]
+        gains = gains.reshape(2, 6, LANES)
+        return results + [gains[:, :4, : gain_widths[0]], gains[:, 4:, : gain_widths[1]]]
 
     def body(*refs):
-        inputs, targets = refs[: len(sources)], refs[len(sources) :]
-        for member, (tall, columns) in enumerate(zip(tall_of, columns_of)):
-            for layer, (source, start) in enumerate(layout[member]):
-                for column in range(columns // LANES):
-                    low = start + column * tall
-                    targets[member][layer, :, column * LANES : (column + 1) * LANES] = inputs[
-                        source
-                    ][low : low + tall, :]
-
-    return pl.pallas_call(
-        body,
-        grid=(1,),
-        in_specs=[pl.BlockSpec(a.shape, lambda i: (0, 0)) for a in sources],
-        out_specs=[pl.BlockSpec(o.shape, lambda i: (0, 0, 0)) for o in outs],
-        out_shape=outs,
-        compiler_params=pltpu.CompilerParams(vmem_limit_bytes=40 << 20),
-    )(*sources)
+        inputs = refs[: len(sources)]
+        here_ref, there_ref, side_ref = refs[len(sources) : len(sources) + 3]
+        *targets, norm_ref, qk_ref = refs[len(sources) + 3 :]
+
+        def put(target, layer, source, start, tall, columns):
+            for column in range(columns // LANES):
+                low = start + column * tall
+                target[layer, :, column * LANES : (column + 1) * LANES] = source[
+                    low : low + tall, :
+                ].astype(F32)
+
+        for member, both in enumerate(layout):
+            for layer, (source, start) in enumerate(both):
+                put(targets[member], layer, inputs[source], start, *sizes[member])
+        key_ref, value_ref = targets[-2:]
+
+        @pl.when(side_ref[0] == 0)
+        def keys_here():
+            for layer, start in enumerate(starts):
+                put(key_ref, layer, here_ref, start, *shared_size)
+                put(value_ref, layer, there_ref, start, *shared_size)
+
+        @pl.when(side_ref[0] != 0)
+        def values_here():
+            for layer, start in enumerate(starts):
+                put(key_ref, layer, there_ref, start, *shared_size)
+                put(value_ref, layer, here_ref, start, *shared_size)
+
+        gains = here_ref[gains_at : gains_at + GAIN_ROWS, :].astype(F32)
+        gains = gains + there_ref[gains_at : gains_at + GAIN_ROWS, :].astype(F32)
+        for layer in range(2):
+            norm_ref[layer] = gains[6 * layer : 6 * layer + 4, : gain_widths[0]]
+            qk_ref[layer] = gains[6 * layer + 4 : 6 * layer + 6, : gain_widths[1]]
+
+    return kernel_call(body, outs, (*sources, here, there, side))
 
 
 def local(
@@ -604,6 +689,10 @@
     pieces = lax.axis_size("dp")
     quarter = lax.axis_index("tensor")
     me = lax.axis_index("dp").astype(jnp.int32).reshape(1)
+    side = jnp.bitwise_and(quarter, 1).astype(jnp.int32).reshape(1)
+    hidden_in, segments, positions, quarter, me, side = lax.optimization_barrier(
+        (hidden_in, segments, positions, quarter, me, side)
+    )
     bits = [1 << place for place in range(pieces.bit_length() - 1)]
     turned_bits = bits[1::-1] + bits[2:]
     seg_rows = relative_order(segments, quarter)
@@ -636,7 +725,7 @@
 
     grad_stream = two_quarters(cotangent)
     output, low, gain3 = turn_around(pair, other, middle, grad_stream, norm_gains, 1)
-    sums = [None, None]
+    sums = {}
     gain_rows = [None, None]
     for layer in (1, 0):
         attn_in, kept_attn, attn_sum, middle, mlp_in, kept_mlp, stream = saved[layer]
@@ -648,62 +737,64 @@
         )
         mlp_out = (low, received)
         pair, other = summed_pair(kept, sent)
-        mlp_order = bits if layer == 1 else turned_bits
-        mlp_blocks = gradient_blocks(
-            [(mlp_in, (gate_low,)), (mlp_in, (up_low,)), ((hidden,), mlp_out)], me, mlp_order
-        )
+        gate_low, up_low = after(pair, gate_low, up_low)
+        gate_term, up_term = (mlp_in, (gate_low,)), (mlp_in, (up_low,))
+        down_term = ((hidden,), mlp_out)
+        if layer == 1:
+            sums["mlp1"] = Halving([gate_term, up_term, down_term], me, bits)
+            (other,) = after(sums["mlp1"].kept, other)
+        else:
+            sums["mlp0"] = Halving([gate_term, up_term, down_term], me, bits)
+            made = sums["mlp0"].kept
+            sums["mlp1"].step(made)
+            sums["attn1"].step(made)
+            (other,) = after([s.kept for s in sums.values()], other)
         grad_middle, low, gain1, gain2 = back_to_attention(
             pair, other, middle, attn_sum, grad_stream, norm_gains, layer
         )
         received = swap(low, "tensor", 1)
-        kept, sent, grad_q, grad_k, grad_v, gain_q, gain_k = attention_back(
+        kept, sent, grad_q, mine, theirs, gain_q, gain_k, *gain0 = attention_back(
             low,
             received,
             attn_weights,
             tables[layer],
             (query_raw, key_raw, queries, key_rows, values, row_lse),
+            side,
             layer,
             windows[layer],
+            () if layer else (*attn_in, norm_gains),
         )
         pair, other = summed_pair(kept, sent)
-        attn_order = turned_bits if layer == 1 else bits
-        attn_blocks = gradient_blocks(
-            [
-                (attn_in, (grad_q,)),
-                ((attended,), (low, received)),
-                (attn_in, (grad_k,)),
-                (attn_in, (grad_v,)),
-            ],
-            me,
-            attn_order,
-        )
-        sums[layer] = (halved(mlp_blocks, mlp_order), halved(attn_blocks, attn_order))
-        gain_rows[layer] = [None, gain1, gain2, gain3, gain_q, gain_k]
+        theirs = swap(theirs, "tensor", 1)
         if layer == 1:
-            grad_stream, low, gain_rows[1][0], gain3 = back_between(
+            grad_q, mine, theirs = after(pair, grad_q, mine, theirs)
+        shared_term = (attn_in + attn_in[::-1], (mine, theirs))
+        query_term, out_term = (attn_in, (grad_q,)), ((attended,), (low, received))
+        gain_rows[layer] = [None, gain1 * 0.5, gain2 * 0.5, gain3 * 0.5, gain_q, gain_k]
+        if layer == 1:
+            sums["attn1"] = Halving([query_term, out_term, shared_term], me, bits)
+            sums["mlp1"].step(sums["attn1"].kept)
+            (other,) = after([s.kept for s in sums.values()], other)
+            grad_stream, low, gain0, gain3 = back_between(
                 pair, other, stream, grad_middle, mlp_sum, norm_gains, layer
             )
+            gain_rows[1][0] = gain0 * 0.5
         else:
-            grad_input, gain_rows[0][0] = back_to_input(
-                pair, other, stream, grad_middle, norm_gains, layer
+            gain_rows[0][0] = gain0[0]
+            sums["attn0"] = Halving(
+                [query_term, out_term, shared_term],
+                me,
+                turned_bits,
+                gain_rows[0] + gain_rows[1],
             )
-
-    width = norm_gains.shape[2]
-    gain_terms = jnp.concatenate(
-        [
-            jnp.pad(row * 0.5 if place < 4 else row, ((0, 0), (0, width - row.shape[1])))
-            for layer in range(2)
-            for place, row in enumerate(gain_rows[layer])
-        ]
-    )
-    gains = over_all(gain_terms).reshape(2, 6, width)
-
-    def own_columns(array, columns):
-        return lax.dynamic_slice_in_dim(array[:, :, :columns], me[0] * (columns // pieces), columns // pieces, 2)
-
-    grad_norm_gains = own_columns(gains[:, :4], width)
-    grad_qk_gains = own_columns(gains[:, 4:], head_width)
-
+            for name in ("mlp1", "attn1", "mlp0"):
+                sums[name].step(sums["attn0"].kept)
+            grad_input = back_to_input(pair, other, stream, grad_middle, norm_gains, layer)
+
+    sums["attn0"].step(sums["mlp0"].kept)
+    sums["attn0"].step()
+    sums["mlp0"].step(sums["attn0"].kept)
+    sums["attn0"].finish()
     tall = {
         "q": w_query.shape[1] // pieces,
         "o": w_out.shape[1] // pieces,
@@ -711,26 +802,45 @@
         "d": w_down.shape[1] // pieces,
     }
     heads_rows = tall["q"] * head_width // LANES
-    out_rows = tall["o"] * w_out.shape[2] // LANES
     gate_rows = tall["g"] * w_gate.shape[2] // LANES
-    shared = [over_tensor(sums[layer][1][heads_rows + out_rows :]) for layer in range(2)]
-    sources = [sums[0][0], sums[1][0], sums[0][1], sums[1][1], shared[0], shared[1]]
-    layout = [
-        [(2, 0), (3, 0)],
-        [(4, 0), (5, 0)],
-        [(4, heads_rows), (5, heads_rows)],
-        [(2, heads_rows), (3, heads_rows)],
-        [(0, 0), (1, 0)],
-        [(0, gate_rows), (1, gate_rows)],
-        [(0, 2 * gate_rows), (1, 2 * gate_rows)],
-    ]
-    grads = assembled(
-        sources,
-        layout,
-        [tall["q"], tall["q"], tall["q"], tall["o"], tall["g"], tall["g"], tall["d"]],
-        [head_width] * 3 + [w_out.shape[2], w_gate.shape[2], w_up.shape[2], w_down.shape[2]],
-    )
-    return (output, grad_input, *grads, grad_norm_gains, grad_qk_gains)
+    both_rows = heads_rows + tall["o"] * w_out.shape[2] // LANES
+    done = {name: halving.finish() for name, halving in sums.items()}
+    low = jnp.concatenate([done["attn0"][both_rows:], done["attn1"][both_rows:]]).astype(BF16)
+    here = (low.astype(F32) + swap(low, "tensor", 2).astype(F32)).astype(BF16)
+    there = swap(here, "tensor", 1)
+    first_rows = done["attn0"].shape[0] - both_rows
+    *grads, grad_norm_gains, grad_qk_gains = assembled(
+        [done[name] for name in ("attn0", "attn1", "mlp0", "mlp1")],
+        [
+            [(0, 0), (1, 0)],
+            [(0, heads_rows), (1, heads_rows)],
+            [(2, 0), (3, 0)],
+            [(2, gate_rows), (3, gate_rows)],
+            [(2, 2 * gate_rows), (3, 2 * gate_rows)],
+        ],
+        [(tall["q"], head_width), (tall["o"], w_out.shape[2])]
+        + [(tall["g"], w_gate.shape[2])] * 2
+        + [(tall["d"], w_down.shape[2])],
+        (here, there, side),
+        [0, first_rows],
+        (tall["q"], head_width),
+        first_rows - GAIN_ROWS,
+        (norm_gains.shape[2] // pieces, head_width // pieces),
+    )
+    grad_query, grad_out, grad_gate, grad_up, grad_down, grad_key, grad_value = grads
+    return (
+        output,
+        grad_input,
+        grad_query,
+        grad_key,
+        grad_value,
+        grad_out,
+        grad_gate,
+        grad_up,
+        grad_down,
+        grad_norm_gains,
+        grad_qk_gains,
+    )
 
 
 def solution(mesh):

time: 262 us -> 188 us (0.72)
  local copies, waits for them, and re-layouts: 36.4 us -> 3.77 us
  waiting for transfers between devices: 134 us -> 109 us
  other arithmetic: 11 us -> 3.82 us
  Pallas kernels: 34.9 us -> 30.3 us
  starting transfers between devices: 42.9 us -> 40 us
    unnamed x258 -> x24, local copies, waits for them, and re-layouts: 32.5 us -> 1.88 us
    ppermute x47 -> x42, waiting for transfers between devices: 134 us -> 109 us  [swap(): return lax.ppermute(array, axis, [(i, i ^ bit) for i in range(size)])]
    convert_element_type x14 -> x9, other arithmetic: 4.29 us -> 0.94 us  [the longest x8 0.91 us: step(): (kept[middle:].astype(F32) + arrived[middle:].astype(F32)).astype(BF16)]
    pallas_call x4, Pallas kernels: 8.02 us -> 4.79 us  [gradient_blocks(): pl.pallas_call(body, grid=(1,), in_specs=specs, out_specs=[pl.BlockSpec(o...]
    ppermute x47 -> x42, starting transfers between devices: 42.9 us -> 40 us  [swap(): return lax.ppermute(array, axis, [(i, i ^ bit) for i in range(size)])]
    pallas_call x17 -> x18, Pallas kernels: 25.6 us -> 25.5 us  [kernel_call(): pl.pallas_call(body, grid=(1,), in_specs=[spec(place, arg) for place, arg...]
  transfers between devices with their start and end apart: 47 -> 42, of which waited for: 30 -> 28; matrix products, arithmetic and copies ran while one was open for 6% -> 3% of each run, Pallas kernels for 8% -> 9%
where the time goes in v3:
time: 188 us
  waiting for transfers between devices  109 us (58%)
  starting transfers between devices  40 us (21%)
  Pallas kernels  30.3 us (16%)
  other arithmetic  3.82 us (2%)
  local copies, waits for them, and re-layouts  3.77 us (2%)
    ppermute x42, waiting for transfers between devices, swap(): return lax.ppermute(array, axis, [(i, i ^ bit) for i in range(size)])  109 us
    ppermute x42, starting transfers between devices, swap(): return lax.ppermute(array, axis, [(i, i ^ bit) for i in range(size)])  40 us
    pallas_call x18, Pallas kernels, kernel_call(): pl.pallas_call(body, grid=(1,), in_specs=[spec(place, arg) for place, arg...  25.5 us
    pallas_call x4, Pallas kernels, gradient_blocks(): pl.pallas_call(body, grid=(1,), in_specs=specs, out_specs=[pl.BlockSpec(o...  4.79 us
  transfers between devices with their start and end apart: 42, of which 28 were waited for; matrix products, arithmetic and copies ran while one was open for 3% of the time, Pallas kernels for 9%

profile of v3, /device:TPU:0, one launch (start us, length us, event | category | flops | bytes accessed | tf_op | source)
XLA Modules:
  0.0 187.7 jit_solution(15269371194728201433)
XLA Ops:
  0.6 3.0 %collective-permute-start = (bf16[128,640]{1,0:T(8,128)(2,1)}, bf16[128,640]{1,0:T(8,128)(2,1)S(1)}, u32[]{:S(2)}, u32[]{:S(2)}) collective-permute-start(bf16[128,640]{1,0:T(8,128)(2,1)} %param.13), channel_id=1, source_target_pairs={{0,2},{1,3},{2,0},{3,1},{4,6},{5,7},{6,4},{7,5},{8,10},{9,11},{10,... | collective-permute-start | bytes 491528 | tf_op jit(solution)/shard_map/ppermute | solution.py:46
  9.1 1.9 %multiply_sine_fusion = (f32[512,128]{1,0:T(8,128)S(1)}, f32[512,128]{1,0:T(8,128)S(1)}, f32[512,128]{1,0:T(8,128)S(1)}, f32[512,128]{1,0:T(8,128)S(1)}) fusion(f32[128]{0:T(128)S(1)} %get-tuple-element.291, f32[512]{0:T(512)S(1)} %get-tuple-element.289, f32[128]{0:T(128)S(1)} %get-tuple-element.292), kind=kLoop, calls=%fused_computation.21 | loop fusion | flops 131072 | bytes 1051648 | tf_op jit(solution)/shard_map/sin | solution.py:41
  11.1 2.4 %shard_map.213 = (bf16[256,640]{1,0:T(8,128)(2,1)S(1)}, bf16[256,640]{1,0:T(8,128)(2,1)S(1)}, f32[512,256]{1,0:T(8,128)S(1)}, f32[512,256]{1,0:T(8,128)S(1)}, bf...) custom-call(bf16[256,640]{1,0:T(8,128)(2,1)S(1)} %shard_map.212.own_, ...), custom_call_target="tpu_custom_call" | custom-call | flops 1 | bytes 1 | tf_op jit(solution)/shard_map/pallas_call | solution.py:77
  15.4 1.8 collective-permute-start.3
  17.3 8.2 %collective-permute-done.3.other_ref = bf16[256,640]{1,0:T(8,128)(2,1)S(1)} collective-permute-done((bf16[256,640]{1,0:T(8,128)(2,1)S(1)}, bf16[256,640]{1,0:T(8,128)(2,1)S(1)}, u32[]{:S(2)}, u32[]{:S(2)}) %collective-permute-start.3) | collective-permute-done | bytes 327712 | tf_op jit(solution)/shard_map/ppermute | solution.py:46
  30.9 1.8 collective-permute-start.6
  32.8 8.0 %collective-permute-done.6.other_ref = bf16[256,640]{1,0:T(8,128)(2,1)S(1)} collective-permute-done((bf16[256,640]{1,0:T(8,128)(2,1)S(1)}, bf16[256,640]{1,0:T(8,128)(2,1)S(1)}, u32[]{:S(2)}, u32[]{:S(2)}) %collective-permute-start.6) | collective-permute-done | bytes 327712 | tf_op jit(solution)/shard_map/ppermute | solution.py:46
  42.8 2.4 %shard_map.217 = (bf16[256,640]{1,0:T(8,128)(2,1)S(1)}, bf16[256,640]{1,0:T(8,128)(2,1)S(1)}, f32[512,256]{1,0:T(8,128)S(1)}, f32[512,256]{1,0:T(8,128)S(1)}, bf...) custom-call(bf16[256,640]{1,0:T(8,128)(2,1)S(1)} %get-tuple-element., ...), custom_call_target="tpu_custom_call" | custom-call | flops 1 | bytes 1 | tf_op jit(solution)/shard_map/pallas_call | solution.py:77
  47.0 1.8 collective-permute-start.9
  48.8 8.0 %collective-permute-done.9.other_ref = bf16[256,640]{1,0:T(8,128)(2,1)S(1)} collective-permute-done((bf16[256,640]{1,0:T(8,128)(2,1)S(1)}, bf16[256,640]{1,0:T(8,128)(2,1)S(1)}, u32[]{:S(2)}, u32[]{:S(2)}) %collective-permute-start.9) | collective-permute-done | bytes 327712 | tf_op jit(solution)/shard_map/ppermute | solution.py:46
  62.2 1.8 collective-permute-start.12
  64.4 11.2 %collective-permute-done.13 = bf16[128,640]{1,0:T(8,128)(2,1)S(1)} collective-permute-done((bf16[128,640]{1,0:T(8,128)(2,1)S(1)}, bf16[128,640]{1,0:T(8,128)(2,1)S(1)}, u32[]{:S(2)}, u32[]{:S(2)}) %collective-permute-start.13) | collective-permute-done | bytes 163872 | tf_op jit(solution)/shard_map/ppermute | solution.py:46
  78.3 2.0 %shard_map.221 = (bf16[256,640]{1,0:T(8,128)(2,1)S(1)}, bf16[256,640]{1,0:T(8,128)(2,1)S(1)}, bf16[512,512]{1,0:T(8,128)(2,1)S(1)}, bf16[512,512]{1,0:T(8,128)(2,1)S(1)}) custom-call(bf16[256,640]{1,0:T(8,128)(2,1)S(1)} %get-tuple-element.154.own_ref.refs_8_, bf16[256,640]{1,0:T(8,128)(2,1)S(1)} %collective-permute-done.14.received_ref.refs_9_, ...), custom_call_target="tpu_custom_call" | custom-call | flops 1 | bytes 1 | tf_op jit(solution)/shard_map/pallas_call | solution.py:77
  82.1 1.8 collective-permute-start.16
  86.9 5.0 %collective-permute-done.16.other_ref = bf16[256,640]{1,0:T(8,128)(2,1)S(1)} collective-permute-done((bf16[256,640]{1,0:T(8,128)(2,1)S(1)}, bf16[256,640]{1,0:T(8,128)(2,1)S(1)}, u32[]{:S(2)}, u32[]{:S(2)}) %collective-permute-start.16) | collective-permute-done | bytes 327712 | tf_op jit(solution)/shard_map/ppermute | solution.py:46
  94.3 3.3 %shard_map.224 = (bf16[256,640]{1,0:T(8,128)(2,1)S(1)}, bf16[256,640]{1,0:T(8,128)(2,1)S(1)}, bf16[512,256]{1,0:T(8,128)(2,1)S(1)}, bf16[512,256]{1,0:T(8,128)(2...) custom-call(bf16[256,640]{1,0:T(8,128)(2,1)S(1)} %get-tuple-element.168.own_ref.refs_5_, ...), custom_call_target="tpu_custom_call" | custom-call | flops 1 | bytes 1 | tf_op jit(solution)/shard_map/pallas_call | solution.py:77
  99.5 1.8 collective-permute-start.21
  102.3 6.6 %collective-permute-done.20 = bf16[4,960,128]{2,1,0:T(8,128)(2,1)S(1)} collective-permute-done((bf16[4,960,128]{2,1,0:T(8,128)(2,1)S(1)}, bf16[4,960,128]{2,1,0:T(8,128)(2,1)S(1)}, u32[]{:S(2)}, u32[]{:S(2)}) %collective-permute-start.20) | collective-permute-done | bytes 983072 | tf_op jit(solution)/shard_map/ppermute | solution.py:46
  110.1 1.8 collective-permute-start.25
  112.0 1.9 %shard_map.227 = (bf16[256,640]{1,0:T(8,128)(2,1)S(1)}, bf16[256,640]{1,0:T(8,128)(2,1)S(1)}, bf16[512,512]{1,0:T(8,128)(2,1)S(1)}, bf16[512,512]{1,0:T(8,128)(2,1)S(1)}) custom-call(bf16[256,640]{1,0:T(8,128)(2,1)S(1)} %get-tuple-element.192.own_ref.refs_8_, bf16[256,640]{1,0:T(8,128)(2,1)S(1)} %collective-permute-done.22.received_ref.refs_9_, ...), custom_call_target="tpu_custom_call" | custom-call | flops 1 | bytes 1 | tf_op jit(solution)/shard_map/pallas_call | solution.py:77
  118.8 4.9 %collective-permute-done.25 = bf16[4,480,128]{2,1,0:T(8,128)(2,1)S(1)} collective-permute-done((bf16[4,480,128]{2,1,0:T(8,128)(2,1)S(1)}, bf16[4,480,128]{2,1,0:T(8,128)(2,1)S(1)}, u32[]{:S(2)}, u32[]{:S(2)}) %collective-permute-start.25) | collective-permute-done | bytes 491552 | tf_op jit(solution)/shard_map/ppermute | solution.py:46
  123.8 1.8 collective-permute-start.31
  125.6 2.0 %collective-permute-done.24 = bf16[2,960,128]{2,1,0:T(8,128)(2,1)S(1)} collective-permute-done((bf16[2,960,128]{2,1,0:T(8,128)(2,1)S(1)}, bf16[2,960,128]{2,1,0:T(8,128)(2,1)S(1)}, u32[]{:S(2)}, u32[]{:S(2)}) %collective-permute-start.24) | collective-permute-done | bytes 491552 | tf_op jit(solution)/shard_map/ppermute | solution.py:46
  130.3 2.6 %collective-permute-start.39 = (bf16[1,960,128]{2,1,0:T(8,128)(2,1)S(1)}, bf16[1,960,128]{2,1,0:T(8,128)(2,1)S(1)}, u32[]{:S(2)}, u32[]{:S(2)}) collective-permute-start(bf16[1,960,128]{2,1,0:T(8,128)(2,1)S(1)} %get-tuple-element.265), channel_id=1, source_target_pairs={{0,16},{4,20},{8,24},{12,28},{16,0},{20,4},{24,8},{28,12},{1,17},{... | collective-permute-start | bytes 737288 | tf_op jit(solution)/shard_map/ppermute | solution.py:46
  132.9 3.6 %shard_map.230 = (bf16[256,640]{1,0:T(8,128)(2,1)S(1)}, bf16[256,640]{1,0:T(8,128)(2,1)S(1)}, bf16[512,256]{1,0:T(8,128)(2,1)S(1)}, bf16[512,256]{1,0:T(8,128)(2...) custom-call(bf16[256,640]{1,0:T(8,128)(2,1)S(1)} %get-tuple-element., ...), custom_call_target="tpu_custom_call" | custom-call | flops 1 | bytes 1 | tf_op jit(solution)/shard_map/pallas_call | solution.py:77
  139.1 5.5 %collective-permute-done.39 = bf16[1,960,128]{2,1,0:T(8,128)(2,1)S(1)} collective-permute-done((bf16[1,960,128]{2,1,0:T(8,128)(2,1)S(1)}, bf16[1,960,128]{2,1,0:T(8,128)(2,1)S(1)}, u32[]{:S(2)}, u32[]{:S(2)}) %collective-permute-start.39) | collective-permute-done | bytes 245792 | tf_op jit(solution)/shard_map/ppermute | solution.py:46
  145.1 2.7 %collective-permute-start.36 = (bf16[1,480,128]{2,1,0:T(8,128)(2,1)S(1)}, bf16[1,480,128]{2,1,0:T(8,128)(2,1)S(1)}, u32[]{:S(2)}, u32[]{:S(2)}) collective-permute-start(bf16[1,480,128]{2,1,0:T(8,128)(2,1)S(1)} %add_convert_fusion.14), channel_id=1, source_target_pairs={{0,16},{4,20},{8,24},{12,28},{16,0},{20,4},{24,8},{28,12},{1,17},{... | collective-permute-start | bytes 368648 | tf_op jit(solution)/shard_map/ppermute | solution.py:46
  149.2 12.5 %collective-permute-done.32 = bf16[4,496,128]{2,1,0:T(8,128)(2,1)S(1)} collective-permute-done((bf16[4,496,128]{2,1,0:T(8,128)(2,1)S(1)}, bf16[4,496,128]{2,1,0:T(8,128)(2,1)S(1)}, u32[]{:S(2)}, u32[]{:S(2)}) %collective-permute-start.32) | collective-permute-done | bytes 507936 | tf_op jit(solution)/shard_map/ppermute | solution.py:46
  165.1 3.1 %collective-permute-done.33 = bf16[2,496,128]{2,1,0:T(8,128)(2,1)S(1)} collective-permute-done((bf16[2,496,128]{2,1,0:T(8,128)(2,1)S(1)}, bf16[2,496,128]{2,1,0:T(8,128)(2,1)S(1)}, u32[]{:S(2)}, u32[]{:S(2)}) %collective-permute-start.33) | collective-permute-done | bytes 253984 | tf_op jit(solution)/shard_map/ppermute | solution.py:46
  168.4 7.0 %collective-permute-done.34 = bf16[1,496,128]{2,1,0:T(8,128)(2,1)S(1)} collective-permute-done((bf16[1,496,128]{2,1,0:T(8,128)(2,1)S(1)}, bf16[1,496,128]{2,1,0:T(8,128)(2,1)S(1)}, u32[]{:S(2)}, u32[]{:S(2)}) %collective-permute-start.34) | collective-permute-done | bytes 127008 | tf_op jit(solution)/shard_map/ppermute | solution.py:46
  175.5 2.1 %collective-permute-start.40 = (bf16[336,128]{1,0:T(8,128)(2,1)S(1)}, bf16[336,128]{1,0:T(8,128)(2,1)S(1)}, u32[]{:S(2)}, u32[]{:S(2)}) collective-permute-start(bf16[336,128]{1,0:T(8,128)(2,1)S(1)} %pad_maximum_fusion), channel_id=1, source_target_pairs={{0,2},{1,3},{2,0},{3,1},{4,6},{5,7},{6,4},{7,5},{8,10},{9,11},{10,... | collective-permute-start | bytes 258056 | tf_op jit(solution)/shard_map/ppermute | solution.py:46
  180.2 6.1 %collective-permute-done.38 = bf16[1,960,128]{2,1,0:T(8,128)(2,1)S(1)} collective-permute-done((bf16[1,960,128]{2,1,0:T(8,128)(2,1)S(1)}, bf16[1,960,128]{2,1,0:T(8,128)(2,1)S(1)}, u32[]{:S(2)}, u32[]{:S(2)}) %collective-permute-start.38) | collective-permute-done | bytes 245792 | tf_op jit(solution)/shard_map/ppermute | solution.py:46
  (142 shorter events, 55.8 us)
Async XLA Ops:
  0.6 7.4 %collective-permute-start = (bf16[128,640]{1,0:T(8,128)(2,1)}, bf16[128,640]{1,0:T(8,128)(2,1)S(1)}, u32[]{:S(2)}, u32[]{:S(2)}) collective-permute-start(bf16[128,640]{1,0:T(8,128)(2,1)} %param.13), channel_id=1, source_target_pairs={{0,2},{1,3},{2,0},{3,1},{4,6},{5,7},{6,4},{7,5},{8,10},{9,11},{10,... | collective-permute-start | bytes 491528 | tf_op jit(solution)/shard_map/ppermute | solution.py:46
  9.0 2.0 %collective-permute-start.1 = (bf16[256,640]{1,0:T(8,128)(2,1)S(1)}, bf16[256,640]{1,0:T(8,128)(2,1)S(1)}, u32[]{:S(2)}, u32[]{:S(2)}) collective-permute-start(bf16[256,640]{1,0:T(8,128)(2,1)S(1)} %shard_map.212.own_ref.rest_0_.refs_1_.refs_7_.refs_10_), channel_id=1, source_target_pairs={{0,1},{1,0},{2,3},{3,2},{4,5},{5,4},{6,7},{7,6},{8,9},{9,8},{10,11... | collective-permute-start | bytes 983048 | tf_op jit(solution)/shard_map/ppermute | solution.py:46
  13.5 1.8 collective-permute-start.2
  15.4 10.1 %collective-permute-start.3 = (bf16[256,640]{1,0:T(8,128)(2,1)S(1)}, bf16[256,640]{1,0:T(8,128)(2,1)S(1)}, u32[]{:S(2)}, u32[]{:S(2)}) collective-permute-start(bf16[256,640]{1,0:T(8,128)(2,1)S(1)} %add_convert_fusion.9.pair_ref), channel_id=1, source_target_pairs={{0,2},{1,3},{2,0},{3,1},{4,6},{5,7},{6,4},{7,5},{8,10},{9,11},{10,... | collective-permute-start | bytes 983048 | tf_op jit(solution)/shard_map/ppermute | solution.py:46
  25.8 1.7 collective-permute-start.4
  30.9 9.8 %collective-permute-start.6 = (bf16[256,640]{1,0:T(8,128)(2,1)S(1)}, bf16[256,640]{1,0:T(8,128)(2,1)S(1)}, u32[]{:S(2)}, u32[]{:S(2)}) collective-permute-start(bf16[256,640]{1,0:T(8,128)(2,1)S(1)} %add_convert_fusion.8.pair_ref), channel_id=1, source_target_pairs={{0,2},{1,3},{2,0},{3,1},{4,6},{5,7},{6,4},{7,5},{8,10},{9,11},{10,... | collective-permute-start | bytes 983048 | tf_op jit(solution)/shard_map/ppermute | solution.py:46
  47.0 9.8 %collective-permute-start.9 = (bf16[256,640]{1,0:T(8,128)(2,1)S(1)}, bf16[256,640]{1,0:T(8,128)(2,1)S(1)}, u32[]{:S(2)}, u32[]{:S(2)}) collective-permute-start(bf16[256,640]{1,0:T(8,128)(2,1)S(1)} %add_convert_fusion.7.pair_ref), channel_id=1, source_target_pairs={{0,2},{1,3},{2,0},{3,1},{4,6},{5,7},{6,4},{7,5},{8,10},{9,11},{10,... | collective-permute-start | bytes 983048 | tf_op jit(solution)/shard_map/ppermute | solution.py:46
  62.2 13.4 %collective-permute-start.12 = (bf16[256,640]{1,0:T(8,128)(2,1)S(1)}, bf16[256,640]{1,0:T(8,128)(2,1)S(1)}, u32[]{:S(2)}, u32[]{:S(2)}) collective-permute-start(bf16[256,640]{1,0:T(8,128)(2,1)S(1)} %add_convert_fusion.6.pair_ref), channel_id=1, source_target_pairs={{0,2},{1,3},{2,0},{3,1},{4,6},{5,7},{6,4},{7,5},{8,10},{9,11},{10,... | collective-permute-start | bytes 983048 | tf_op jit(solution)/shard_map/ppermute | solution.py:46
  64.1 11.5 %collective-permute-start.13 = (bf16[128,640]{1,0:T(8,128)(2,1)S(1)}, bf16[128,640]{1,0:T(8,128)(2,1)S(1)}, u32[]{:S(2)}, u32[]{:S(2)}) collective-permute-start(bf16[128,640]{1,0:T(8,128)(2,1)S(1)} %copy-done.10), channel_id=1, source_target_pairs={{0,2},{1,3},{2,0},{3,1},{4,6},{5,7},{6,4},{7,5},{8,10},{9,11},{10,... | collective-permute-start | bytes 491528 | tf_op jit(solution)/shard_map/ppermute | solution.py:46
  82.1 9.8 %collective-permute-start.16 = (bf16[256,640]{1,0:T(8,128)(2,1)S(1)}, bf16[256,640]{1,0:T(8,128)(2,1)S(1)}, u32[]{:S(2)}, u32[]{:S(2)}) collective-permute-start(bf16[256,640]{1,0:T(8,128)(2,1)S(1)} %add_convert_fusion.5.pair_ref), channel_id=1, source_target_pairs={{0,2},{1,3},{2,0},{3,1},{4,6},{5,7},{6,4},{7,5},{8,10},{9,11},{10,... | collective-permute-start | bytes 983048 | tf_op jit(solution)/shard_map/ppermute | solution.py:46
  85.3 23.6 %collective-permute-start.20 = (bf16[4,960,128]{2,1,0:T(8,128)(2,1)S(1)}, bf16[4,960,128]{2,1,0:T(8,128)(2,1)S(1)}, u32[]{:S(2)}, u32[]{:S(2)}) collective-permute-start(bf16[4,960,128]{2,1,0:T(8,128)(2,1)S(1)} %get-tuple-element.186), channel_id=1, source_target_pairs={{0,4},{4,0},{8,12},{12,8},{16,20},{20,16},{24,28},{28,24},{1,5},{5... | collective-permute-start | bytes 2949128 | tf_op jit(solution)/shard_map/ppermute | solution.py:46
  97.9 3.4 %collective-permute-start.19 = (bf16[512,256]{1,0:T(8,128)(2,1)S(1)}, bf16[512,256]{1,0:T(8,128)(2,1)S(1)}, u32[]{:S(2)}, u32[]{:S(2)}) collective-permute-start(bf16[512,256]{1,0:T(8,128)(2,1)S(1)} %get-tuple-element.180), channel_id=1, source_target_pairs={{0,1},{1,0},{2,3},{3,2},{4,5},{5,4},{6,7},{7,6},{8,9},{9,8},{10,11... | collective-permute-start | bytes 786440 | tf_op jit(solution)/shard_map/ppermute | solution.py:46
  99.5 9.8 %collective-permute-start.21 = (bf16[256,640]{1,0:T(8,128)(2,1)S(1)}, bf16[256,640]{1,0:T(8,128)(2,1)S(1)}, u32[]{:S(2)}, u32[]{:S(2)}) collective-permute-start(bf16[256,640]{1,0:T(8,128)(2,1)S(1)} %add_convert_fusion.4.pair_ref), channel_id=1, source_target_pairs={{0,2},{1,3},{2,0},{3,1},{4,6},{5,7},{6,4},{7,5},{8,10},{9,11},{10,... | collective-permute-start | bytes 983048 | tf_op jit(solution)/shard_map/ppermute | solution.py:46
  110.0 1.9 %collective-permute-start.22 = (bf16[256,640]{1,0:T(8,128)(2,1)S(1)}, bf16[256,640]{1,0:T(8,128)(2,1)S(1)}, u32[]{:S(2)}, u32[]{:S(2)}) collective-permute-start(bf16[256,640]{1,0:T(8,128)(2,1)S(1)} %get-tuple-element.192.own_ref.refs_8_), channel_id=1, source_target_pairs={{0,1},{1,0},{2,3},{3,2},{4,5},{5,4},{6,7},{7,6},{8,9},{9,8},{10,11... | collective-permute-start | bytes 983048 | tf_op jit(solution)/shard_map/ppermute | solution.py:46
  110.1 13.6 %collective-permute-start.25 = (bf16[4,480,128]{2,1,0:T(8,128)(2,1)S(1)}, bf16[4,480,128]{2,1,0:T(8,128)(2,1)S(1)}, u32[]{:S(2)}, u32[]{:S(2)}) collective-permute-start(bf16[4,480,128]{2,1,0:T(8,128)(2,1)S(1)} %get-tuple-element.205), channel_id=1, source_target_pairs={{0,4},{4,0},{8,12},{12,8},{16,20},{20,16},{24,28},{28,24},{1,5},{5... | collective-permute-start | bytes 1474568 | tf_op jit(solution)/shard_map/ppermute | solution.py:46
  113.9 1.9 %collective-permute-start.23 = (bf16[256,640]{1,0:T(8,128)(2,1)S(1)}, bf16[256,640]{1,0:T(8,128)(2,1)S(1)}, u32[]{:S(2)}, u32[]{:S(2)}) collective-permute-start(bf16[256,640]{1,0:T(8,128)(2,1)S(1)} %get-tuple-element.196), channel_id=1, source_target_pairs={{0,1},{1,0},{2,3},{3,2},{4,5},{5,4},{6,7},{7,6},{8,9},{9,8},{10,11... | collective-permute-start | bytes 983048 | tf_op jit(solution)/shard_map/ppermute | solution.py:46
  114.1 13.5 %collective-permute-start.24 = (bf16[2,960,128]{2,1,0:T(8,128)(2,1)S(1)}, bf16[2,960,128]{2,1,0:T(8,128)(2,1)S(1)}, u32[]{:S(2)}, u32[]{:S(2)}) collective-permute-start(bf16[2,960,128]{2,1,0:T(8,128)(2,1)S(1)} %get-tuple-element.263), channel_id=1, source_target_pairs={{0,8},{4,12},{8,0},{12,4},{16,24},{20,28},{24,16},{28,20},{1,9},{5... | collective-permute-start | bytes 1474568 | tf_op jit(solution)/shard_map/ppermute | solution.py:46
  115.9 11.9 %collective-permute-start.26 = (bf16[256,640]{1,0:T(8,128)(2,1)S(1)}, bf16[256,640]{1,0:T(8,128)(2,1)S(1)}, u32[]{:S(2)}, u32[]{:S(2)}) collective-permute-start(bf16[256,640]{1,0:T(8,128)(2,1)S(1)} %add_convert_fusion.3.pair_ref), channel_id=1, source_target_pairs={{0,2},{1,3},{2,0},{3,1},{4,6},{5,7},{6,4},{7,5},{8,10},{9,11},{10,... | collective-permute-start | bytes 983048 | tf_op jit(solution)/shard_map/ppermute | solution.py:46
  123.8 24.0 %collective-permute-start.31 = (bf16[4,960,128]{2,1,0:T(8,128)(2,1)S(1)}, bf16[4,960,128]{2,1,0:T(8,128)(2,1)S(1)}, u32[]{:S(2)}, u32[]{:S(2)}) collective-permute-start(bf16[4,960,128]{2,1,0:T(8,128)(2,1)S(1)} %get-tuple-element.238), channel_id=1, source_target_pairs={{0,4},{4,0},{8,12},{12,8},{16,20},{20,16},{24,28},{28,24},{1,5},{5... | collective-permute-start | bytes 2949128 | tf_op jit(solution)/shard_map/ppermute | solution.py:46
  128.6 4.4 %collective-permute-start.27 = (bf16[256,640]{1,0:T(8,128)(2,1)S(1)}, bf16[256,640]{1,0:T(8,128)(2,1)S(1)}, u32[]{:S(2)}, u32[]{:S(2)}) collective-permute-start(bf16[256,640]{1,0:T(8,128)(2,1)S(1)} %get-tuple-element.211.own_ref.refs_5_), channel_id=1, source_target_pairs={{0,1},{1,0},{2,3},{3,2},{4,5},{5,4},{6,7},{7,6},{8,9},{9,8},{10,11... | collective-permute-start | bytes 983048 | tf_op jit(solution)/shard_map/ppermute | solution.py:46
  128.7 15.9 %collective-permute-start.35 = (bf16[2,480,128]{2,1,0:T(8,128)(2,1)S(1)}, bf16[2,480,128]{2,1,0:T(8,128)(2,1)S(1)}, u32[]{:S(2)}, u32[]{:S(2)}) collective-permute-start(bf16[2,480,128]{2,1,0:T(8,128)(2,1)S(1)} %get-tuple-element.269), channel_id=1, source_target_pairs={{0,8},{4,12},{8,0},{12,4},{16,24},{20,28},{24,16},{28,20},{1,9},{5... | collective-permute-start | bytes 737288 | tf_op jit(solution)/shard_map/ppermute | solution.py:46
  130.3 14.3 %collective-permute-start.39 = (bf16[1,960,128]{2,1,0:T(8,128)(2,1)S(1)}, bf16[1,960,128]{2,1,0:T(8,128)(2,1)S(1)}, u32[]{:S(2)}, u32[]{:S(2)}) collective-permute-start(bf16[1,960,128]{2,1,0:T(8,128)(2,1)S(1)} %get-tuple-element.265), channel_id=1, source_target_pairs={{0,16},{4,20},{8,24},{12,28},{16,0},{20,4},{24,8},{28,12},{1,17},{... | collective-permute-start | bytes 737288 | tf_op jit(solution)/shard_map/ppermute | solution.py:46
  136.6 26.8 %collective-permute-start.28 = (bf16[256,640]{1,0:T(8,128)(2,1)S(1)}, bf16[256,640]{1,0:T(8,128)(2,1)S(1)}, u32[]{:S(2)}, u32[]{:S(2)}) collective-permute-start(bf16[256,640]{1,0:T(8,128)(2,1)S(1)} %get-tuple-element.219), channel_id=1, source_target_pairs={{0,1},{1,0},{2,3},{3,2},{4,5},{5,4},{6,7},{7,6},{8,9},{9,8},{10,11... | collective-permute-start | bytes 983048 | tf_op jit(solution)/shard_map/ppermute | solution.py:46
  144.6 17.1 %collective-permute-start.32 = (bf16[4,496,128]{2,1,0:T(8,128)(2,1)S(1)}, bf16[4,496,128]{2,1,0:T(8,128)(2,1)S(1)}, u32[]{:S(2)}, u32[]{:S(2)}) collective-permute-start(bf16[4,496,128]{2,1,0:T(8,128)(2,1)S(1)} %get-tuple-element.241), channel_id=1, source_target_pairs={{0,8},{4,12},{8,0},{12,4},{16,24},{20,28},{24,16},{28,20},{1,9},{5... | collective-permute-start | bytes 1523720 | tf_op jit(solution)/shard_map/ppermute | solution.py:46
  145.1 20.0 %collective-permute-start.36 = (bf16[1,480,128]{2,1,0:T(8,128)(2,1)S(1)}, bf16[1,480,128]{2,1,0:T(8,128)(2,1)S(1)}, u32[]{:S(2)}, u32[]{:S(2)}) collective-permute-start(bf16[1,480,128]{2,1,0:T(8,128)(2,1)S(1)} %add_convert_fusion.14), channel_id=1, source_target_pairs={{0,16},{4,20},{8,24},{12,28},{16,0},{20,4},{24,8},{28,12},{1,17},{... | collective-permute-start | bytes 368648 | tf_op jit(solution)/shard_map/ppermute | solution.py:46
  148.0 29.7 %collective-permute-start.37 = (bf16[2,960,128]{2,1,0:T(8,128)(2,1)S(1)}, bf16[2,960,128]{2,1,0:T(8,128)(2,1)S(1)}, u32[]{:S(2)}, u32[]{:S(2)}) collective-permute-start(bf16[2,960,128]{2,1,0:T(8,128)(2,1)S(1)} %get-tuple-element.261), channel_id=1, source_target_pairs={{0,8},{4,12},{8,0},{12,4},{16,24},{20,28},{24,16},{28,20},{1,9},{5... | collective-permute-start | bytes 1474568 | tf_op jit(solution)/shard_map/ppermute | solution.py:46
  161.8 6.3 %collective-permute-start.33 = (bf16[2,496,128]{2,1,0:T(8,128)(2,1)S(1)}, bf16[2,496,128]{2,1,0:T(8,128)(2,1)S(1)}, u32[]{:S(2)}, u32[]{:S(2)}) collective-permute-start(bf16[2,496,128]{2,1,0:T(8,128)(2,1)S(1)} %get-tuple-element.267), channel_id=1, source_target_pairs={{0,4},{4,0},{8,12},{12,8},{16,20},{20,16},{24,28},{28,24},{1,5},{5... | collective-permute-start | bytes 761864 | tf_op jit(solution)/shard_map/ppermute | solution.py:46
  163.5 14.4 %collective-permute-start.29 = (bf16[256,640]{1,0:T(8,128)(2,1)S(1)}, bf16[256,640]{1,0:T(8,128)(2,1)S(1)}, u32[]{:S(2)}, u32[]{:S(2)}) collective-permute-start(bf16[256,640]{1,0:T(8,128)(2,1)S(1)} %add_convert_fusion.2.pair_ref), channel_id=1, source_target_pairs={{0,2},{1,3},{2,0},{3,1},{4,6},{5,7},{6,4},{7,5},{8,10},{9,11},{10,... | collective-permute-start | bytes 983048 | tf_op jit(solution)/shard_map/ppermute | solution.py:46
  168.2 7.2 %collective-permute-start.34 = (bf16[1,496,128]{2,1,0:T(8,128)(2,1)S(1)}, bf16[1,496,128]{2,1,0:T(8,128)(2,1)S(1)}, u32[]{:S(2)}, u32[]{:S(2)}) collective-permute-start(bf16[1,496,128]{2,1,0:T(8,128)(2,1)S(1)} %fusion), channel_id=1, source_target_pairs={{0,16},{4,20},{8,24},{12,28},{16,0},{20,4},{24,8},{28,12},{1,17},{... | collective-permute-start | bytes 380936 | tf_op jit(solution)/shard_map/ppermute | solution.py:46
  175.5 4.6 %collective-permute-start.40 = (bf16[336,128]{1,0:T(8,128)(2,1)S(1)}, bf16[336,128]{1,0:T(8,128)(2,1)S(1)}, u32[]{:S(2)}, u32[]{:S(2)}) collective-permute-start(bf16[336,128]{1,0:T(8,128)(2,1)S(1)} %pad_maximum_fusion), channel_id=1, source_target_pairs={{0,2},{1,3},{2,0},{3,1},{4,6},{5,7},{6,4},{7,5},{8,10},{9,11},{10,... | collective-permute-start | bytes 258056 | tf_op jit(solution)/shard_map/ppermute | solution.py:46
  177.7 8.6 %collective-permute-start.38 = (bf16[1,960,128]{2,1,0:T(8,128)(2,1)S(1)}, bf16[1,960,128]{2,1,0:T(8,128)(2,1)S(1)}, u32[]{:S(2)}, u32[]{:S(2)}) collective-permute-start(bf16[1,960,128]{2,1,0:T(8,128)(2,1)S(1)} %add_convert_fusion.12), channel_id=1, source_target_pairs={{0,16},{4,20},{8,24},{12,28},{16,0},{20,4},{24,8},{28,12},{1,17},{... | collective-permute-start | bytes 737288 | tf_op jit(solution)/shard_map/ppermute | solution.py:46
  180.1 6.2 %collective-permute-start.41 = (bf16[336,128]{1,0:T(8,128)(2,1)S(1)}, bf16[336,128]{1,0:T(8,128)(2,1)S(1)}, u32[]{:S(2)}, u32[]{:S(2)}) collective-permute-start(bf16[336,128]{1,0:T(8,128)(2,1)S(1)} %add_convert_fusion.15.refs_4_), channel_id=1, source_target_pairs={{0,1},{1,0},{2,3},{3,2},{4,5},{5,4},{6,7},{7,6},{8,9},{9,8},{10,11... | collective-permute-start | bytes 258056 | tf_op jit(solution)/shard_map/ppermute | solution.py:46
  (21 other events, 113.7 us)

commit v4 on v3

--- a/solution.py
+++ b/solution.py
@@ -9,6 +9,7 @@
 SEQ_LEN = 512
 LANES = 128
 VMEM_BYTES = 12 << 20
+FORWARD_COST = (1_000_000_000, 4_000_000)
 GAIN_ROWS = 16
 
 epsilon = 1e-06
@@ -34,35 +35,17 @@
     return lax.dot_general(left, right, (((1,), (1,)), ((), ())), preferred_element_type=F32)
 
 
-def angles(place, width, theta):
-    half_width = width // 2
-    frequency = theta ** (-(2.0 * jnp.arange(half_width, dtype=F32)) / width)
-    phases = place.astype(F32)[:, None] * frequency[None, :]
-    return (jnp.cos(phases), jnp.sin(phases))
-
-
 def swap(array, axis, bit):
     size = lax.axis_size(axis)
     return lax.ppermute(array, axis, [(i, i ^ bit) for i in range(size)])
 
 
-def relative_order(array, quarter):
-    parts = array.reshape((4, -1) + array.shape[1:])
-    return jnp.concatenate(
-        [lax.dynamic_index_in_dim(parts, quarter ^ bit, 0, False) for bit in (0, 2, 1, 3)]
-    )
-
-
-def two_quarters(array):
-    return jnp.concatenate([array, swap(array, "tensor", 2)])
-
-
 def summed_pair(kept, sent):
     pair = (kept.astype(F32) + swap(sent, "tensor", 1).astype(F32)).astype(BF16)
     return (pair, swap(pair, "tensor", 2))
 
 
-def kernel_call(body, outs, args, layers=None, scratch=()):
+def kernel_call(body, outs, args, layers=None, scratch=(), cost=(1, 1)):
     layers = layers or {}
 
     def spec(place, arg):
@@ -82,7 +65,9 @@
         out_shape=list(outs),
         scratch_shapes=list(scratch),
         compiler_params=pltpu.CompilerParams(vmem_limit_bytes=VMEM_BYTES),
-        cost_estimate=pl.CostEstimate(flops=1, transcendentals=0, bytes_accessed=1),
+        cost_estimate=pl.CostEstimate(
+            flops=cost[0], transcendentals=0, bytes_accessed=cost[1]
+        ),
     )(*args)
 
 
@@ -123,13 +108,54 @@
     return pair_ref[...].astype(F32) + other.astype(F32)
 
 
-def first_norm(stream, gains, layer):
-    def body(stream_ref, gains_ref, normed_ref):
-        normed_ref[...] = norm_forward(
-            stream_ref[...].astype(F32), gains_ref[0, 0:1, :]
-        ).astype(BF16)
-
-    return kernel_call(body, [shape(*stream.shape, BF16)], (stream, gains), {1: layer})[0]
+def first_norm(own, beside, gains, layer):
+    def body(own_ref, beside_ref, gains_ref, stream_ref, normed_ref):
+        stream = jnp.concatenate([own_ref[...], beside_ref[...]], axis=0)
+        stream_ref[...] = stream
+        normed_ref[...] = norm_forward(stream.astype(F32), gains_ref[0, 0:1, :]).astype(BF16)
+
+    rows, columns = own.shape
+    return kernel_call(
+        body, [shape(2 * rows, columns, BF16)] * 2, (own, beside, gains), {2: layer}, cost=FORWARD_COST)
+
+
+def ordered_rows(segments, positions, quarter):
+    size = segments.shape[0] // 4
+
+    def body(seg_ref, pos_ref, quarter_ref, across_ref, down_ref):
+        lanes = lax.broadcasted_iota(jnp.int32, (1, size), 1)
+        lines = [[], [], []]
+        for bit in (0, 2, 1, 3):
+            index = jnp.bitwise_xor(quarter_ref[0], bit)
+            lines[0].append(seg_ref[pl.ds(index, 1), :])
+            lines[1].append(lanes + index * size)
+            lines[2].append(pos_ref[pl.ds(index, 1), :])
+        rows = [jnp.concatenate(line, axis=1).astype(F32) for line in lines]
+        across = jnp.concatenate(rows + [jnp.zeros((5, 4 * size), F32)], axis=0)
+        across_ref[...] = across
+        down_ref[...] = across.T
+
+    return kernel_call(
+        body,
+        [shape(8, 4 * size, F32), shape(4 * size, 8, F32)],
+        (segments.reshape(4, size), positions.reshape(4, size), quarter), cost=FORWARD_COST)
+
+
+def angles(down, width, theta):
+    half_width = width // 2
+    frequency = theta ** (-(2.0 * jnp.arange(half_width, dtype=F32)) / width)
+
+    def body(down_ref, frequency_ref, cosine_ref, sine_ref):
+        phases = down_ref[:, 2:3] * frequency_ref[...]
+        cosine_ref[...] = jnp.cos(phases)
+        sine_ref[...] = jnp.sin(phases)
+
+    return tuple(
+        kernel_call(
+            body,
+            [shape(down.shape[0], half_width, F32)] * 2,
+            (down, frequency.reshape(1, half_width)), cost=FORWARD_COST)
+    )
 
 
 def after_attention(pair, other, stream, gains, layer):
@@ -145,8 +171,7 @@
         body,
         [shape(*size, F32), shape(*size, F32), shape(*size, BF16)],
         (pair, other, stream, gains),
-        {3: layer},
-    )
+        {3: layer}, cost=FORWARD_COST)
 
 
 def between_layers(pair, other, middle, gains, layer):
@@ -162,8 +187,7 @@
         body,
         [shape(*size, F32), shape(*size, F32), shape(*size, BF16)],
         (pair, other, middle, gains, gains),
-        {3: layer, 4: layer + 1},
-    )
+        {3: layer, 4: layer + 1}, cost=FORWARD_COST)
 
 
 def turn_around(pair, other, middle, cotangent, gains, layer):
@@ -306,8 +330,7 @@
         + [shape(length, head_width, BF16)] * 4
         + [shape(length, 1, F32)],
         (own, received, w_query, w_key, w_value, w_out, qk_gains, cosine, sine, down, across),
-        {place: layer for place in (2, 3, 4, 5, 6)},
-    )
+        {place: layer for place in (2, 3, 4, 5, 6)}, cost=FORWARD_COST)
 
 
 def feed_forward(own, received, weights, layer):
@@ -335,8 +358,7 @@
         + [shape(length, hidden_width, F32)] * 2
         + [shape(length, hidden_width, BF16)],
         (own, received, w_gate, w_up, w_down),
-        {2: layer, 3: layer, 4: layer},
-    )
+        {2: layer, 3: layer, 4: layer}, cost=FORWARD_COST)
 
 
 def feed_forward_back(own, received, weights, gate, up, layer):
@@ -694,18 +716,18 @@
         (hidden_in, segments, positions, quarter, me, side)
     )
     bits = [1 << place for place in range(pieces.bit_length() - 1)]
-    turned_bits = bits[1::-1] + bits[2:]
-    seg_rows = relative_order(segments, quarter)
-    pos_rows = relative_order(positions, quarter)
-    places = relative_order(jnp.arange(SEQ_LEN, dtype=jnp.int32), quarter)
-    down = jnp.stack([seg_rows, places], axis=1)
-    across = jnp.stack([seg_rows, places], axis=0)
+    mlp1_bits = [bits[p] for p in [0, 1, 2]] + bits[3:] if len(bits) > 2 else bits
+    attn1_bits = [bits[p] for p in [0, 1, 2]] + bits[3:] if len(bits) > 2 else bits
+    mlp0_bits = [bits[p] for p in [0, 1, 2]] + bits[3:] if len(bits) > 2 else bits
+    attn0_bits = [bits[p] for p in [1, 0, 2]] + bits[3:] if len(bits) > 2 else bits
+    across, down = ordered_rows(segments, positions, quarter.reshape(1))
     attn_weights = (w_query, w_key, w_value, w_out, qk_gains)
     mlp_weights = (w_gate, w_up, w_down)
-    tables = [angles(pos_rows, head_width, theta) + (down, across) for theta in thetas]
-
-    stream = two_quarters(hidden_in)
-    low = first_norm(stream, norm_gains, 0)
+    tables = [angles(down, head_width, thetas[0]) + (down, across), None]
+
+    beside = swap(hidden_in, "tensor", 2)
+    (beside,) = after(tables[0], beside)
+    stream, low = first_norm(hidden_in, beside, norm_gains, 0)
     saved = []
     for layer in range(2):
         received = swap(low, "tensor", 1)
@@ -714,6 +736,10 @@
         )
         attn_in = (low, received)
         pair, other = summed_pair(kept, sent)
+        if layer == 0:
+            (rows,) = after(pair, down)
+            tables[1] = angles(rows, head_width, thetas[1]) + (down, across)
+            (other,) = after(tables[1], other)
         attn_sum, middle, low = after_attention(pair, other, stream, norm_gains, layer)
         received = swap(low, "tensor", 1)
         kept, sent, *kept_mlp = feed_forward(low, received, mlp_weights, layer)
@@ -723,7 +749,7 @@
         if layer == 0:
             mlp_sum, stream, low = between_layers(pair, other, middle, norm_gains, layer)
 
-    grad_stream = two_quarters(cotangent)
+    grad_stream = jnp.concatenate([cotangent, swap(cotangent, "tensor", 2)])
     output, low, gain3 = turn_around(pair, other, middle, grad_stream, norm_gains, 1)
     sums = {}
     gain_rows = [None, None]
@@ -736,18 +762,19 @@
             low, received, mlp_weights, gate, up, layer
         )
         mlp_out = (low, received)
+        if layer == 0:
+            sums["attn1"].step(gate_low)
+            (kept,) = after(sums["attn1"].kept, kept)
         pair, other = summed_pair(kept, sent)
         gate_low, up_low = after(pair, gate_low, up_low)
         gate_term, up_term = (mlp_in, (gate_low,)), (mlp_in, (up_low,))
         down_term = ((hidden,), mlp_out)
         if layer == 1:
-            sums["mlp1"] = Halving([gate_term, up_term, down_term], me, bits)
+            sums["mlp1"] = Halving([gate_term, up_term, down_term], me, mlp1_bits)
             (other,) = after(sums["mlp1"].kept, other)
         else:
-            sums["mlp0"] = Halving([gate_term, up_term, down_term], me, bits)
-            made = sums["mlp0"].kept
-            sums["mlp1"].step(made)
-            sums["attn1"].step(made)
+            sums["mlp0"] = Halving([gate_term, up_term, down_term], me, mlp0_bits)
+            sums["mlp1"].step((sums["mlp0"].kept, other))
             (other,) = after([s.kept for s in sums.values()], other)
         grad_middle, low, gain1, gain2 = back_to_attention(
             pair, other, middle, attn_sum, grad_stream, norm_gains, layer
@@ -772,7 +799,7 @@
         query_term, out_term = (attn_in, (grad_q,)), ((attended,), (low, received))
         gain_rows[layer] = [None, gain1 * 0.5, gain2 * 0.5, gain3 * 0.5, gain_q, gain_k]
         if layer == 1:
-            sums["attn1"] = Halving([query_term, out_term, shared_term], me, bits)
+            sums["attn1"] = Halving([query_term, out_term, shared_term], me, attn1_bits)
             sums["mlp1"].step(sums["attn1"].kept)
             (other,) = after([s.kept for s in sums.values()], other)
             grad_stream, low, gain0, gain3 = back_between(
@@ -784,17 +811,19 @@
             sums["attn0"] = Halving(
                 [query_term, out_term, shared_term],
                 me,
-                turned_bits,
+                attn0_bits,
                 gain_rows[0] + gain_rows[1],
             )
-            for name in ("mlp1", "attn1", "mlp0"):
-                sums[name].step(sums["attn0"].kept)
             grad_input = back_to_input(pair, other, stream, grad_middle, norm_gains, layer)
 
+    sums["mlp1"].step(sums["attn0"].kept)
+    sums["attn1"].step(sums["attn0"].kept)
+    sums["mlp0"].step(sums["attn0"].kept)
     sums["attn0"].step(sums["mlp0"].kept)
     sums["attn0"].step()
     sums["mlp0"].step(sums["attn0"].kept)
     sums["attn0"].finish()
+
     tall = {
         "q": w_query.shape[1] // pieces,
         "o": w_out.shape[1] // pieces,

time: 188 us -> 187 us (level)
  waiting for transfers between devices: 109 us -> 115 us
  starting transfers between devices: 40 us -> 34.3 us
  local copies, waits for them, and re-layouts: 3.77 us -> 1.47 us
  Pallas kernels: 30.3 us -> 32.3 us
  other arithmetic: 3.82 us -> 1.91 us
    ppermute x42, waiting for transfers between devices: 109 us -> 115 us  [swap(): return lax.ppermute(array, axis, [(i, i ^ bit) for i in range(size)])]
    ppermute x42, starting transfers between devices: 40 us -> 34.3 us  [swap(): return lax.ppermute(array, axis, [(i, i ^ bit) for i in range(size)])]
    pallas_call x18 -> x21, Pallas kernels: 25.5 us -> 27.5 us  [kernel_call(): pl.pallas_call(body, grid=(1,), in_specs=[spec(place, arg) for place, arg...]
    sin x1 -> x0, other arithmetic: 1.89 us -> none  [angles(): return (jnp.cos(phases), jnp.sin(phases))]
  transfers between devices with their start and end apart: 42 -> 42, of which waited for: 28 -> 30; matrix products, arithmetic and copies ran while one was open for 3% -> 1% of each run, Pallas kernels for 9% -> 10%
where the time goes in v4:
time: 187 us
  waiting for transfers between devices  115 us (61%)
  starting transfers between devices  34.3 us (18%)
  Pallas kernels  32.3 us (17%)
  other arithmetic  1.91 us (1%)
    ppermute x42, waiting for transfers between devices, swap(): return lax.ppermute(array, axis, [(i, i ^ bit) for i in range(size)])  115 us
    ppermute x42, starting transfers between devices, swap(): return lax.ppermute(array, axis, [(i, i ^ bit) for i in range(size)])  34.3 us
    pallas_call x21, Pallas kernels, kernel_call(): pl.pallas_call(body, grid=(1,), in_specs=[spec(place, arg) for place, arg...  27.5 us
    pallas_call x4, Pallas kernels, gradient_blocks(): pl.pallas_call(body, grid=(1,), in_specs=specs, out_specs=[pl.BlockSpec(o...  4.79 us
  transfers between devices with their start and end apart: 42, of which 30 were waited for; matrix products, arithmetic and copies ran while one was open for 1% of the time, Pallas kernels for 10%

profile of v4, /device:TPU:0, one launch (start us, length us, event | category | flops | bytes accessed | tf_op | source)
XLA Modules:
  0.0 186.5 jit_solution(17855536639514571206)
XLA Ops:
  0.6 3.0 %collective-permute-start = (bf16[128,640]{1,0:T(8,128)(2,1)}, bf16[128,640]{1,0:T(8,128)(2,1)S(1)}, u32[]{:S(2)}, u32[]{:S(2)}) collective-permute-start(bf16[128,640]{1,0:T(8,128)(2,1)} %own_ref), channel_id=1, source_target_pairs={{0,2},{1,3},{2,0},{3,1},{4,6},{5,7},{6,4},{7,5},{8,10},{9,11},{10,... | collective-permute-start | bytes 491528 | tf_op jit(solution)/shard_map/ppermute | solution.py:40
  6.2 1.9 %collective-permute-done.beside_ref = bf16[128,640]{1,0:T(8,128)(2,1)S(1)} collective-permute-done((bf16[128,640]{1,0:T(8,128)(2,1)}, bf16[128,640]{1,0:T(8,128)(2,1)S(1)}, u32[]{:S(2)}, u32[]{:S(2)}) %collective-permute-start) | collective-permute-done | bytes 163872 | tf_op jit(solution)/shard_map/ppermute | solution.py:40
  10.1 2.5 %shard_map.215 = (bf16[256,640]{1,0:T(8,128)(2,1)S(1)}, bf16[256,640]{1,0:T(8,128)(2,1)S(1)}, f32[512,256]{1,0:T(8,128)S(1)}, f32[512,256]{1,0:T(8,128)S(1)}, bf...) custom-call(bf16[256,640]{1,0:T(8,128)(2,1)S(1)} %get-tuple-element., ...), custom_call_target="tpu_custom_call" | custom-call | flops 1000000000 | bytes 4000000 | tf_op jit(solution)/shard_map/pallas_call | solution.py:60
  14.3 1.8 collective-permute-start.3
  17.1 7.0 %collective-permute-done.3.other_ref = bf16[256,640]{1,0:T(8,128)(2,1)S(1)} collective-permute-done((bf16[256,640]{1,0:T(8,128)(2,1)S(1)}, bf16[256,640]{1,0:T(8,128)(2,1)S(1)}, u32[]{:S(2)}, u32[]{:S(2)}) %collective-permute-start.3) | collective-permute-done | bytes 327712 | tf_op jit(solution)/shard_map/ppermute | solution.py:40
  29.5 1.8 collective-permute-start.6
  31.3 8.0 %collective-permute-done.6.other_ref = bf16[256,640]{1,0:T(8,128)(2,1)S(1)} collective-permute-done((bf16[256,640]{1,0:T(8,128)(2,1)S(1)}, bf16[256,640]{1,0:T(8,128)(2,1)S(1)}, u32[]{:S(2)}, u32[]{:S(2)}) %collective-permute-start.6) | collective-permute-done | bytes 327712 | tf_op jit(solution)/shard_map/ppermute | solution.py:40
  41.4 2.4 %shard_map.220 = (bf16[256,640]{1,0:T(8,128)(2,1)S(1)}, bf16[256,640]{1,0:T(8,128)(2,1)S(1)}, f32[512,256]{1,0:T(8,128)S(1)}, f32[512,256]{1,0:T(8,128)S(1)}, bf...) custom-call(bf16[256,640]{1,0:T(8,128)(2,1)S(1)} %get-tuple-element., ...), custom_call_target="tpu_custom_call" | custom-call | flops 1000000000 | bytes 4000000 | tf_op jit(solution)/shard_map/pallas_call | solution.py:60
  45.6 1.8 collective-permute-start.9
  47.4 8.0 %collective-permute-done.9.other_ref = bf16[256,640]{1,0:T(8,128)(2,1)S(1)} collective-permute-done((bf16[256,640]{1,0:T(8,128)(2,1)S(1)}, bf16[256,640]{1,0:T(8,128)(2,1)S(1)}, u32[]{:S(2)}, u32[]{:S(2)}) %collective-permute-start.9) | collective-permute-done | bytes 327712 | tf_op jit(solution)/shard_map/ppermute | solution.py:40
  60.8 1.8 collective-permute-start.12
  63.0 11.2 %collective-permute-done.13 = bf16[128,640]{1,0:T(8,128)(2,1)S(1)} collective-permute-done((bf16[128,640]{1,0:T(8,128)(2,1)S(1)}, bf16[128,640]{1,0:T(8,128)(2,1)S(1)}, u32[]{:S(2)}, u32[]{:S(2)}) %collective-permute-start.13) | collective-permute-done | bytes 163872 | tf_op jit(solution)/shard_map/ppermute | solution.py:40
  76.8 2.0 %shard_map.224 = (bf16[256,640]{1,0:T(8,128)(2,1)S(1)}, bf16[256,640]{1,0:T(8,128)(2,1)S(1)}, bf16[512,512]{1,0:T(8,128)(2,1)S(1)}, bf16[512,512]{1,0:T(8,128)(2,1)S(1)}) custom-call(bf16[256,640]{1,0:T(8,128)(2,1)S(1)} %get-tuple-element.177.own_ref.refs_8_, bf16[256,640]{1,0:T(8,128)(2,1)S(1)} %collective-permute-done.14.received_ref.refs_9_, ...), custom_call_target="tpu_custom_call" | custom-call | flops 1 | bytes 1 | tf_op jit(solution)/shard_map/pallas_call | solution.py:60
  80.7 1.8 collective-permute-start.16
  85.5 5.0 %collective-permute-done.16.other_ref = bf16[256,640]{1,0:T(8,128)(2,1)S(1)} collective-permute-done((bf16[256,640]{1,0:T(8,128)(2,1)S(1)}, bf16[256,640]{1,0:T(8,128)(2,1)S(1)}, u32[]{:S(2)}, u32[]{:S(2)}) %collective-permute-start.16) | collective-permute-done | bytes 327712 | tf_op jit(solution)/shard_map/ppermute | solution.py:40
  92.9 3.3 %shard_map.227 = (bf16[256,640]{1,0:T(8,128)(2,1)S(1)}, bf16[256,640]{1,0:T(8,128)(2,1)S(1)}, bf16[512,256]{1,0:T(8,128)(2,1)S(1)}, bf16[512,256]{1,0:T(8,128)(2...) custom-call(bf16[256,640]{1,0:T(8,128)(2,1)S(1)} %get-tuple-element.191.own_ref.refs_5_, ...), custom_call_target="tpu_custom_call" | custom-call | flops 1 | bytes 1 | tf_op jit(solution)/shard_map/pallas_call | solution.py:60
  98.0 1.8 collective-permute-start.21
  102.4 6.2 %collective-permute-done.20 = bf16[4,960,128]{2,1,0:T(8,128)(2,1)S(1)} collective-permute-done((bf16[4,960,128]{2,1,0:T(8,128)(2,1)S(1)}, bf16[4,960,128]{2,1,0:T(8,128)(2,1)S(1)}, u32[]{:S(2)}, u32[]{:S(2)}) %collective-permute-start.20) | collective-permute-done | bytes 983072 | tf_op jit(solution)/shard_map/ppermute | solution.py:40
  111.3 1.8 shard_map.230
  114.9 3.1 %collective-permute-done.23 = bf16[4,480,128]{2,1,0:T(8,128)(2,1)S(1)} collective-permute-done((bf16[4,480,128]{2,1,0:T(8,128)(2,1)S(1)}, bf16[4,480,128]{2,1,0:T(8,128)(2,1)S(1)}, u32[]{:S(2)}, u32[]{:S(2)}) %collective-permute-start.23) | collective-permute-done | bytes 491552 | tf_op jit(solution)/shard_map/ppermute | solution.py:40
  120.0 1.8 collective-permute-start.31
  121.8 5.0 %collective-permute-done.26 = bf16[2,960,128]{2,1,0:T(8,128)(2,1)S(1)} collective-permute-done((bf16[2,960,128]{2,1,0:T(8,128)(2,1)S(1)}, bf16[2,960,128]{2,1,0:T(8,128)(2,1)S(1)}, u32[]{:S(2)}, u32[]{:S(2)}) %collective-permute-start.26) | collective-permute-done | bytes 491552 | tf_op jit(solution)/shard_map/ppermute | solution.py:40
  127.8 1.6 collective-permute-start.35
  129.5 2.6 %collective-permute-start.39 = (bf16[1,960,128]{2,1,0:T(8,128)(2,1)S(1)}, bf16[1,960,128]{2,1,0:T(8,128)(2,1)S(1)}, u32[]{:S(2)}, u32[]{:S(2)}) collective-permute-start(bf16[1,960,128]{2,1,0:T(8,128)(2,1)S(1)} %get-tuple-element.289), channel_id=1, source_target_pairs={{0,16},{4,20},{8,24},{12,28},{16,0},{20,4},{24,8},{28,12},{1,17},{... | collective-permute-start | bytes 737288 | tf_op jit(solution)/shard_map/ppermute | solution.py:40
  132.1 3.6 %shard_map.233 = (bf16[256,640]{1,0:T(8,128)(2,1)S(1)}, bf16[256,640]{1,0:T(8,128)(2,1)S(1)}, bf16[512,256]{1,0:T(8,128)(2,1)S(1)}, bf16[512,256]{1,0:T(8,128)(2...) custom-call(bf16[256,640]{1,0:T(8,128)(2,1)S(1)} %get-tuple-element., ...), custom_call_target="tpu_custom_call" | custom-call | flops 1 | bytes 1 | tf_op jit(solution)/shard_map/pallas_call | solution.py:60
  138.3 5.4 %collective-permute-done.39 = bf16[1,960,128]{2,1,0:T(8,128)(2,1)S(1)} collective-permute-done((bf16[1,960,128]{2,1,0:T(8,128)(2,1)S(1)}, bf16[1,960,128]{2,1,0:T(8,128)(2,1)S(1)}, u32[]{:S(2)}, u32[]{:S(2)}) %collective-permute-start.39) | collective-permute-done | bytes 245792 | tf_op jit(solution)/shard_map/ppermute | solution.py:40
  144.3 2.7 %collective-permute-start.36 = (bf16[1,480,128]{2,1,0:T(8,128)(2,1)S(1)}, bf16[1,480,128]{2,1,0:T(8,128)(2,1)S(1)}, u32[]{:S(2)}, u32[]{:S(2)}) collective-permute-start(bf16[1,480,128]{2,1,0:T(8,128)(2,1)S(1)} %add_convert_fusion.14), channel_id=1, source_target_pairs={{0,16},{4,20},{8,24},{12,28},{16,0},{20,4},{24,8},{28,12},{1,17},{... | collective-permute-start | bytes 368648 | tf_op jit(solution)/shard_map/ppermute | solution.py:40
  147.3 13.6 %collective-permute-done.32 = bf16[4,496,128]{2,1,0:T(8,128)(2,1)S(1)} collective-permute-done((bf16[4,496,128]{2,1,0:T(8,128)(2,1)S(1)}, bf16[4,496,128]{2,1,0:T(8,128)(2,1)S(1)}, u32[]{:S(2)}, u32[]{:S(2)}) %collective-permute-start.32) | collective-permute-done | bytes 507936 | tf_op jit(solution)/shard_map/ppermute | solution.py:40
  163.5 3.9 %collective-permute-done.33 = bf16[2,496,128]{2,1,0:T(8,128)(2,1)S(1)} collective-permute-done((bf16[2,496,128]{2,1,0:T(8,128)(2,1)S(1)}, bf16[2,496,128]{2,1,0:T(8,128)(2,1)S(1)}, u32[]{:S(2)}, u32[]{:S(2)}) %collective-permute-start.33) | collective-permute-done | bytes 253984 | tf_op jit(solution)/shard_map/ppermute | solution.py:40
  167.6 7.5 %collective-permute-done.34 = bf16[1,496,128]{2,1,0:T(8,128)(2,1)S(1)} collective-permute-done((bf16[1,496,128]{2,1,0:T(8,128)(2,1)S(1)}, bf16[1,496,128]{2,1,0:T(8,128)(2,1)S(1)}, u32[]{:S(2)}, u32[]{:S(2)}) %collective-permute-start.34) | collective-permute-done | bytes 127008 | tf_op jit(solution)/shard_map/ppermute | solution.py:40
  176.5 3.2 %collective-permute-done.40 = bf16[336,128]{1,0:T(8,128)(2,1)S(1)} collective-permute-done((bf16[336,128]{1,0:T(8,128)(2,1)S(1)}, bf16[336,128]{1,0:T(8,128)(2,1)S(1)}, u32[]{:S(2)}, u32[]{:S(2)}) %collective-permute-start.40) | collective-permute-done | bytes 86048 | tf_op jit(solution)/shard_map/ppermute | solution.py:40
  179.8 5.4 %collective-permute-done.38 = bf16[1,960,128]{2,1,0:T(8,128)(2,1)S(1)} collective-permute-done((bf16[1,960,128]{2,1,0:T(8,128)(2,1)S(1)}, bf16[1,960,128]{2,1,0:T(8,128)(2,1)S(1)}, u32[]{:S(2)}, u32[]{:S(2)}) %collective-permute-start.38) | collective-permute-done | bytes 245792 | tf_op jit(solution)/shard_map/ppermute | solution.py:40
  (135 shorter events, 52.9 us)
Async XLA Ops:
  0.6 7.4 %collective-permute-start = (bf16[128,640]{1,0:T(8,128)(2,1)}, bf16[128,640]{1,0:T(8,128)(2,1)S(1)}, u32[]{:S(2)}, u32[]{:S(2)}) collective-permute-start(bf16[128,640]{1,0:T(8,128)(2,1)} %own_ref), channel_id=1, source_target_pairs={{0,2},{1,3},{2,0},{3,1},{4,6},{5,7},{6,4},{7,5},{8,10},{9,11},{10,... | collective-permute-start | bytes 491528 | tf_op jit(solution)/shard_map/ppermute | solution.py:40
  8.3 1.7 collective-permute-start.1
  12.5 1.7 collective-permute-start.2
  14.3 9.8 %collective-permute-start.3 = (bf16[256,640]{1,0:T(8,128)(2,1)S(1)}, bf16[256,640]{1,0:T(8,128)(2,1)S(1)}, u32[]{:S(2)}, u32[]{:S(2)}) collective-permute-start(bf16[256,640]{1,0:T(8,128)(2,1)S(1)} %add_convert_fusion.9.pair_ref), channel_id=1, source_target_pairs={{0,2},{1,3},{2,0},{3,1},{4,6},{5,7},{6,4},{7,5},{8,10},{9,11},{10,... | collective-permute-start | bytes 983048 | tf_op jit(solution)/shard_map/ppermute | solution.py:40
  24.5 1.7 collective-permute-start.4
  27.8 1.7 collective-permute-start.5
  29.5 9.8 %collective-permute-start.6 = (bf16[256,640]{1,0:T(8,128)(2,1)S(1)}, bf16[256,640]{1,0:T(8,128)(2,1)S(1)}, u32[]{:S(2)}, u32[]{:S(2)}) collective-permute-start(bf16[256,640]{1,0:T(8,128)(2,1)S(1)} %add_convert_fusion.8.pair_ref), channel_id=1, source_target_pairs={{0,2},{1,3},{2,0},{3,1},{4,6},{5,7},{6,4},{7,5},{8,10},{9,11},{10,... | collective-permute-start | bytes 983048 | tf_op jit(solution)/shard_map/ppermute | solution.py:40
  45.6 9.8 %collective-permute-start.9 = (bf16[256,640]{1,0:T(8,128)(2,1)S(1)}, bf16[256,640]{1,0:T(8,128)(2,1)S(1)}, u32[]{:S(2)}, u32[]{:S(2)}) collective-permute-start(bf16[256,640]{1,0:T(8,128)(2,1)S(1)} %add_convert_fusion.7.pair_ref), channel_id=1, source_target_pairs={{0,2},{1,3},{2,0},{3,1},{4,6},{5,7},{6,4},{7,5},{8,10},{9,11},{10,... | collective-permute-start | bytes 983048 | tf_op jit(solution)/shard_map/ppermute | solution.py:40
  60.8 13.4 %collective-permute-start.12 = (bf16[256,640]{1,0:T(8,128)(2,1)S(1)}, bf16[256,640]{1,0:T(8,128)(2,1)S(1)}, u32[]{:S(2)}, u32[]{:S(2)}) collective-permute-start(bf16[256,640]{1,0:T(8,128)(2,1)S(1)} %add_convert_fusion.6.pair_ref), channel_id=1, source_target_pairs={{0,2},{1,3},{2,0},{3,1},{4,6},{5,7},{6,4},{7,5},{8,10},{9,11},{10,... | collective-permute-start | bytes 983048 | tf_op jit(solution)/shard_map/ppermute | solution.py:40
  62.6 11.5 %collective-permute-start.13 = (bf16[128,640]{1,0:T(8,128)(2,1)S(1)}, bf16[128,640]{1,0:T(8,128)(2,1)S(1)}, u32[]{:S(2)}, u32[]{:S(2)}) collective-permute-start(bf16[128,640]{1,0:T(8,128)(2,1)S(1)} %copy-done.12), channel_id=1, source_target_pairs={{0,2},{1,3},{2,0},{3,1},{4,6},{5,7},{6,4},{7,5},{8,10},{9,11},{10,... | collective-permute-start | bytes 491528 | tf_op jit(solution)/shard_map/ppermute | solution.py:40
  80.7 9.8 %collective-permute-start.16 = (bf16[256,640]{1,0:T(8,128)(2,1)S(1)}, bf16[256,640]{1,0:T(8,128)(2,1)S(1)}, u32[]{:S(2)}, u32[]{:S(2)}) collective-permute-start(bf16[256,640]{1,0:T(8,128)(2,1)S(1)} %add_convert_fusion.5.pair_ref), channel_id=1, source_target_pairs={{0,2},{1,3},{2,0},{3,1},{4,6},{5,7},{6,4},{7,5},{8,10},{9,11},{10,... | collective-permute-start | bytes 983048 | tf_op jit(solution)/shard_map/ppermute | solution.py:40
  83.9 24.7 %collective-permute-start.20 = (bf16[4,960,128]{2,1,0:T(8,128)(2,1)S(1)}, bf16[4,960,128]{2,1,0:T(8,128)(2,1)S(1)}, u32[]{:S(2)}, u32[]{:S(2)}) collective-permute-start(bf16[4,960,128]{2,1,0:T(8,128)(2,1)S(1)} %get-tuple-element.209), channel_id=1, source_target_pairs={{0,4},{4,0},{8,12},{12,8},{16,20},{20,16},{24,28},{28,24},{1,5},{5... | collective-permute-start | bytes 2949128 | tf_op jit(solution)/shard_map/ppermute | solution.py:40
  96.5 3.4 %collective-permute-start.19 = (bf16[512,256]{1,0:T(8,128)(2,1)S(1)}, bf16[512,256]{1,0:T(8,128)(2,1)S(1)}, u32[]{:S(2)}, u32[]{:S(2)}) collective-permute-start(bf16[512,256]{1,0:T(8,128)(2,1)S(1)} %get-tuple-element.203), channel_id=1, source_target_pairs={{0,1},{1,0},{2,3},{3,2},{4,5},{5,4},{6,7},{7,6},{8,9},{9,8},{10,11... | collective-permute-start | bytes 786440 | tf_op jit(solution)/shard_map/ppermute | solution.py:40
  98.0 10.8 %collective-permute-start.21 = (bf16[256,640]{1,0:T(8,128)(2,1)S(1)}, bf16[256,640]{1,0:T(8,128)(2,1)S(1)}, u32[]{:S(2)}, u32[]{:S(2)}) collective-permute-start(bf16[256,640]{1,0:T(8,128)(2,1)S(1)} %add_convert_fusion.4.pair_ref), channel_id=1, source_target_pairs={{0,2},{1,3},{2,0},{3,1},{4,6},{5,7},{6,4},{7,5},{8,10},{9,11},{10,... | collective-permute-start | bytes 983048 | tf_op jit(solution)/shard_map/ppermute | solution.py:40
  100.8 17.2 %collective-permute-start.23 = (bf16[4,480,128]{2,1,0:T(8,128)(2,1)S(1)}, bf16[4,480,128]{2,1,0:T(8,128)(2,1)S(1)}, u32[]{:S(2)}, u32[]{:S(2)}) collective-permute-start(bf16[4,480,128]{2,1,0:T(8,128)(2,1)S(1)} %get-tuple-element.219), channel_id=1, source_target_pairs={{0,4},{4,0},{8,12},{12,8},{16,20},{20,16},{24,28},{28,24},{1,5},{5... | collective-permute-start | bytes 1474568 | tf_op jit(solution)/shard_map/ppermute | solution.py:40
  113.1 5.0 %collective-permute-start.24 = (bf16[256,640]{1,0:T(8,128)(2,1)S(1)}, bf16[256,640]{1,0:T(8,128)(2,1)S(1)}, u32[]{:S(2)}, u32[]{:S(2)}) collective-permute-start(bf16[256,640]{1,0:T(8,128)(2,1)S(1)} %get-tuple-element.224), channel_id=1, source_target_pairs={{0,1},{1,0},{2,3},{3,2},{4,5},{5,4},{6,7},{7,6},{8,9},{9,8},{10,11... | collective-permute-start | bytes 983048 | tf_op jit(solution)/shard_map/ppermute | solution.py:40
  113.3 13.5 %collective-permute-start.26 = (bf16[2,960,128]{2,1,0:T(8,128)(2,1)S(1)}, bf16[2,960,128]{2,1,0:T(8,128)(2,1)S(1)}, u32[]{:S(2)}, u32[]{:S(2)}) collective-permute-start(bf16[2,960,128]{2,1,0:T(8,128)(2,1)S(1)} %get-tuple-element.287), channel_id=1, source_target_pairs={{0,8},{4,12},{8,0},{12,4},{16,24},{20,28},{24,16},{28,20},{1,9},{5... | collective-permute-start | bytes 1474568 | tf_op jit(solution)/shard_map/ppermute | solution.py:40
  118.2 8.7 %collective-permute-start.25 = (bf16[256,640]{1,0:T(8,128)(2,1)S(1)}, bf16[256,640]{1,0:T(8,128)(2,1)S(1)}, u32[]{:S(2)}, u32[]{:S(2)}) collective-permute-start(bf16[256,640]{1,0:T(8,128)(2,1)S(1)} %add_convert_fusion.3.pair_ref), channel_id=1, source_target_pairs={{0,2},{1,3},{2,0},{3,1},{4,6},{5,7},{6,4},{7,5},{8,10},{9,11},{10,... | collective-permute-start | bytes 983048 | tf_op jit(solution)/shard_map/ppermute | solution.py:40
  120.0 26.9 %collective-permute-start.31 = (bf16[4,960,128]{2,1,0:T(8,128)(2,1)S(1)}, bf16[4,960,128]{2,1,0:T(8,128)(2,1)S(1)}, u32[]{:S(2)}, u32[]{:S(2)}) collective-permute-start(bf16[4,960,128]{2,1,0:T(8,128)(2,1)S(1)} %get-tuple-element.262), channel_id=1, source_target_pairs={{0,4},{4,0},{8,12},{12,8},{16,20},{20,16},{24,28},{28,24},{1,5},{5... | collective-permute-start | bytes 2949128 | tf_op jit(solution)/shard_map/ppermute | solution.py:40
  127.7 4.4 %collective-permute-start.27 = (bf16[256,640]{1,0:T(8,128)(2,1)S(1)}, bf16[256,640]{1,0:T(8,128)(2,1)S(1)}, u32[]{:S(2)}, u32[]{:S(2)}) collective-permute-start(bf16[256,640]{1,0:T(8,128)(2,1)S(1)} %get-tuple-element.235.own_ref.refs_5_), channel_id=1, source_target_pairs={{0,1},{1,0},{2,3},{3,2},{4,5},{5,4},{6,7},{7,6},{8,9},{9,8},{10,11... | collective-permute-start | bytes 983048 | tf_op jit(solution)/shard_map/ppermute | solution.py:40
  127.8 15.9 %collective-permute-start.35 = (bf16[2,480,128]{2,1,0:T(8,128)(2,1)S(1)}, bf16[2,480,128]{2,1,0:T(8,128)(2,1)S(1)}, u32[]{:S(2)}, u32[]{:S(2)}) collective-permute-start(bf16[2,480,128]{2,1,0:T(8,128)(2,1)S(1)} %get-tuple-element.293), channel_id=1, source_target_pairs={{0,8},{4,12},{8,0},{12,4},{16,24},{20,28},{24,16},{28,20},{1,9},{5... | collective-permute-start | bytes 737288 | tf_op jit(solution)/shard_map/ppermute | solution.py:40
  129.5 14.3 %collective-permute-start.39 = (bf16[1,960,128]{2,1,0:T(8,128)(2,1)S(1)}, bf16[1,960,128]{2,1,0:T(8,128)(2,1)S(1)}, u32[]{:S(2)}, u32[]{:S(2)}) collective-permute-start(bf16[1,960,128]{2,1,0:T(8,128)(2,1)S(1)} %get-tuple-element.289), channel_id=1, source_target_pairs={{0,16},{4,20},{8,24},{12,28},{16,0},{20,4},{24,8},{28,12},{1,17},{... | collective-permute-start | bytes 737288 | tf_op jit(solution)/shard_map/ppermute | solution.py:40
  135.8 26.8 %collective-permute-start.28 = (bf16[256,640]{1,0:T(8,128)(2,1)S(1)}, bf16[256,640]{1,0:T(8,128)(2,1)S(1)}, u32[]{:S(2)}, u32[]{:S(2)}) collective-permute-start(bf16[256,640]{1,0:T(8,128)(2,1)S(1)} %get-tuple-element.243), channel_id=1, source_target_pairs={{0,1},{1,0},{2,3},{3,2},{4,5},{5,4},{6,7},{7,6},{8,9},{9,8},{10,11... | collective-permute-start | bytes 983048 | tf_op jit(solution)/shard_map/ppermute | solution.py:40
  143.8 17.1 %collective-permute-start.32 = (bf16[4,496,128]{2,1,0:T(8,128)(2,1)S(1)}, bf16[4,496,128]{2,1,0:T(8,128)(2,1)S(1)}, u32[]{:S(2)}, u32[]{:S(2)}) collective-permute-start(bf16[4,496,128]{2,1,0:T(8,128)(2,1)S(1)} %get-tuple-element.265), channel_id=1, source_target_pairs={{0,8},{4,12},{8,0},{12,4},{16,24},{20,28},{24,16},{28,20},{1,9},{5... | collective-permute-start | bytes 1523720 | tf_op jit(solution)/shard_map/ppermute | solution.py:40
  144.3 19.2 %collective-permute-start.36 = (bf16[1,480,128]{2,1,0:T(8,128)(2,1)S(1)}, bf16[1,480,128]{2,1,0:T(8,128)(2,1)S(1)}, u32[]{:S(2)}, u32[]{:S(2)}) collective-permute-start(bf16[1,480,128]{2,1,0:T(8,128)(2,1)S(1)} %add_convert_fusion.14), channel_id=1, source_target_pairs={{0,16},{4,20},{8,24},{12,28},{16,0},{20,4},{24,8},{28,12},{1,17},{... | collective-permute-start | bytes 368648 | tf_op jit(solution)/shard_map/ppermute | solution.py:40
  147.2 28.3 %collective-permute-start.37 = (bf16[2,960,128]{2,1,0:T(8,128)(2,1)S(1)}, bf16[2,960,128]{2,1,0:T(8,128)(2,1)S(1)}, u32[]{:S(2)}, u32[]{:S(2)}) collective-permute-start(bf16[2,960,128]{2,1,0:T(8,128)(2,1)S(1)} %get-tuple-element.285), channel_id=1, source_target_pairs={{0,8},{4,12},{8,0},{12,4},{16,24},{20,28},{24,16},{28,20},{1,9},{5... | collective-permute-start | bytes 1474568 | tf_op jit(solution)/shard_map/ppermute | solution.py:40
  161.0 6.3 %collective-permute-start.33 = (bf16[2,496,128]{2,1,0:T(8,128)(2,1)S(1)}, bf16[2,496,128]{2,1,0:T(8,128)(2,1)S(1)}, u32[]{:S(2)}, u32[]{:S(2)}) collective-permute-start(bf16[2,496,128]{2,1,0:T(8,128)(2,1)S(1)} %get-tuple-element.291), channel_id=1, source_target_pairs={{0,4},{4,0},{8,12},{12,8},{16,20},{20,16},{24,28},{28,24},{1,5},{5... | collective-permute-start | bytes 761864 | tf_op jit(solution)/shard_map/ppermute | solution.py:40
  162.7 13.0 %collective-permute-start.29 = (bf16[256,640]{1,0:T(8,128)(2,1)S(1)}, bf16[256,640]{1,0:T(8,128)(2,1)S(1)}, u32[]{:S(2)}, u32[]{:S(2)}) collective-permute-start(bf16[256,640]{1,0:T(8,128)(2,1)S(1)} %add_convert_fusion.2.pair_ref), channel_id=1, source_target_pairs={{0,2},{1,3},{2,0},{3,1},{4,6},{5,7},{6,4},{7,5},{8,10},{9,11},{10,... | collective-permute-start | bytes 983048 | tf_op jit(solution)/shard_map/ppermute | solution.py:40
  167.4 7.7 %collective-permute-start.34 = (bf16[1,496,128]{2,1,0:T(8,128)(2,1)S(1)}, bf16[1,496,128]{2,1,0:T(8,128)(2,1)S(1)}, u32[]{:S(2)}, u32[]{:S(2)}) collective-permute-start(bf16[1,496,128]{2,1,0:T(8,128)(2,1)S(1)} %fusion), channel_id=1, source_target_pairs={{0,16},{4,20},{8,24},{12,28},{16,0},{20,4},{24,8},{28,12},{1,17},{... | collective-permute-start | bytes 380936 | tf_op jit(solution)/shard_map/ppermute | solution.py:40
  175.1 4.6 %collective-permute-start.40 = (bf16[336,128]{1,0:T(8,128)(2,1)S(1)}, bf16[336,128]{1,0:T(8,128)(2,1)S(1)}, u32[]{:S(2)}, u32[]{:S(2)}) collective-permute-start(bf16[336,128]{1,0:T(8,128)(2,1)S(1)} %pad_maximum_fusion), channel_id=1, source_target_pairs={{0,2},{1,3},{2,0},{3,1},{4,6},{5,7},{6,4},{7,5},{8,10},{9,11},{10,... | collective-permute-start | bytes 258056 | tf_op jit(solution)/shard_map/ppermute | solution.py:40
  175.5 9.6 %collective-permute-start.38 = (bf16[1,960,128]{2,1,0:T(8,128)(2,1)S(1)}, bf16[1,960,128]{2,1,0:T(8,128)(2,1)S(1)}, u32[]{:S(2)}, u32[]{:S(2)}) collective-permute-start(bf16[1,960,128]{2,1,0:T(8,128)(2,1)S(1)} %add_convert_fusion.12), channel_id=1, source_target_pairs={{0,16},{4,20},{8,24},{12,28},{16,0},{20,4},{24,8},{28,12},{1,17},{... | collective-permute-start | bytes 737288 | tf_op jit(solution)/shard_map/ppermute | solution.py:40
  179.7 5.5 %collective-permute-start.41 = (bf16[336,128]{1,0:T(8,128)(2,1)S(1)}, bf16[336,128]{1,0:T(8,128)(2,1)S(1)}, u32[]{:S(2)}, u32[]{:S(2)}) collective-permute-start(bf16[336,128]{1,0:T(8,128)(2,1)S(1)} %add_convert_fusion.15.refs_4_), channel_id=1, source_target_pairs={{0,1},{1,0},{2,3},{3,2},{4,5},{5,4},{6,7},{7,6},{8,9},{9,8},{10,11... | collective-permute-start | bytes 258056 | tf_op jit(solution)/shard_map/ppermute | solution.py:40
  (23 other events, 54.7 us)

commit v5 on v4

--- a/solution.py
+++ b/solution.py
@@ -816,8 +816,8 @@
             )
             grad_input = back_to_input(pair, other, stream, grad_middle, norm_gains, layer)
 
-    sums["mlp1"].step(sums["attn0"].kept)
     sums["attn1"].step(sums["attn0"].kept)
+    sums["mlp1"].step(sums["attn1"].kept)
     sums["mlp0"].step(sums["attn0"].kept)
     sums["attn0"].step(sums["mlp0"].kept)
     sums["attn0"].step()

time: 187 us -> 185 us (0.989)
  waiting for transfers between devices: 115 us -> 111 us
  starting transfers between devices: 34.3 us -> 37.4 us
    ppermute x42, waiting for transfers between devices: 115 us -> 111 us  [swap(): return lax.ppermute(array, axis, [(i, i ^ bit) for i in range(size)])]
    ppermute x42, starting transfers between devices: 34.3 us -> 37.4 us  [swap(): return lax.ppermute(array, axis, [(i, i ^ bit) for i in range(size)])]
  transfers between devices with their start and end apart: 42 -> 42, of which waited for: 30 -> 29; matrix products, arithmetic and copies ran while one was open for 1% -> 1% of each run, Pallas kernels for 10% -> 10%
where the time goes in v5:
time: 185 us
  waiting for transfers between devices  111 us (60%)
  starting transfers between devices  37.4 us (20%)
  Pallas kernels  32.3 us (17%)
  other arithmetic  1.91 us (1%)
    ppermute x42, waiting for transfers between devices, swap(): return lax.ppermute(array, axis, [(i, i ^ bit) for i in range(size)])  111 us
    ppermute x42, starting transfers between devices, swap(): return lax.ppermute(array, axis, [(i, i ^ bit) for i in range(size)])  37.4 us
    pallas_call x21, Pallas kernels, kernel_call(): pl.pallas_call(body, grid=(1,), in_specs=[spec(place, arg) for place, arg...  27.5 us
    pallas_call x4, Pallas kernels, gradient_blocks(): pl.pallas_call(body, grid=(1,), in_specs=specs, out_specs=[pl.BlockSpec(o...  4.8 us
  transfers between devices with their start and end apart: 42, of which 29 were waited for; matrix products, arithmetic and copies ran while one was open for 1% of the time, Pallas kernels for 10%

profile of v5, /device:TPU:0, one launch (start us, length us, event | category | flops | bytes accessed | tf_op | source)
XLA Modules:
  0.0 185.0 jit_solution(12778363532666997973)
XLA Ops:
  0.6 3.0 %collective-permute-start = (bf16[128,640]{1,0:T(8,128)(2,1)}, bf16[128,640]{1,0:T(8,128)(2,1)S(1)}, u32[]{:S(2)}, u32[]{:S(2)}) collective-permute-start(bf16[128,640]{1,0:T(8,128)(2,1)} %own_ref), channel_id=1, source_target_pairs={{0,2},{1,3},{2,0},{3,1},{4,6},{5,7},{6,4},{7,5},{8,10},{9,11},{10,... | collective-permute-start | bytes 491528 | tf_op jit(solution)/shard_map/ppermute | solution.py:40
  6.2 1.9 %collective-permute-done.beside_ref = bf16[128,640]{1,0:T(8,128)(2,1)S(1)} collective-permute-done((bf16[128,640]{1,0:T(8,128)(2,1)}, bf16[128,640]{1,0:T(8,128)(2,1)S(1)}, u32[]{:S(2)}, u32[]{:S(2)}) %collective-permute-start) | collective-permute-done | bytes 163872 | tf_op jit(solution)/shard_map/ppermute | solution.py:40
  10.1 2.5 %shard_map.215 = (bf16[256,640]{1,0:T(8,128)(2,1)S(1)}, bf16[256,640]{1,0:T(8,128)(2,1)S(1)}, f32[512,256]{1,0:T(8,128)S(1)}, f32[512,256]{1,0:T(8,128)S(1)}, bf...) custom-call(bf16[256,640]{1,0:T(8,128)(2,1)S(1)} %get-tuple-element., ...), custom_call_target="tpu_custom_call" | custom-call | flops 1000000000 | bytes 4000000 | tf_op jit(solution)/shard_map/pallas_call | solution.py:60
  14.3 1.8 collective-permute-start.3
  17.1 7.0 %collective-permute-done.3.other_ref = bf16[256,640]{1,0:T(8,128)(2,1)S(1)} collective-permute-done((bf16[256,640]{1,0:T(8,128)(2,1)S(1)}, bf16[256,640]{1,0:T(8,128)(2,1)S(1)}, u32[]{:S(2)}, u32[]{:S(2)}) %collective-permute-start.3) | collective-permute-done | bytes 327712 | tf_op jit(solution)/shard_map/ppermute | solution.py:40
  29.5 1.8 collective-permute-start.6
  31.3 8.0 %collective-permute-done.6.other_ref = bf16[256,640]{1,0:T(8,128)(2,1)S(1)} collective-permute-done((bf16[256,640]{1,0:T(8,128)(2,1)S(1)}, bf16[256,640]{1,0:T(8,128)(2,1)S(1)}, u32[]{:S(2)}, u32[]{:S(2)}) %collective-permute-start.6) | collective-permute-done | bytes 327712 | tf_op jit(solution)/shard_map/ppermute | solution.py:40
  41.4 2.4 %shard_map.220 = (bf16[256,640]{1,0:T(8,128)(2,1)S(1)}, bf16[256,640]{1,0:T(8,128)(2,1)S(1)}, f32[512,256]{1,0:T(8,128)S(1)}, f32[512,256]{1,0:T(8,128)S(1)}, bf...) custom-call(bf16[256,640]{1,0:T(8,128)(2,1)S(1)} %get-tuple-element., ...), custom_call_target="tpu_custom_call" | custom-call | flops 1000000000 | bytes 4000000 | tf_op jit(solution)/shard_map/pallas_call | solution.py:60
  45.6 1.8 collective-permute-start.9
  47.4 8.0 %collective-permute-done.9.other_ref = bf16[256,640]{1,0:T(8,128)(2,1)S(1)} collective-permute-done((bf16[256,640]{1,0:T(8,128)(2,1)S(1)}, bf16[256,640]{1,0:T(8,128)(2,1)S(1)}, u32[]{:S(2)}, u32[]{:S(2)}) %collective-permute-start.9) | collective-permute-done | bytes 327712 | tf_op jit(solution)/shard_map/ppermute | solution.py:40
  60.8 1.8 collective-permute-start.12
  63.0 11.2 %collective-permute-done.13 = bf16[128,640]{1,0:T(8,128)(2,1)S(1)} collective-permute-done((bf16[128,640]{1,0:T(8,128)(2,1)S(1)}, bf16[128,640]{1,0:T(8,128)(2,1)S(1)}, u32[]{:S(2)}, u32[]{:S(2)}) %collective-permute-start.13) | collective-permute-done | bytes 163872 | tf_op jit(solution)/shard_map/ppermute | solution.py:40
  76.8 2.0 %shard_map.224 = (bf16[256,640]{1,0:T(8,128)(2,1)S(1)}, bf16[256,640]{1,0:T(8,128)(2,1)S(1)}, bf16[512,512]{1,0:T(8,128)(2,1)S(1)}, bf16[512,512]{1,0:T(8,128)(2,1)S(1)}) custom-call(bf16[256,640]{1,0:T(8,128)(2,1)S(1)} %get-tuple-element.177.own_ref.refs_8_, bf16[256,640]{1,0:T(8,128)(2,1)S(1)} %collective-permute-done.14.received_ref.refs_9_, ...), custom_call_target="tpu_custom_call" | custom-call | flops 1 | bytes 1 | tf_op jit(solution)/shard_map/pallas_call | solution.py:60
  80.7 1.8 collective-permute-start.16
  85.5 5.0 %collective-permute-done.16.other_ref = bf16[256,640]{1,0:T(8,128)(2,1)S(1)} collective-permute-done((bf16[256,640]{1,0:T(8,128)(2,1)S(1)}, bf16[256,640]{1,0:T(8,128)(2,1)S(1)}, u32[]{:S(2)}, u32[]{:S(2)}) %collective-permute-start.16) | collective-permute-done | bytes 327712 | tf_op jit(solution)/shard_map/ppermute | solution.py:40
  92.9 3.3 %shard_map.227 = (bf16[256,640]{1,0:T(8,128)(2,1)S(1)}, bf16[256,640]{1,0:T(8,128)(2,1)S(1)}, bf16[512,256]{1,0:T(8,128)(2,1)S(1)}, bf16[512,256]{1,0:T(8,128)(2...) custom-call(bf16[256,640]{1,0:T(8,128)(2,1)S(1)} %get-tuple-element.191.own_ref.refs_5_, ...), custom_call_target="tpu_custom_call" | custom-call | flops 1 | bytes 1 | tf_op jit(solution)/shard_map/pallas_call | solution.py:60
  98.0 1.8 collective-permute-start.21
  102.4 6.2 %collective-permute-done.20 = bf16[4,960,128]{2,1,0:T(8,128)(2,1)S(1)} collective-permute-done((bf16[4,960,128]{2,1,0:T(8,128)(2,1)S(1)}, bf16[4,960,128]{2,1,0:T(8,128)(2,1)S(1)}, u32[]{:S(2)}, u32[]{:S(2)}) %collective-permute-start.20) | collective-permute-done | bytes 983072 | tf_op jit(solution)/shard_map/ppermute | solution.py:40
  111.3 1.8 shard_map.230
  114.9 3.1 %collective-permute-done.23 = bf16[4,480,128]{2,1,0:T(8,128)(2,1)S(1)} collective-permute-done((bf16[4,480,128]{2,1,0:T(8,128)(2,1)S(1)}, bf16[4,480,128]{2,1,0:T(8,128)(2,1)S(1)}, u32[]{:S(2)}, u32[]{:S(2)}) %collective-permute-start.23) | collective-permute-done | bytes 491552 | tf_op jit(solution)/shard_map/ppermute | solution.py:40
  120.0 1.8 collective-permute-start.31
  121.8 5.0 %collective-permute-done.26 = bf16[2,960,128]{2,1,0:T(8,128)(2,1)S(1)} collective-permute-done((bf16[2,960,128]{2,1,0:T(8,128)(2,1)S(1)}, bf16[2,960,128]{2,1,0:T(8,128)(2,1)S(1)}, u32[]{:S(2)}, u32[]{:S(2)}) %collective-permute-start.26) | collective-permute-done | bytes 491552 | tf_op jit(solution)/shard_map/ppermute | solution.py:40
  129.5 3.6 %shard_map.233 = (bf16[256,640]{1,0:T(8,128)(2,1)S(1)}, bf16[256,640]{1,0:T(8,128)(2,1)S(1)}, bf16[512,256]{1,0:T(8,128)(2,1)S(1)}, bf16[512,256]{1,0:T(8,128)(2...) custom-call(bf16[256,640]{1,0:T(8,128)(2,1)S(1)} %get-tuple-element., ...), custom_call_target="tpu_custom_call" | custom-call | flops 1 | bytes 1 | tf_op jit(solution)/shard_map/pallas_call | solution.py:60
  133.4 2.6 %collective-permute-start.39 = (bf16[1,960,128]{2,1,0:T(8,128)(2,1)S(1)}, bf16[1,960,128]{2,1,0:T(8,128)(2,1)S(1)}, u32[]{:S(2)}, u32[]{:S(2)}) collective-permute-start(bf16[1,960,128]{2,1,0:T(8,128)(2,1)S(1)} %get-tuple-element.291), channel_id=1, source_target_pairs={{0,16},{4,20},{8,24},{12,28},{16,0},{20,4},{24,8},{28,12},{1,17},{... | collective-permute-start | bytes 737288 | tf_op jit(solution)/shard_map/ppermute | solution.py:40
  138.7 1.9 %collective-permute-start.36 = (bf16[1,480,128]{2,1,0:T(8,128)(2,1)S(1)}, bf16[1,480,128]{2,1,0:T(8,128)(2,1)S(1)}, u32[]{:S(2)}, u32[]{:S(2)}) collective-permute-start(bf16[1,480,128]{2,1,0:T(8,128)(2,1)S(1)} %add_convert_fusion.14), channel_id=1, source_target_pairs={{0,16},{4,20},{8,24},{12,28},{16,0},{20,4},{24,8},{28,12},{1,17},{... | collective-permute-start | bytes 368648 | tf_op jit(solution)/shard_map/ppermute | solution.py:40
  140.5 1.9 %collective-permute-done.31 = bf16[4,960,128]{2,1,0:T(8,128)(2,1)S(1)} collective-permute-done((bf16[4,960,128]{2,1,0:T(8,128)(2,1)S(1)}, bf16[4,960,128]{2,1,0:T(8,128)(2,1)S(1)}, u32[]{:S(2)}, u32[]{:S(2)}) %collective-permute-start.31) | collective-permute-done | bytes 983072 | tf_op jit(solution)/shard_map/ppermute | solution.py:40
  142.7 1.9 %collective-permute-start.37 = (bf16[2,960,128]{2,1,0:T(8,128)(2,1)S(1)}, bf16[2,960,128]{2,1,0:T(8,128)(2,1)S(1)}, u32[]{:S(2)}, u32[]{:S(2)}) collective-permute-start(bf16[2,960,128]{2,1,0:T(8,128)(2,1)S(1)} %get-tuple-element.287), channel_id=1, source_target_pairs={{0,8},{4,12},{8,0},{12,4},{16,24},{20,28},{24,16},{28,20},{1,9},{5... | collective-permute-start | bytes 1474568 | tf_op jit(solution)/shard_map/ppermute | solution.py:40
  144.6 13.6 %collective-permute-done.32 = bf16[4,496,128]{2,1,0:T(8,128)(2,1)S(1)} collective-permute-done((bf16[4,496,128]{2,1,0:T(8,128)(2,1)S(1)}, bf16[4,496,128]{2,1,0:T(8,128)(2,1)S(1)}, u32[]{:S(2)}, u32[]{:S(2)}) %collective-permute-start.32) | collective-permute-done | bytes 507936 | tf_op jit(solution)/shard_map/ppermute | solution.py:40
  160.8 4.9 %collective-permute-done.33 = bf16[2,496,128]{2,1,0:T(8,128)(2,1)S(1)} collective-permute-done((bf16[2,496,128]{2,1,0:T(8,128)(2,1)S(1)}, bf16[2,496,128]{2,1,0:T(8,128)(2,1)S(1)}, u32[]{:S(2)}, u32[]{:S(2)}) %collective-permute-start.33) | collective-permute-done | bytes 253984 | tf_op jit(solution)/shard_map/ppermute | solution.py:40
  166.8 6.2 %collective-permute-done.34 = bf16[1,496,128]{2,1,0:T(8,128)(2,1)S(1)} collective-permute-done((bf16[1,496,128]{2,1,0:T(8,128)(2,1)S(1)}, bf16[1,496,128]{2,1,0:T(8,128)(2,1)S(1)}, u32[]{:S(2)}, u32[]{:S(2)}) %collective-permute-start.34) | collective-permute-done | bytes 127008 | tf_op jit(solution)/shard_map/ppermute | solution.py:40
  174.9 2.8 %collective-permute-done.40 = bf16[336,128]{1,0:T(8,128)(2,1)S(1)} collective-permute-done((bf16[336,128]{1,0:T(8,128)(2,1)S(1)}, bf16[336,128]{1,0:T(8,128)(2,1)S(1)}, u32[]{:S(2)}, u32[]{:S(2)}) %collective-permute-start.40) | collective-permute-done | bytes 86048 | tf_op jit(solution)/shard_map/ppermute | solution.py:40
  177.7 5.9 %collective-permute-done.38 = bf16[1,960,128]{2,1,0:T(8,128)(2,1)S(1)} collective-permute-done((bf16[1,960,128]{2,1,0:T(8,128)(2,1)S(1)}, bf16[1,960,128]{2,1,0:T(8,128)(2,1)S(1)}, u32[]{:S(2)}, u32[]{:S(2)}) %collective-permute-start.38) | collective-permute-done | bytes 245792 | tf_op jit(solution)/shard_map/ppermute | solution.py:40
  (135 shorter events, 55.6 us)
Async XLA Ops:
  0.6 7.4 %collective-permute-start = (bf16[128,640]{1,0:T(8,128)(2,1)}, bf16[128,640]{1,0:T(8,128)(2,1)S(1)}, u32[]{:S(2)}, u32[]{:S(2)}) collective-permute-start(bf16[128,640]{1,0:T(8,128)(2,1)} %own_ref), channel_id=1, source_target_pairs={{0,2},{1,3},{2,0},{3,1},{4,6},{5,7},{6,4},{7,5},{8,10},{9,11},{10,... | collective-permute-start | bytes 491528 | tf_op jit(solution)/shard_map/ppermute | solution.py:40
  8.3 1.7 collective-permute-start.1
  14.3 9.8 %collective-permute-start.3 = (bf16[256,640]{1,0:T(8,128)(2,1)S(1)}, bf16[256,640]{1,0:T(8,128)(2,1)S(1)}, u32[]{:S(2)}, u32[]{:S(2)}) collective-permute-start(bf16[256,640]{1,0:T(8,128)(2,1)S(1)} %add_convert_fusion.9.pair_ref), channel_id=1, source_target_pairs={{0,2},{1,3},{2,0},{3,1},{4,6},{5,7},{6,4},{7,5},{8,10},{9,11},{10,... | collective-permute-start | bytes 983048 | tf_op jit(solution)/shard_map/ppermute | solution.py:40
  24.5 1.7 collective-permute-start.4
  29.5 9.8 %collective-permute-start.6 = (bf16[256,640]{1,0:T(8,128)(2,1)S(1)}, bf16[256,640]{1,0:T(8,128)(2,1)S(1)}, u32[]{:S(2)}, u32[]{:S(2)}) collective-permute-start(bf16[256,640]{1,0:T(8,128)(2,1)S(1)} %add_convert_fusion.8.pair_ref), channel_id=1, source_target_pairs={{0,2},{1,3},{2,0},{3,1},{4,6},{5,7},{6,4},{7,5},{8,10},{9,11},{10,... | collective-permute-start | bytes 983048 | tf_op jit(solution)/shard_map/ppermute | solution.py:40
  39.7 1.7 collective-permute-start.7
  45.6 9.8 %collective-permute-start.9 = (bf16[256,640]{1,0:T(8,128)(2,1)S(1)}, bf16[256,640]{1,0:T(8,128)(2,1)S(1)}, u32[]{:S(2)}, u32[]{:S(2)}) collective-permute-start(bf16[256,640]{1,0:T(8,128)(2,1)S(1)} %add_convert_fusion.7.pair_ref), channel_id=1, source_target_pairs={{0,2},{1,3},{2,0},{3,1},{4,6},{5,7},{6,4},{7,5},{8,10},{9,11},{10,... | collective-permute-start | bytes 983048 | tf_op jit(solution)/shard_map/ppermute | solution.py:40
  60.8 13.4 %collective-permute-start.12 = (bf16[256,640]{1,0:T(8,128)(2,1)S(1)}, bf16[256,640]{1,0:T(8,128)(2,1)S(1)}, u32[]{:S(2)}, u32[]{:S(2)}) collective-permute-start(bf16[256,640]{1,0:T(8,128)(2,1)S(1)} %add_convert_fusion.6.pair_ref), channel_id=1, source_target_pairs={{0,2},{1,3},{2,0},{3,1},{4,6},{5,7},{6,4},{7,5},{8,10},{9,11},{10,... | collective-permute-start | bytes 983048 | tf_op jit(solution)/shard_map/ppermute | solution.py:40
  62.6 11.5 %collective-permute-start.13 = (bf16[128,640]{1,0:T(8,128)(2,1)S(1)}, bf16[128,640]{1,0:T(8,128)(2,1)S(1)}, u32[]{:S(2)}, u32[]{:S(2)}) collective-permute-start(bf16[128,640]{1,0:T(8,128)(2,1)S(1)} %copy-done.12), channel_id=1, source_target_pairs={{0,2},{1,3},{2,0},{3,1},{4,6},{5,7},{6,4},{7,5},{8,10},{9,11},{10,... | collective-permute-start | bytes 491528 | tf_op jit(solution)/shard_map/ppermute | solution.py:40
  80.7 9.8 %collective-permute-start.16 = (bf16[256,640]{1,0:T(8,128)(2,1)S(1)}, bf16[256,640]{1,0:T(8,128)(2,1)S(1)}, u32[]{:S(2)}, u32[]{:S(2)}) collective-permute-start(bf16[256,640]{1,0:T(8,128)(2,1)S(1)} %add_convert_fusion.5.pair_ref), channel_id=1, source_target_pairs={{0,2},{1,3},{2,0},{3,1},{4,6},{5,7},{6,4},{7,5},{8,10},{9,11},{10,... | collective-permute-start | bytes 983048 | tf_op jit(solution)/shard_map/ppermute | solution.py:40
  83.9 24.7 %collective-permute-start.20 = (bf16[4,960,128]{2,1,0:T(8,128)(2,1)S(1)}, bf16[4,960,128]{2,1,0:T(8,128)(2,1)S(1)}, u32[]{:S(2)}, u32[]{:S(2)}) collective-permute-start(bf16[4,960,128]{2,1,0:T(8,128)(2,1)S(1)} %get-tuple-element.209), channel_id=1, source_target_pairs={{0,4},{4,0},{8,12},{12,8},{16,20},{20,16},{24,28},{28,24},{1,5},{5... | collective-permute-start | bytes 2949128 | tf_op jit(solution)/shard_map/ppermute | solution.py:40
  96.5 3.4 %collective-permute-start.19 = (bf16[512,256]{1,0:T(8,128)(2,1)S(1)}, bf16[512,256]{1,0:T(8,128)(2,1)S(1)}, u32[]{:S(2)}, u32[]{:S(2)}) collective-permute-start(bf16[512,256]{1,0:T(8,128)(2,1)S(1)} %get-tuple-element.203), channel_id=1, source_target_pairs={{0,1},{1,0},{2,3},{3,2},{4,5},{5,4},{6,7},{7,6},{8,9},{9,8},{10,11... | collective-permute-start | bytes 786440 | tf_op jit(solution)/shard_map/ppermute | solution.py:40
  98.0 10.8 %collective-permute-start.21 = (bf16[256,640]{1,0:T(8,128)(2,1)S(1)}, bf16[256,640]{1,0:T(8,128)(2,1)S(1)}, u32[]{:S(2)}, u32[]{:S(2)}) collective-permute-start(bf16[256,640]{1,0:T(8,128)(2,1)S(1)} %add_convert_fusion.4.pair_ref), channel_id=1, source_target_pairs={{0,2},{1,3},{2,0},{3,1},{4,6},{5,7},{6,4},{7,5},{8,10},{9,11},{10,... | collective-permute-start | bytes 983048 | tf_op jit(solution)/shard_map/ppermute | solution.py:40
  100.8 17.2 %collective-permute-start.23 = (bf16[4,480,128]{2,1,0:T(8,128)(2,1)S(1)}, bf16[4,480,128]{2,1,0:T(8,128)(2,1)S(1)}, u32[]{:S(2)}, u32[]{:S(2)}) collective-permute-start(bf16[4,480,128]{2,1,0:T(8,128)(2,1)S(1)} %get-tuple-element.219), channel_id=1, source_target_pairs={{0,4},{4,0},{8,12},{12,8},{16,20},{20,16},{24,28},{28,24},{1,5},{5... | collective-permute-start | bytes 1474568 | tf_op jit(solution)/shard_map/ppermute | solution.py:40
  113.1 5.0 %collective-permute-start.24 = (bf16[256,640]{1,0:T(8,128)(2,1)S(1)}, bf16[256,640]{1,0:T(8,128)(2,1)S(1)}, u32[]{:S(2)}, u32[]{:S(2)}) collective-permute-start(bf16[256,640]{1,0:T(8,128)(2,1)S(1)} %get-tuple-element.224), channel_id=1, source_target_pairs={{0,1},{1,0},{2,3},{3,2},{4,5},{5,4},{6,7},{7,6},{8,9},{9,8},{10,11... | collective-permute-start | bytes 983048 | tf_op jit(solution)/shard_map/ppermute | solution.py:40
  113.3 13.5 %collective-permute-start.26 = (bf16[2,960,128]{2,1,0:T(8,128)(2,1)S(1)}, bf16[2,960,128]{2,1,0:T(8,128)(2,1)S(1)}, u32[]{:S(2)}, u32[]{:S(2)}) collective-permute-start(bf16[2,960,128]{2,1,0:T(8,128)(2,1)S(1)} %get-tuple-element.289), channel_id=1, source_target_pairs={{0,8},{4,12},{8,0},{12,4},{16,24},{20,28},{24,16},{28,20},{1,9},{5... | collective-permute-start | bytes 1474568 | tf_op jit(solution)/shard_map/ppermute | solution.py:40
  118.2 8.7 %collective-permute-start.25 = (bf16[256,640]{1,0:T(8,128)(2,1)S(1)}, bf16[256,640]{1,0:T(8,128)(2,1)S(1)}, u32[]{:S(2)}, u32[]{:S(2)}) collective-permute-start(bf16[256,640]{1,0:T(8,128)(2,1)S(1)} %add_convert_fusion.3.pair_ref), channel_id=1, source_target_pairs={{0,2},{1,3},{2,0},{3,1},{4,6},{5,7},{6,4},{7,5},{8,10},{9,11},{10,... | collective-permute-start | bytes 983048 | tf_op jit(solution)/shard_map/ppermute | solution.py:40
  120.0 22.4 %collective-permute-start.31 = (bf16[4,960,128]{2,1,0:T(8,128)(2,1)S(1)}, bf16[4,960,128]{2,1,0:T(8,128)(2,1)S(1)}, u32[]{:S(2)}, u32[]{:S(2)}) collective-permute-start(bf16[4,960,128]{2,1,0:T(8,128)(2,1)S(1)} %get-tuple-element.262), channel_id=1, source_target_pairs={{0,4},{4,0},{8,12},{12,8},{16,20},{20,16},{24,28},{28,24},{1,5},{5... | collective-permute-start | bytes 2949128 | tf_op jit(solution)/shard_map/ppermute | solution.py:40
  127.7 1.8 collective-permute-start.27
  127.8 9.2 %collective-permute-start.35 = (bf16[2,480,128]{2,1,0:T(8,128)(2,1)S(1)}, bf16[2,480,128]{2,1,0:T(8,128)(2,1)S(1)}, u32[]{:S(2)}, u32[]{:S(2)}) collective-permute-start(bf16[2,480,128]{2,1,0:T(8,128)(2,1)S(1)} %get-tuple-element.295), channel_id=1, source_target_pairs={{0,8},{4,12},{8,0},{12,4},{16,24},{20,28},{24,16},{28,20},{1,9},{5... | collective-permute-start | bytes 737288 | tf_op jit(solution)/shard_map/ppermute | solution.py:40
  133.1 2.9 %collective-permute-start.30 = (bf16[512,256]{1,0:T(8,128)(2,1)S(1)}, bf16[512,256]{1,0:T(8,128)(2,1)S(1)}, u32[]{:S(2)}, u32[]{:S(2)}) collective-permute-start(bf16[512,256]{1,0:T(8,128)(2,1)S(1)} %get-tuple-element.248), channel_id=1, source_target_pairs={{0,1},{1,0},{2,3},{3,2},{4,5},{5,4},{6,7},{7,6},{8,9},{9,8},{10,11... | collective-permute-start | bytes 786440 | tf_op jit(solution)/shard_map/ppermute | solution.py:40
  133.4 27.4 %collective-permute-start.39 = (bf16[1,960,128]{2,1,0:T(8,128)(2,1)S(1)}, bf16[1,960,128]{2,1,0:T(8,128)(2,1)S(1)}, u32[]{:S(2)}, u32[]{:S(2)}) collective-permute-start(bf16[1,960,128]{2,1,0:T(8,128)(2,1)S(1)} %get-tuple-element.291), channel_id=1, source_target_pairs={{0,16},{4,20},{8,24},{12,28},{16,0},{20,4},{24,8},{28,12},{1,17},{... | collective-permute-start | bytes 737288 | tf_op jit(solution)/shard_map/ppermute | solution.py:40
  136.0 23.9 %collective-permute-start.28 = (bf16[256,640]{1,0:T(8,128)(2,1)S(1)}, bf16[256,640]{1,0:T(8,128)(2,1)S(1)}, u32[]{:S(2)}, u32[]{:S(2)}) collective-permute-start(bf16[256,640]{1,0:T(8,128)(2,1)S(1)} %get-tuple-element.243), channel_id=1, source_target_pairs={{0,1},{1,0},{2,3},{3,2},{4,5},{5,4},{6,7},{7,6},{8,9},{9,8},{10,11... | collective-permute-start | bytes 983048 | tf_op jit(solution)/shard_map/ppermute | solution.py:40
  137.1 21.1 %collective-permute-start.32 = (bf16[4,496,128]{2,1,0:T(8,128)(2,1)S(1)}, bf16[4,496,128]{2,1,0:T(8,128)(2,1)S(1)}, u32[]{:S(2)}, u32[]{:S(2)}) collective-permute-start(bf16[4,496,128]{2,1,0:T(8,128)(2,1)S(1)} %get-tuple-element.265), channel_id=1, source_target_pairs={{0,8},{4,12},{8,0},{12,4},{16,24},{20,28},{24,16},{28,20},{1,9},{5... | collective-permute-start | bytes 1523720 | tf_op jit(solution)/shard_map/ppermute | solution.py:40
  138.7 22.1 %collective-permute-start.36 = (bf16[1,480,128]{2,1,0:T(8,128)(2,1)S(1)}, bf16[1,480,128]{2,1,0:T(8,128)(2,1)S(1)}, u32[]{:S(2)}, u32[]{:S(2)}) collective-permute-start(bf16[1,480,128]{2,1,0:T(8,128)(2,1)S(1)} %add_convert_fusion.14), channel_id=1, source_target_pairs={{0,16},{4,20},{8,24},{12,28},{16,0},{20,4},{24,8},{28,12},{1,17},{... | collective-permute-start | bytes 368648 | tf_op jit(solution)/shard_map/ppermute | solution.py:40
  142.7 31.1 %collective-permute-start.37 = (bf16[2,960,128]{2,1,0:T(8,128)(2,1)S(1)}, bf16[2,960,128]{2,1,0:T(8,128)(2,1)S(1)}, u32[]{:S(2)}, u32[]{:S(2)}) collective-permute-start(bf16[2,960,128]{2,1,0:T(8,128)(2,1)S(1)} %get-tuple-element.287), channel_id=1, source_target_pairs={{0,8},{4,12},{8,0},{12,4},{16,24},{20,28},{24,16},{28,20},{1,9},{5... | collective-permute-start | bytes 1474568 | tf_op jit(solution)/shard_map/ppermute | solution.py:40
  158.3 7.4 %collective-permute-start.33 = (bf16[2,496,128]{2,1,0:T(8,128)(2,1)S(1)}, bf16[2,496,128]{2,1,0:T(8,128)(2,1)S(1)}, u32[]{:S(2)}, u32[]{:S(2)}) collective-permute-start(bf16[2,496,128]{2,1,0:T(8,128)(2,1)S(1)} %get-tuple-element.293), channel_id=1, source_target_pairs={{0,4},{4,0},{8,12},{12,8},{16,20},{20,16},{24,28},{28,24},{1,5},{5... | collective-permute-start | bytes 761864 | tf_op jit(solution)/shard_map/ppermute | solution.py:40
  160.0 14.0 %collective-permute-start.29 = (bf16[256,640]{1,0:T(8,128)(2,1)S(1)}, bf16[256,640]{1,0:T(8,128)(2,1)S(1)}, u32[]{:S(2)}, u32[]{:S(2)}) collective-permute-start(bf16[256,640]{1,0:T(8,128)(2,1)S(1)} %add_convert_fusion.2.pair_ref), channel_id=1, source_target_pairs={{0,2},{1,3},{2,0},{3,1},{4,6},{5,7},{6,4},{7,5},{8,10},{9,11},{10,... | collective-permute-start | bytes 983048 | tf_op jit(solution)/shard_map/ppermute | solution.py:40
  165.7 7.2 %collective-permute-start.34 = (bf16[1,496,128]{2,1,0:T(8,128)(2,1)S(1)}, bf16[1,496,128]{2,1,0:T(8,128)(2,1)S(1)}, u32[]{:S(2)}, u32[]{:S(2)}) collective-permute-start(bf16[1,496,128]{2,1,0:T(8,128)(2,1)S(1)} %fusion), channel_id=1, source_target_pairs={{0,16},{4,20},{8,24},{12,28},{16,0},{20,4},{24,8},{28,12},{1,17},{... | collective-permute-start | bytes 380936 | tf_op jit(solution)/shard_map/ppermute | solution.py:40
  173.1 4.6 %collective-permute-start.40 = (bf16[336,128]{1,0:T(8,128)(2,1)S(1)}, bf16[336,128]{1,0:T(8,128)(2,1)S(1)}, u32[]{:S(2)}, u32[]{:S(2)}) collective-permute-start(bf16[336,128]{1,0:T(8,128)(2,1)S(1)} %pad_maximum_fusion), channel_id=1, source_target_pairs={{0,2},{1,3},{2,0},{3,1},{4,6},{5,7},{6,4},{7,5},{8,10},{9,11},{10,... | collective-permute-start | bytes 258056 | tf_op jit(solution)/shard_map/ppermute | solution.py:40
  173.9 9.8 %collective-permute-start.38 = (bf16[1,960,128]{2,1,0:T(8,128)(2,1)S(1)}, bf16[1,960,128]{2,1,0:T(8,128)(2,1)S(1)}, u32[]{:S(2)}, u32[]{:S(2)}) collective-permute-start(bf16[1,960,128]{2,1,0:T(8,128)(2,1)S(1)} %add_convert_fusion.12), channel_id=1, source_target_pairs={{0,16},{4,20},{8,24},{12,28},{16,0},{20,4},{24,8},{28,12},{1,17},{... | collective-permute-start | bytes 737288 | tf_op jit(solution)/shard_map/ppermute | solution.py:40
  177.6 6.1 %collective-permute-start.41 = (bf16[336,128]{1,0:T(8,128)(2,1)S(1)}, bf16[336,128]{1,0:T(8,128)(2,1)S(1)}, u32[]{:S(2)}, u32[]{:S(2)}) collective-permute-start(bf16[336,128]{1,0:T(8,128)(2,1)S(1)} %add_convert_fusion.15.refs_4_), channel_id=1, source_target_pairs={{0,1},{1,0},{2,3},{3,2},{4,5},{5,4},{6,7},{7,6},{8,9},{9,8},{10,11... | collective-permute-start | bytes 258056 | tf_op jit(solution)/shard_map/ppermute | solution.py:40
  (23 other events, 54.8 us)
